TPU v7x, 32 devices: a whole 2x2x4 slice. The times are simulated.
32 devices in a mesh: ri: 4 (over z), orb: 8 (over y, x, core).
Axes of the slice: x: 2, y: 2, z: 4, core: 2. Of those that a mesh axis runs over, the one named last changes fastest.
Arguments:
- integrals: bfloat16 [2048, 8, 3072], P(('ri', 'orb')), may hold values from -0.41992188 to 0.41992188
- screen: int32 [8, 3, 128], P(None, None, ('ri', 'orb')), may hold values 0 or 1
- green_occ: bfloat16 [8, 3, 32, 32], replicated, may hold values from -0.625 to 0.625
- green_virt: bfloat16 [8, 32, 32], replicated, may hold values from -1 to 1
Outputs:
- chi: float32 [2048, 2048], P('ri', 'orb')
All inputs are finite; a program needn't handle non-finite values. No bound on the sum of `screen` on one device may be relied on, other than what follows from the above.
Results may differ from a plain program's by a relative error of at most 0.0041.
Values may be sent and summed in bfloat16 or wider, within the bound.
No kernel may reach another device: no remote copies, remote signals or barrier semaphores. Data moves between devices by JAX's collectives and lax.ppermute only.
A program may use at most 256 MiB of HBM per device.

v0:
```python
import functools

import jax
import jax.numpy as jnp
from jax import lax
from jax.experimental import pallas as pl
from jax.experimental.pallas import tpu as pltpu
from jax.sharding import PartitionSpec as P

RB = 16
CHUNKS = 2
BF16 = jnp.bfloat16
F32 = jnp.float32
VMEM = pl.BlockSpec(memory_space=pltpu.VMEM)
SMEM = pl.BlockSpec(memory_space=pltpu.SMEM)
MIB = 1024 * 1024


def iota(shape, dim):
    return lax.broadcasted_iota(jnp.int32, shape, dim)


def dot(x, y):
    return lax.dot_general(x, y, (((1,), (0,)), ((), ())), preferred_element_type=F32)


def dot_t(x, y):
    return lax.dot_general(x, y, (((1,), (1,)), ((), ())), preferred_element_type=F32)


def ones_where(test):
    return jnp.where(test, 1.0, 0.0).astype(BF16)


def cost(flops, moved):
    return pl.CostEstimate(flops=int(flops), bytes_accessed=int(moved), transcendentals=0)


def prep_kernel(groups, blocks, c, per, screen_ref, x_ref, out_ref, *refs):
    lanes_ref = refs[-1]
    rows, first = per * groups, c * (per // RB)
    lane, row = iota((1536, 128), 1), iota((1536, 128), 0)
    base = row - (lane // 8) * 96 - lane % 8
    for g in range(12):
        lanes_ref[:, g * 128 : (g + 1) * 128] = ones_where(base == g * 8)
    to, of = iota((rows, rows), 0), iota((rows, rows), 1)
    by_group = ones_where(of == (to % per) * groups + to // per)
    for h in range(2):
        x = dot(by_group, x_ref[:, h * 1536 : (h + 1) * 1536]).astype(BF16)
        for s in range(3):
            y = dot(x, lanes_ref[:, s * 512 : (s + 1) * 512])
            for a in range(groups):
                d = a + s - 1
                if not 0 <= d < groups:
                    continue
                for b in range(per // RB):
                    keep = screen_ref[(a * 3 + s) * blocks + first + b].astype(F32)
                    at = a * per + b * RB
                    z = (y[at : at + RB] * keep).astype(BF16)
                    for j in range(4):
                        col = (2 - s) * 1024 + j * 256 + h * 128
                        out_ref[d, b * RB : (b + 1) * RB, col : col + 128] = z[:, j * 128 : (j + 1) * 128]
    zeros = jnp.zeros((per, 1024), BF16)
    out_ref[0, :, :1024] = zeros
    out_ref[groups - 1, :, 2048:] = zeros
    for odd, half_ref in enumerate(refs[:-1]):
        for k in range(groups // 2):
            half_ref[k] = out_ref[2 * k + odd]


def prep(c, x, screen, groups, per, halves):
    blocks = screen.shape[0] // (groups * 3)
    rows = per * groups
    shapes = [jax.ShapeDtypeStruct((groups, per, 3072), BF16)]
    shapes += [jax.ShapeDtypeStruct((groups // 2, per, 3072), BF16)] * (2 * halves)
    return pl.pallas_call(
        functools.partial(prep_kernel, groups, blocks, c, per),
        out_shape=shapes,
        in_specs=[SMEM, VMEM],
        out_specs=[VMEM] * len(shapes),
        scratch_shapes=[pltpu.VMEM((1536, 1536), BF16)],
        compiler_params=pltpu.CompilerParams(vmem_limit_bytes=24 * MIB),
        cost_estimate=cost(4 * rows * 1536 * 1536, rows * 3072 * 4),
    )(screen, x[c * rows : (c + 1) * rows])


def unpack_kernel(even_ref, odd_ref, *outs):
    me = lax.axis_index("orb")
    for k, out_ref in enumerate(outs):
        to = me ^ k
        for odd, x_ref in enumerate((even_ref, odd_ref)):

            @pl.when(to % 2 == odd)
            def _(x_ref=x_ref, out_ref=out_ref, to=to):
                out_ref[...] = x_ref[to // 2]


def unpack(even, odd):
    return pl.pallas_call(
        unpack_kernel,
        out_shape=[jax.ShapeDtypeStruct(even.shape[1:], BF16)] * 8,
        in_specs=[VMEM] * 2,
        out_specs=[VMEM] * 8,
        compiler_params=pltpu.CompilerParams(vmem_limit_bytes=12 * MIB),
        cost_estimate=cost(1e5, 8 * even.size),
        name="unpack",
    )(even, odd)


def assemble_kernel(*refs):
    out_ref = refs[-1]
    per = refs[0].shape[0]
    me = lax.axis_index("orb")
    for k, x_ref in enumerate(refs[:-1]):
        out_ref[pl.ds(pl.multiple_of((me ^ k) * per, per), per)] = x_ref[...]


def assemble(pieces):
    per, width = pieces[0].shape
    return pl.pallas_call(
        assemble_kernel,
        out_shape=jax.ShapeDtypeStruct((8 * per, width), BF16),
        in_specs=[VMEM] * 8,
        out_specs=VMEM,
        compiler_params=pltpu.CompilerParams(vmem_limit_bytes=12 * MIB),
        cost_estimate=cost(1e5, 32 * per * width),
        name="assemble",
    )(*pieces)


def weights_kernel(occ_ref, virt_ref, w1_ref, w2_ref):
    d = lax.axis_index("orb")
    last = occ_ref.shape[0] - 1
    spread = ones_where(iota((256, 32), 0) // 8 == iota((256, 32), 1))
    same = iota((256, 256), 0) % 8 == iota((256, 256), 1) % 8
    for c in range(3):
        at = jnp.clip(d + (c - 1), 0, last)
        for a in range(3):
            t = a - c + 1
            if 0 <= t <= 2:
                half = dot_t(spread, occ_ref[at, t]).astype(BF16)
                block = jnp.where(same, dot_t(half, spread), 0.0)
            else:
                block = jnp.zeros((256, 256), F32)
            w1_ref[a * 256 : (a + 1) * 256, c * 256 : (c + 1) * 256] = block.astype(BF16)
    row = iota((512, 32), 0)
    spread = ones_where((row // 128) * 8 + row % 8 == iota((512, 32), 1))
    same = (iota((512, 512), 0) % 128) // 8 == (iota((512, 512), 1) % 128) // 8
    half = dot(spread, virt_ref[d]).astype(BF16)
    w2_ref[...] = jnp.where(same, dot_t(half, spread), 0.0).astype(BF16)


def weights(occ, virt):
    return pl.pallas_call(
        weights_kernel,
        out_shape=(jax.ShapeDtypeStruct((768, 768), BF16), jax.ShapeDtypeStruct((512, 512), BF16)),
        in_specs=[VMEM, VMEM],
        out_specs=(VMEM, VMEM),
        compiler_params=pltpu.CompilerParams(vmem_limit_bytes=12 * MIB),
        cost_estimate=cost(1e8, 2e6),
        name="weights",
    )(occ, virt)


def apply_green(m_ref, w1_ref, w2_ref, y_ref, out_ref):
    for j in range(4):
        for c in range(3):
            lo, hi = max(c - 1, 0), min(c + 1, 2) + 1
            x = jnp.concatenate([m_ref[:, a * 1024 + j * 256 : a * 1024 + (j + 1) * 256] for a in range(lo, hi)], axis=1)
            y = dot(x, w1_ref[lo * 256 : hi * 256, c * 256 : (c + 1) * 256])
            y_ref[:, j * 768 + c * 256 : j * 768 + (c + 1) * 256] = y.astype(BF16)
    for c in range(3):
        for h in range(2):
            at = c * 256 + h * 128
            x = jnp.concatenate([y_ref[:, j * 768 + at : j * 768 + at + 128] for j in range(4)], axis=1)
            z = dot(x, w2_ref[...]).astype(BF16)
            for j in range(4):
                col = c * 1024 + j * 256 + h * 128
                out_ref[:, col : col + 128] = z[:, j * 128 : (j + 1) * 128]


def green_kernel(m0_ref, m1_ref, w1_ref, w2_ref, out_ref, kept_ref, y_ref):
    kept_ref[0] = m0_ref[...]
    kept_ref[1] = m1_ref[...]

    @pl.loop(0, 2)
    def _(c):
        apply_green(kept_ref.at[c], w1_ref, w2_ref, y_ref, out_ref.at[c])


def green(ms, w1, w2):
    rows = ms[0].shape[0]
    return pl.pallas_call(
        green_kernel,
        out_shape=(jax.ShapeDtypeStruct((2, rows, 3072), BF16),) * 2,
        in_specs=[VMEM] * 4,
        out_specs=(VMEM,) * 2,
        scratch_shapes=[pltpu.VMEM((rows, 3072), BF16)],
        compiler_params=pltpu.CompilerParams(vmem_limit_bytes=12 * MIB),
        cost_estimate=cost(rows * 14e6, rows * 3072 * 12),
        name="green",
    )(*ms, w1, w2)


def halves_to(x, out_ref, i):
    width = out_ref.shape[3]
    for h in range(2):
        out_ref[h, i] = x[:, h * width : (h + 1) * width].astype(BF16)


def own_kernel(c, b_ref, m_ref, out_ref):
    @pl.loop(0, 2)
    def _(i):
        halves_to(dot_t(b_ref[i], m_ref[c]), out_ref, i)


def own(b, m, c):
    rows = m.shape[1]
    return pl.pallas_call(
        functools.partial(own_kernel, c),
        out_shape=jax.ShapeDtypeStruct((2, 2, rows, rows // 2), BF16),
        in_specs=[VMEM] * 2,
        out_specs=VMEM,
        compiler_params=pltpu.CompilerParams(vmem_limit_bytes=12 * MIB),
        cost_estimate=cost(4 * rows * rows * 3072, 3 * rows * 3072 * 2),
        name="own",
    )(b, m)


USERS = {"f1": (1, 2), "f2": (2, 3), "g": (2, 2)}


def place():
    r, odd = lax.axis_index("ri"), lax.axis_index("orb") % 2
    return jnp.where(odd == 1, 3 - r, r), odd


def pair_kernel(kind, m_ref, w1_ref, w2_ref, kept_ref, green_ref, mine_ref, theirs_ref, b_ref, y_ref):
    p, _ = place()
    first, last = USERS[kind]

    @pl.when((p >= first) & (p <= last))
    def _():
        apply_green(m_ref, w1_ref, w2_ref, y_ref, b_ref)

        @pl.loop(0, 2)
        def _(i):
            halves_to(dot_t(b_ref[...], kept_ref[i]), theirs_ref, i)
            halves_to(dot_t(green_ref[i], m_ref[...]), mine_ref, i)


def pair(kind, m, w1, w2, kept, b):
    rows = m.shape[0]
    block = jax.ShapeDtypeStruct((2, 2, rows, rows // 2), BF16)
    return pl.pallas_call(
        functools.partial(pair_kernel, kind),
        out_shape=(block, block, jax.ShapeDtypeStruct(m.shape, BF16)),
        in_specs=[VMEM] * 5,
        out_specs=(VMEM,) * 3,
        scratch_shapes=[pltpu.VMEM((rows, 3072), BF16)],
        compiler_params=pltpu.CompilerParams(vmem_limit_bytes=12 * MIB),
        cost_estimate=cost(rows * 7e6 + 8 * rows * rows * 3072, 5 * rows * 3072 * 2),
    )(m, w1, w2, kept, b)


def cross_kernel(m_ref, b_ref, m0_ref, m1_ref, b0_ref, b1_ref, held_ref, up_ref, down_ref):
    @pl.when(place()[0] == 2)
    def _():
        for i, (far_m_ref, far_b_ref) in enumerate(((m0_ref, b0_ref), (m1_ref, b1_ref))):
            halves_to(dot_t(b_ref[...], far_m_ref[...]), down_ref, i)
            halves_to(dot_t(far_b_ref[...], m_ref[...]), up_ref.at[1], i)
        up_ref[0] = held_ref[...]


def cross(m, b, ms, bs, held):
    rows = m.shape[0]
    return pl.pallas_call(
        cross_kernel,
        out_shape=(jax.ShapeDtypeStruct((2,) + held.shape, BF16), jax.ShapeDtypeStruct(held.shape, BF16)),
        in_specs=[VMEM] * 7,
        out_specs=(VMEM,) * 2,
        compiler_params=pltpu.CompilerParams(vmem_limit_bytes=12 * MIB),
        cost_estimate=cost(8 * rows * rows * 3072, 5 * rows * 3072 * 2),
        name="cross",
    )(m, b, *ms, *bs, held)


def select_kernel(own_ref, m1_ref, m2_ref, mg_ref, t1_ref, t2_ref, up_ref, down_ref, *refs):
    outs, all_ref = refs[:-1], refs[-1]
    p, odd = place()
    me = lax.axis_index("orb")

    def put(used, at, x_ref, *index):
        @pl.when(used)
        def _():
            q = jnp.where(odd == 1, 3 - at, at)
            for h in range(2):
                all_ref[(q * 2 + h) ^ me] = x_ref[(*index, h)]

    put(p >= 0, p, own_ref)
    put((p == 1) | (p == 2), p - 1, m1_ref)
    put(p >= 2, p - 2, m2_ref)
    put(p == 2, 3, mg_ref)
    put(p <= 1, p + 1, t1_ref)
    put(p <= 1, p + 2, t2_ref)
    put(p == 3, 2, up_ref, 0)
    put(p == 3, 0, up_ref, 1)
    put(p == 0, 3, down_ref)
    for k, out_ref in enumerate(outs):
        out_ref[...] = all_ref[k]


def select(parts):
    shape = (2,) + parts[0].shape[2:]
    return pl.pallas_call(
        select_kernel,
        out_shape=(jax.ShapeDtypeStruct(shape, BF16),) * 8,
        in_specs=[VMEM] * len(parts),
        out_specs=(VMEM,) * 8,
        scratch_shapes=[pltpu.VMEM((8,) + shape, BF16)],
        compiler_params=pltpu.CompilerParams(vmem_limit_bytes=12 * MIB),
        cost_estimate=cost(1e5, 16 * parts[0].size),
        name="select",
    )(*parts)


def total_kernel(per, *refs):
    x0, x1, out_ref = refs[:8], refs[8:16], refs[16]
    _, rows, width = x0[0].shape
    me = lax.axis_index("orb")
    r, q = lax.axis_index("ri"), me // 2
    straight = []
    for other in range(2):
        odd = (me + other) % 2
        p, t = jnp.where(odd == 1, 3 - r, r), jnp.where(odd == 1, 3 - q, q)
        straight.append((p == t) | ((t < p) & (t < 2)) | ((t > p) & (p >= 2)))
    blocks = width // per
    lane = iota((per, width), 1) // per
    for o in range(rows // per):
        at = slice(o * per, (o + 1) * per)

        def sums(xs, i, at=at):
            x = xs[0][i, at].astype(F32)
            for x_ref in xs[1:]:
                x = x + x_ref[i, at].astype(F32)
            return x

        quads = {(0, 0): sums(x0, 0), (1, 1): sums(x1, 1)}
        low, high = 0.0, 0.0
        for other in range(2):
            a, b = sums(x0[other::2], 1), sums(x1[other::2], 0)
            low = low + jnp.where(straight[other], a, b)
            high = high + jnp.where(straight[other], b, a)
        quads[1, 0], quads[0, 1] = low, high
        for i in range(2):
            for tile in range(2):
                moved = None
                for b in range(blocks):
                    came = blocks // 2 * tile + b // 2
                    shift = ((b - came) * per) % width
                    x = quads[i, b % 2]
                    x = pltpu.roll(x, shift, 1) if shift else x
                    moved = x if moved is None else jnp.where(lane == b, x, moved)
                to = (o * 2 + i) * per
                out_ref[to : to + per, tile * width : (tile + 1) * width] = moved


def total(per, parts):
    _, rows, width = parts[0].shape
    return pl.pallas_call(
        functools.partial(total_kernel, per),
        out_shape=jax.ShapeDtypeStruct((2 * rows, 2 * width), F32),
        in_specs=[VMEM] * len(parts),
        out_specs=VMEM,
        compiler_params=pltpu.CompilerParams(vmem_limit_bytes=12 * MIB),
        cost_estimate=cost(1e7, 4 * parts[0].size),
        name="total",
    )(*parts)


def local(planes, orbs, integrals, screen, green_occ, green_virt):
    rows, groups, _ = integrals.shape
    per = rows // CHUNKS

    def send(x, pairs):
        flat = []
        for orb in range(orbs):
            for source, target in pairs:
                if orb % 2:
                    source, target = planes - 1 - source, planes - 1 - target
                flat.append((source * orbs + orb, target * orbs + orb))
        return lax.ppermute(x, ("ri", "orb"), flat)

    def swap(x):
        return lax.all_to_all(x, "orb", split_axis=0, concat_axis=0, tiled=True)

    x = integrals.reshape(rows * groups, 3072)
    screen = screen.reshape(-1)
    w1, w2 = weights(green_occ, green_virt)

    def xors(pieces):
        out = [pieces[0]]
        for k in range(1, orbs):
            pairs = [(q * orbs + i, q * orbs + (i ^ k)) for q in range(planes) for i in range(orbs)]
            out.append(lax.ppermute(pieces[k], ("ri", "orb"), pairs))
        return out

    ms = []
    for c in range(CHUNKS):
        m, *halves = prep(c, x, screen, groups, per, c > 0)
        ms.append(swap(m).reshape(orbs * per, 3072))
    b, kept = green(ms, w1, w2)
    even = lax.ppermute(halves[0], "ri", [(0, 1), (1, 2)])
    odd = lax.ppermute(halves[1], "ri", [(3, 2), (2, 1)])
    pieces = unpack(even, odd)
    pieces = xors(pieces)
    hopped = assemble(pieces)

    mine, theirs, b_of, got = {}, {}, {}, {}
    for c in range(CHUNKS):
        got["f1", c] = send(ms[c], [(0, 1), (1, 2)]) if c == 0 else hopped
        got["f2", c] = send(got["f1", c], [(1, 2), (2, 3)])
        got["g", c] = send(ms[c], [(3, 2)])
        for kind in USERS:
            mine[kind, c], theirs[kind, c], b_of[kind, c] = pair(kind, got[kind, c], w1, w2, kept, b)
    sums = []
    for c in range(CHUNKS):
        own_block = own(b, kept, c)
        far = [[x["g", i] for i in range(CHUNKS)] for x in (got, b_of)]
        up, down = cross(got["f2", c], b_of["f2", c], *far, theirs["g", c])
        back = [
            send(theirs["f1", c], [(1, 0), (2, 1)]),
            send(theirs["f2", c], [(2, 0), (3, 1)]),
            send(up, [(2, 3)]),
            send(down, [(2, 0)]),
        ]
        pieces = select([own_block] + [mine[kind, c] for kind in USERS] + back)
        sums += xors(pieces)
    return total(per, sums)


def padded_2(block, sides, width):
    for axis, dim in sides:
        count = lax.axis_size(axis)
        forward = [(i, i + 1) for i in range(count - 1)]
        backward = [(target, source) for source, target in forward]
        low = lax.ppermute(
            lax.slice_in_dim(block, block.shape[dim] - width, None, axis=dim), axis, forward
        )
        high = lax.ppermute(lax.slice_in_dim(block, 0, width, axis=dim), axis, backward)
        block = jnp.concatenate([low, block, high], axis=dim)
    return block


def green_apply(extended, green_occ, green_ext):
    groups = green_occ.shape[0]
    rows = extended.shape[0]
    basis = green_occ.shape[-1]
    shaped = extended.reshape(rows, groups + 2, basis, 3, basis)
    total = None
    for t in range(3):
        slab = shaped[:, t : t + groups]
        padded = jnp.pad(slab, ((0, 0), (0, 0), (0, 0), (1, 1), (0, 0)))
        window = padded[:, :, :, 2 - t : 5 - t]
        term = jnp.einsum(
            "gnm,pgmsl->pgnsl", green_occ[:, t], window, preferred_element_type=jnp.float32
        )
        total = term if total is None else total + term
    occ_side = total.astype(jnp.bfloat16)
    chosen = jnp.stack([green_ext[s : s + groups] for s in range(3)], axis=1)
    both = jnp.einsum("pgnsl,gsla->pgnsa", occ_side, chosen, preferred_element_type=jnp.float32)
    return both.astype(jnp.bfloat16).reshape(rows, groups, -1)


def local_any(integrals, screen, green_occ, green_virt):
    rows = integrals.shape[0]
    groups = integrals.shape[1]
    basis = green_occ.shape[-1]
    blocks = jnp.repeat(screen, RB, axis=2)
    target = jnp.arange(groups)[:, None] + jnp.arange(3)[None, :] - 1
    inside = ((target >= 0) & (target < groups)).astype(jnp.int32)
    keep = jnp.transpose(blocks * inside[:, :, None], (2, 0, 1)).astype(jnp.bfloat16)
    shaped = integrals.reshape(rows, groups, basis, 3, basis)
    masked = (shaped * keep[:, :, None, :, None]).reshape(rows, groups, -1)
    green_ext = jnp.pad(green_virt, ((1, 1), (0, 0), (0, 0)))
    masked_mine = lax.all_to_all(masked, "orb", split_axis=1, concat_axis=0, tiled=True)
    local_groups = masked_mine.shape[1]
    first = lax.axis_index("orb") * local_groups
    extended = padded_2(masked_mine, (("orb", 1),), 1)
    occ_mine = lax.dynamic_slice_in_dim(green_occ, first, local_groups, 0)
    virt_mine = lax.dynamic_slice_in_dim(green_ext, first, local_groups + 2, 0)
    both_mine = green_apply(extended, occ_mine, virt_mine)
    left = both_mine.reshape(both_mine.shape[0], -1)
    piece = lax.all_gather(masked_mine, "ri", axis=0, tiled=True)
    right = piece.reshape(piece.shape[0], -1)
    partial_chi = lax.dot_general(
        left, right, (((1,), (1,)), ((), ())), preferred_element_type=jnp.float32
    )
    return lax.psum_scatter(partial_chi, "orb", scatter_dimension=1, tiled=True)


def solution(mesh):
    planes, orbs = mesh.shape["ri"], mesh.shape["orb"]
    placed = (P(("ri", "orb"), None, None), P(None, None, ("ri", "orb")), P(), P())

    if planes != 4 or orbs != 8:
        return jax.shard_map(local_any, mesh=mesh, in_specs=placed, out_specs=P("ri", "orb"), check_vma=False)

    def body(*args):
        return local(planes, orbs, *args)

    return jax.shard_map(body, mesh=mesh, in_specs=placed, out_specs=P("ri", "orb"), check_vma=False)
```

profile of v0, /device:TPU:0, one launch (start us, length us, event | category | flops | bytes accessed | tf_op | source)
XLA Modules:
  0.0 184.6 jit_solution(15253307785774567018)
XLA Ops:
  0.0 0.8 copy.6
  0.8 0.1 reshape.12.screen_ref
  0.9 2.1 %slice_bitcast_fusion = (bf16[256,3072]{1,0:T(8,128)(2,1)S(1)}, bf16[256,3072]{1,0:T(8,128)(2,1)S(1)}) fusion(bf16[64,8,3072]{2,1,0:T(8,128)(2,1)} %param.4), kind=kLoop, calls=%fused_computation | loop fusion | bytes 6291456 | tf_op jit(solution)/shard_map/slice | solution.py:84
  3.0 4.9 %shard_map.46 = bf16[8,32,3072]{2,1,0:T(8,128)(2,1)} custom-call(s32[96]{0:T(128)S(1)} %reshape.12.screen_ref, bf16[256,3072]{1,0:T(8,128)(2,1)S(1)} %get-tuple-element.108.x_ref), custom_call_target="tpu_custom_call" | custom-call | flops 2415919104 | bytes 3145728 | tf_op jit(solution)/shard_map/pallas_call | solution.py:76
  7.9 5.2 %all-to-all-start = ((bf16[8,32,3072]{2,1,0:T(8,128)(2,1)}), bf16[8,32,3072]{2,1,0:T(8,128)(2,1)}, u32[]{:S(2)}, u32[]{:S(2)}) async-start(bf16[8,32,3072]{2,1,0:T(8,128)(2,1)} %shard_map.46), calls=%async_computation | async-start | bytes 3145728 | tf_op jit(solution)/shard_map/all_to_all | solution.py:395
  13.1 5.0 %shard_map.47 = (bf16[8,32,3072]{2,1,0:T(8,128)(2,1)}, bf16[4,32,3072]{2,1,0:T(8,128)(2,1)S(1)}, bf16[4,32,3072]{2,1,0:T(8,128)(2,1)S(1)}) custom-call(s32[96]{0:T(128)S(1)} %reshape.12.screen_ref, bf16[256,3072]{1,0:T(8,128)(2,1)S(1)} %get-tuple-element.107.x_ref), custom_call_target="tpu_custom_call" | custom-call | flops 2415919104 | bytes 3145728 | tf_op jit(solution)/shard_map/pallas_call | solution.py:76
  18.0 4.1 %collective-permute-start.15 = (bf16[4,32,3072]{2,1,0:T(8,128)(2,1)S(1)}, bf16[4,32,3072]{2,1,0:T(8,128)(2,1)S(1)}, u32[]{:S(2)}, u32[]{:S(2)}) collective-permute-start(bf16[4,32,3072]{2,1,0:T(8,128)(2,1)S(1)} %get-tuple-element.80), channel_id=1, source_target_pairs={{0,8},{8,16},{1,9},{9,17},{2,10},{10,18},{3,11},{11,19},{4,12},{12... | collective-permute-start | bytes 2359304 | tf_op jit(solution)/shard_map/ppermute | solution.py:413
  22.2 0.7 collective-permute-start.16
  22.9 11.3 %all-to-all-done = bf16[8,32,3072]{2,1,0:T(8,128)(2,1)} async-done(((bf16[8,32,3072]{2,1,0:T(8,128)(2,1)}), bf16[8,32,3072]{2,1,0:T(8,128)(2,1)}, u32[]{:S(2)}, u32[]{:S(2)}) %all-to-all-start) | async-done | bytes 1572896 | tf_op jit(solution)/shard_map/all_to_all | solution.py:395
  34.2 4.3 %all-to-all-start.1 = ((bf16[8,32,3072]{2,1,0:T(8,128)(2,1)}), bf16[8,32,3072]{2,1,0:T(8,128)(2,1)}, u32[]{:S(2)}, u32[]{:S(2)}) async-start(bf16[8,32,3072]{2,1,0:T(8,128)(2,1)} %get-tuple-element.56), calls=%async_computation.1 | async-start | bytes 3145728 | tf_op jit(solution)/shard_map/all_to_all | solution.py:395
  38.5 5.1 %collective-permute-start = (bf16[256,3072]{1,0:T(8,128)(2,1)}, bf16[256,3072]{1,0:T(8,128)(2,1)}, u32[]{:S(2)}, u32[]{:S(2)}) collective-permute-start(bf16[256,3072]{1,0:T(8,128)(2,1)} %bitcast.1.m0_ref), channel_id=1, source_target_pairs={{0,8},{8,16},{25,17},{17,9},{2,10},{10,18},{27,19},{19,11},{4,12},... | collective-permute-start | bytes 4718600 | tf_op jit(solution)/shard_map/ppermute | solution.py:392
  43.6 0.2 unpack.1
  43.8 0.1 collective-permute-start.17
  43.9 2.0 %collective-permute-start.18 = (bf16[32,3072]{1,0:T(8,128)(2,1)S(1)}, bf16[32,3072]{1,0:T(8,128)(2,1)S(1)}, u32[]{:S(2)}, u32[]{:S(2)}) collective-permute-start(bf16[32,3072]{1,0:T(8,128)(2,1)S(1)} %get-tuple-element.84), channel_id=1, source_target_pairs={{0,2},{1,3},{2,0},{3,1},{4,6},{5,7},{6,4},{7,5},{8,10},{9,11},{10,... | collective-permute-start | bytes 589832 | tf_op jit(solution)/shard_map/ppermute | solution.py:405
  45.9 1.8 collective-permute-start.20
  47.7 15.6 %collective-permute-done.18.refs_2_ = bf16[32,3072]{1,0:T(8,128)(2,1)S(1)} collective-permute-done((bf16[32,3072]{1,0:T(8,128)(2,1)S(1)}, bf16[32,3072]{1,0:T(8,128)(2,1)S(1)}, u32[]{:S(2)}, u32[]{:S(2)}) %collective-permute-start.18) | collective-permute-done | bytes 196640 | tf_op jit(solution)/shard_map/ppermute | solution.py:405
  63.3 1.5 collective-permute-start.22
  64.7 1.6 collective-permute-done.19.refs_3_
  66.3 2.0 %collective-permute-start.23 = (bf16[32,3072]{1,0:T(8,128)(2,1)S(1)}, bf16[32,3072]{1,0:T(8,128)(2,1)S(1)}, u32[]{:S(2)}, u32[]{:S(2)}) collective-permute-start(bf16[32,3072]{1,0:T(8,128)(2,1)S(1)} %get-tuple-element.89), channel_id=1, source_target_pairs={{0,7},{1,6},{2,5},{3,4},{4,3},{5,2},{6,1},{7,0},{8,15},{9,14},{10,... | collective-permute-start | bytes 589832 | tf_op jit(solution)/shard_map/ppermute | solution.py:405
  68.4 4.2 %collective-permute-done.22.refs_6_ = bf16[32,3072]{1,0:T(8,128)(2,1)S(1)} collective-permute-done((bf16[32,3072]{1,0:T(8,128)(2,1)S(1)}, bf16[32,3072]{1,0:T(8,128)(2,1)S(1)}, u32[]{:S(2)}, u32[]{:S(2)}) %collective-permute-start.22) | collective-permute-done | bytes 196640 | tf_op jit(solution)/shard_map/ppermute | solution.py:405
  72.6 3.1 %collective-permute-done.23.refs_7_ = bf16[32,3072]{1,0:T(8,128)(2,1)S(1)} collective-permute-done((bf16[32,3072]{1,0:T(8,128)(2,1)S(1)}, bf16[32,3072]{1,0:T(8,128)(2,1)S(1)}, u32[]{:S(2)}, u32[]{:S(2)}) %collective-permute-start.23) | collective-permute-done | bytes 196640 | tf_op jit(solution)/shard_map/ppermute | solution.py:405
  75.7 1.3 assemble.1.m_ref
  77.0 0.7 collective-permute-start.24
  77.8 0.8 collective-permute-start.2
  78.6 0.8 collective-permute-start.5
  79.3 1.1 weights.1
  80.4 0.8 collective-permute-start.1
  81.2 6.0 %green.1 = (bf16[2,256,3072]{2,1,0:T(8,128)(2,1)S(1)}, bf16[2,256,3072]{2,1,0:T(8,128)(2,1)S(1)}) custom-call(bf16[256,3072]{1,0:T(8,128)(2,1)} %bitcast.1.m0_ref, bf16[256,3072]{1,0:T(8,128)(2,1)} %bitcast.3.m1_ref, bf16[768,768]{1,0:T(8,128)(2,1)S(1)} %get-tuple-element.57.w1_ref, bf16[512,512]{1,0:T(8,128)(2,1)S(1)} %get-tuple-element.58.w2_ref), custom_call_target="tpu_custom_call" | custom-call | flops 3584000000 | bytes 9437184 | tf_op jit(solution)/shard_map/green/pallas_call | solution.py:193
  87.2 2.6 %shard_map.52 = (bf16[2,2,256,128]{3,2,1,0:T(8,128)(2,1)S(1)}, bf16[2,2,256,128]{3,2,1,0:T(8,128)(2,1)S(1)}, bf16[256,3072]{1,0:T(8,128)(2,1)}) custom-call(bf16[256,3072]{1,0:T(8,128)(2,1)} %assemble.1.m_ref, bf16[768,768]{1,0:T(8,128)(2,1)S(1)} %get-tuple-element.57.w1_ref, bf16[512,512]{1,0:T(8,128)(2,1)S(1)} %get-tuple-element.58.w2_ref, ...), custom_call_target="tpu_custom_call" | custom-call | flops 3402612736 | bytes 7864320 | tf_op jit(solution)/shard_map/pallas_call | solution.py:255
  89.7 1.3 collective-permute-start.25
  91.1 1.3 collective-permute-start.26
  92.5 0.7 collective-permute-start.27
  93.2 1.3 collective-permute-start.28
  94.5 0.2 shard_map.49
  94.8 0.7 collective-permute-start.6
  95.5 2.6 %shard_map.48 = (bf16[2,2,256,128]{3,2,1,0:T(8,128)(2,1)S(1)}, bf16[2,2,256,128]{3,2,1,0:T(8,128)(2,1)S(1)}, bf16[256,3072]{1,0:T(8,128)(2,1)}) custom-call(bf16[256,3072]{1,0:T(8,128)(2,1)} %collective-permute-done.m_ref, bf16[768,768]{1,0:T(8,128)(2,1)S(1)} %get-tuple-element.57.w1_ref, bf16[512,512]{1,0:T(8,128)(2,1)S(1)} %get-tuple-element.58.w2_ref, ...), custom_call_target="tpu_custom_call" | custom-call | flops 3402612736 | bytes 7864320 | tf_op jit(solution)/shard_map/pallas_call | solution.py:255
  98.1 13.4 %collective-permute-done.25.t1_ref = bf16[2,2,256,128]{3,2,1,0:T(8,128)(2,1)S(1)} collective-permute-done((bf16[2,2,256,128]{3,2,1,0:T(8,128)(2,1)S(1)}, bf16[2,2,256,128]{3,2,1,0:T(8,128)(2,1)S(1)}, u32[]{:S(2)}, u32[]{:S(2)}) %collective-permute-start.25) | collective-permute-done | bytes 262176 | tf_op jit(solution)/shard_map/ppermute | solution.py:392
  111.4 1.3 collective-permute-start.3
  112.7 5.9 %collective-permute-done.26.t2_ref = bf16[2,2,256,128]{3,2,1,0:T(8,128)(2,1)S(1)} collective-permute-done((bf16[2,2,256,128]{3,2,1,0:T(8,128)(2,1)S(1)}, bf16[2,2,256,128]{3,2,1,0:T(8,128)(2,1)S(1)}, u32[]{:S(2)}, u32[]{:S(2)}) %collective-permute-start.26) | collective-permute-done | bytes 262176 | tf_op jit(solution)/shard_map/ppermute | solution.py:392
  118.6 1.3 collective-permute-start.4
  119.9 15.9 %collective-permute-done.28.down_ref = bf16[2,2,256,128]{3,2,1,0:T(8,128)(2,1)S(1)} collective-permute-done((bf16[2,2,256,128]{3,2,1,0:T(8,128)(2,1)S(1)}, bf16[2,2,256,128]{3,2,1,0:T(8,128)(2,1)S(1)}, u32[]{:S(2)}, u32[]{:S(2)}) %collective-permute-start.28) | collective-permute-done | bytes 262176 | tf_op jit(solution)/shard_map/ppermute | solution.py:392
  135.8 1.3 collective-permute-start.7
  137.1 1.2 own.3.own_ref
  138.4 0.2 select.3
  138.6 0.1 collective-permute-start.29
  138.6 3.7 %collective-permute-done.3.t1_ref = bf16[2,2,256,128]{3,2,1,0:T(8,128)(2,1)S(1)} collective-permute-done((bf16[2,2,256,128]{3,2,1,0:T(8,128)(2,1)S(1)}, bf16[2,2,256,128]{3,2,1,0:T(8,128)(2,1)S(1)}, u32[]{:S(2)}, u32[]{:S(2)}) %collective-permute-start.3) | collective-permute-done | bytes 262176 | tf_op jit(solution)/shard_map/ppermute | solution.py:392
  142.4 0.6 collective-permute-start.30
  142.9 10.9 %collective-permute-done.4.t2_ref = bf16[2,2,256,128]{3,2,1,0:T(8,128)(2,1)S(1)} collective-permute-done((bf16[2,2,256,128]{3,2,1,0:T(8,128)(2,1)S(1)}, bf16[2,2,256,128]{3,2,1,0:T(8,128)(2,1)S(1)}, u32[]{:S(2)}, u32[]{:S(2)}) %collective-permute-start.4) | collective-permute-done | bytes 262176 | tf_op jit(solution)/shard_map/ppermute | solution.py:392
  153.8 2.8 %collective-permute-done.7.down_ref = bf16[2,2,256,128]{3,2,1,0:T(8,128)(2,1)S(1)} collective-permute-done((bf16[2,2,256,128]{3,2,1,0:T(8,128)(2,1)S(1)}, bf16[2,2,256,128]{3,2,1,0:T(8,128)(2,1)S(1)}, u32[]{:S(2)}, u32[]{:S(2)}) %collective-permute-start.7) | collective-permute-done | bytes 262176 | tf_op jit(solution)/shard_map/ppermute | solution.py:392
  156.6 0.3 collective-permute-start.32
  156.9 1.2 own.2.own_ref
  158.1 0.1 collective-permute-start.33
  158.2 0.2 select.2
  158.4 1.8 collective-permute-start.34
  160.2 2.3 %collective-permute-start.35 = (bf16[2,256,128]{2,1,0:T(8,128)(2,1)S(1)}, bf16[2,256,128]{2,1,0:T(8,128)(2,1)S(1)}, u32[]{:S(2)}, u32[]{:S(2)}) collective-permute-start(bf16[2,256,128]{2,1,0:T(8,128)(2,1)S(1)} %get-tuple-element.106), channel_id=1, source_target_pairs={{0,7},{1,6},{2,5},{3,4},{4,3},{5,2},{6,1},{7,0},{8,15},{9,14},{10,... | collective-permute-start | bytes 393224 | tf_op jit(solution)/shard_map/ppermute | solution.py:405
  162.6 0.6 collective-permute-start.9
  163.2 6.4 %collective-permute-done.33.refs_13_ = bf16[2,256,128]{2,1,0:T(8,128)(2,1)S(1)} collective-permute-done((bf16[2,256,128]{2,1,0:T(8,128)(2,1)S(1)}, bf16[2,256,128]{2,1,0:T(8,128)(2,1)S(1)}, u32[]{:S(2)}, u32[]{:S(2)}) %collective-permute-start.33) | collective-permute-done | bytes 131104 | tf_op jit(solution)/shard_map/ppermute | solution.py:405
  169.6 0.7 collective-permute-start.10
  170.3 1.4 collective-permute-start.12
  171.7 1.6 collective-permute-start.13
  173.3 1.4 collective-permute-start.14
  174.7 7.6 %collective-permute-done.11.refs_4_ = bf16[2,256,128]{2,1,0:T(8,128)(2,1)S(1)} collective-permute-done((bf16[2,256,128]{2,1,0:T(8,128)(2,1)S(1)}, bf16[2,256,128]{2,1,0:T(8,128)(2,1)S(1)}, u32[]{:S(2)}, u32[]{:S(2)}) %collective-permute-start.11) | collective-permute-done | bytes 131104 | tf_op jit(solution)/shard_map/ppermute | solution.py:405
  182.3 1.0 collective-permute-done.12.refs_5_
  183.3 1.3 total.1
  (38 shorter events, 0.2 us)
Async XLA Ops:
  7.9 26.3 %all-to-all-start = ((bf16[8,32,3072]{2,1,0:T(8,128)(2,1)}), bf16[8,32,3072]{2,1,0:T(8,128)(2,1)}, u32[]{:S(2)}, u32[]{:S(2)}) async-start(bf16[8,32,3072]{2,1,0:T(8,128)(2,1)} %shard_map.46), calls=%async_computation | async-start | bytes 3145728 | tf_op jit(solution)/shard_map/all_to_all | solution.py:395
  18.0 25.5 %collective-permute-start.15 = (bf16[4,32,3072]{2,1,0:T(8,128)(2,1)S(1)}, bf16[4,32,3072]{2,1,0:T(8,128)(2,1)S(1)}, u32[]{:S(2)}, u32[]{:S(2)}) collective-permute-start(bf16[4,32,3072]{2,1,0:T(8,128)(2,1)S(1)} %get-tuple-element.80), channel_id=1, source_target_pairs={{0,8},{8,16},{1,9},{9,17},{2,10},{10,18},{3,11},{11,19},{4,12},{12... | collective-permute-start | bytes 2359304 | tf_op jit(solution)/shard_map/ppermute | solution.py:413
  22.2 21.4 %collective-permute-start.16 = (bf16[4,32,3072]{2,1,0:T(8,128)(2,1)S(1)}, bf16[4,32,3072]{2,1,0:T(8,128)(2,1)S(1)}, u32[]{:S(2)}, u32[]{:S(2)}) collective-permute-start(bf16[4,32,3072]{2,1,0:T(8,128)(2,1)S(1)} %get-tuple-element.81), channel_id=1, source_target_pairs={{24,16},{16,8},{25,17},{17,9},{26,18},{18,10},{27,19},{19,11},{28,... | collective-permute-start | bytes 2359304 | tf_op jit(solution)/shard_map/ppermute | solution.py:414
  34.2 44.4 %all-to-all-start.1 = ((bf16[8,32,3072]{2,1,0:T(8,128)(2,1)}), bf16[8,32,3072]{2,1,0:T(8,128)(2,1)}, u32[]{:S(2)}, u32[]{:S(2)}) async-start(bf16[8,32,3072]{2,1,0:T(8,128)(2,1)} %get-tuple-element.56), calls=%async_computation.1 | async-start | bytes 3145728 | tf_op jit(solution)/shard_map/all_to_all | solution.py:395
  38.5 42.0 %collective-permute-start = (bf16[256,3072]{1,0:T(8,128)(2,1)}, bf16[256,3072]{1,0:T(8,128)(2,1)}, u32[]{:S(2)}, u32[]{:S(2)}) collective-permute-start(bf16[256,3072]{1,0:T(8,128)(2,1)} %bitcast.1.m0_ref), channel_id=1, source_target_pairs={{0,8},{8,16},{25,17},{17,9},{2,10},{10,18},{27,19},{19,11},{4,12},... | collective-permute-start | bytes 4718600 | tf_op jit(solution)/shard_map/ppermute | solution.py:392
  43.8 3.8 %collective-permute-start.17 = (bf16[32,3072]{1,0:T(8,128)(2,1)S(1)}, bf16[32,3072]{1,0:T(8,128)(2,1)S(1)}, u32[]{:S(2)}, u32[]{:S(2)}) collective-permute-start(bf16[32,3072]{1,0:T(8,128)(2,1)S(1)} %get-tuple-element.83), channel_id=1, source_target_pairs={{0,1},{1,0},{2,3},{3,2},{4,5},{5,4},{6,7},{7,6},{8,9},{9,8},{10,11... | collective-permute-start | bytes 589832 | tf_op jit(solution)/shard_map/ppermute | solution.py:405
  43.9 19.3 %collective-permute-start.18 = (bf16[32,3072]{1,0:T(8,128)(2,1)S(1)}, bf16[32,3072]{1,0:T(8,128)(2,1)S(1)}, u32[]{:S(2)}, u32[]{:S(2)}) collective-permute-start(bf16[32,3072]{1,0:T(8,128)(2,1)S(1)} %get-tuple-element.84), channel_id=1, source_target_pairs={{0,2},{1,3},{2,0},{3,1},{4,6},{5,7},{6,4},{7,5},{8,10},{9,11},{10,... | collective-permute-start | bytes 589832 | tf_op jit(solution)/shard_map/ppermute | solution.py:405
  45.9 20.5 %collective-permute-start.19 = (bf16[32,3072]{1,0:T(8,128)(2,1)S(1)}, bf16[32,3072]{1,0:T(8,128)(2,1)S(1)}, u32[]{:S(2)}, u32[]{:S(2)}) collective-permute-start(bf16[32,3072]{1,0:T(8,128)(2,1)S(1)} %get-tuple-element.85), channel_id=1, source_target_pairs={{0,3},{1,2},{2,1},{3,0},{4,7},{5,6},{6,5},{7,4},{8,11},{9,10},{10,... | collective-permute-start | bytes 589832 | tf_op jit(solution)/shard_map/ppermute | solution.py:405
  45.9 22.5 %collective-permute-start.20 = (bf16[32,3072]{1,0:T(8,128)(2,1)S(1)}, bf16[32,3072]{1,0:T(8,128)(2,1)S(1)}, u32[]{:S(2)}, u32[]{:S(2)}) collective-permute-start(bf16[32,3072]{1,0:T(8,128)(2,1)S(1)} %get-tuple-element.86), channel_id=1, source_target_pairs={{0,4},{1,5},{2,6},{3,7},{4,0},{5,1},{6,2},{7,3},{8,12},{9,13},{10,... | collective-permute-start | bytes 589832 | tf_op jit(solution)/shard_map/ppermute | solution.py:405
  47.7 20.7 %collective-permute-start.21 = (bf16[32,3072]{1,0:T(8,128)(2,1)S(1)}, bf16[32,3072]{1,0:T(8,128)(2,1)S(1)}, u32[]{:S(2)}, u32[]{:S(2)}) collective-permute-start(bf16[32,3072]{1,0:T(8,128)(2,1)S(1)} %get-tuple-element.87), channel_id=1, source_target_pairs={{0,5},{1,4},{2,7},{3,6},{4,1},{5,0},{6,3},{7,2},{8,13},{9,12},{10,... | collective-permute-start | bytes 589832 | tf_op jit(solution)/shard_map/ppermute | solution.py:405
  63.3 9.4 %collective-permute-start.22 = (bf16[32,3072]{1,0:T(8,128)(2,1)S(1)}, bf16[32,3072]{1,0:T(8,128)(2,1)S(1)}, u32[]{:S(2)}, u32[]{:S(2)}) collective-permute-start(bf16[32,3072]{1,0:T(8,128)(2,1)S(1)} %get-tuple-element.88), channel_id=1, source_target_pairs={{0,6},{1,7},{2,4},{3,5},{4,2},{5,3},{6,0},{7,1},{8,14},{9,15},{10,... | collective-permute-start | bytes 589832 | tf_op jit(solution)/shard_map/ppermute | solution.py:405
  66.3 9.4 %collective-permute-start.23 = (bf16[32,3072]{1,0:T(8,128)(2,1)S(1)}, bf16[32,3072]{1,0:T(8,128)(2,1)S(1)}, u32[]{:S(2)}, u32[]{:S(2)}) collective-permute-start(bf16[32,3072]{1,0:T(8,128)(2,1)S(1)} %get-tuple-element.89), channel_id=1, source_target_pairs={{0,7},{1,6},{2,5},{3,4},{4,3},{5,2},{6,1},{7,0},{8,15},{9,14},{10,... | collective-permute-start | bytes 589832 | tf_op jit(solution)/shard_map/ppermute | solution.py:405
  75.7 3.6 %copy-start = (bf16[8,3,32,32]{3,2,1,0:T(8,128)(2,1)S(1)}, bf16[8,3,32,32]{3,2,1,0:T(8,128)(2,1)}, u32[]{:S(2)}) copy-start(bf16[8,3,32,32]{3,2,1,0:T(8,128)(2,1)} %occ_ref.1) | copy-start | bytes 147460
  75.7 3.6 %copy-start.1 = (bf16[8,32,32]{2,1,0:T(8,128)(2,1)S(1)}, bf16[8,32,32]{2,1,0:T(8,128)(2,1)}, u32[]{:S(2)}) copy-start(bf16[8,32,32]{2,1,0:T(8,128)(2,1)} %virt_ref.1) | copy-start | bytes 49156
  77.0 14.0 %collective-permute-start.24 = (bf16[256,3072]{1,0:T(8,128)(2,1)}, bf16[256,3072]{1,0:T(8,128)(2,1)S(1)}, u32[]{:S(2)}, u32[]{:S(2)}) collective-permute-start(bf16[256,3072]{1,0:T(8,128)(2,1)} %assemble.1.m_ref), channel_id=1, source_target_pairs={{8,16},{16,24},{17,9},{9,1},{10,18},{18,26},{19,11},{11,3},{12,20}... | collective-permute-start | bytes 4718600 | tf_op jit(solution)/shard_map/ppermute | solution.py:392
  77.8 14.6 %collective-permute-start.2 = (bf16[256,3072]{1,0:T(8,128)(2,1)}, bf16[256,3072]{1,0:T(8,128)(2,1)S(1)}, u32[]{:S(2)}, u32[]{:S(2)}) collective-permute-start(bf16[256,3072]{1,0:T(8,128)(2,1)} %bitcast.1.m0_ref), channel_id=1, source_target_pairs={{24,16},{1,9},{26,18},{3,11},{28,20},{5,13},{30,22},{7,15}} | collective-permute-start | bytes 4718600 | tf_op jit(solution)/shard_map/ppermute | solution.py:392
  78.6 13.8 %collective-permute-start.5 = (bf16[256,3072]{1,0:T(8,128)(2,1)}, bf16[256,3072]{1,0:T(8,128)(2,1)S(1)}, u32[]{:S(2)}, u32[]{:S(2)}) collective-permute-start(bf16[256,3072]{1,0:T(8,128)(2,1)} %bitcast.3.m1_ref), channel_id=1, source_target_pairs={{24,16},{1,9},{26,18},{3,11},{28,20},{5,13},{30,22},{7,15}} | collective-permute-start | bytes 4718600 | tf_op jit(solution)/shard_map/ppermute | solution.py:392
  80.4 14.1 %collective-permute-start.1 = (bf16[256,3072]{1,0:T(8,128)(2,1)}, bf16[256,3072]{1,0:T(8,128)(2,1)S(1)}, u32[]{:S(2)}, u32[]{:S(2)}) collective-permute-start(bf16[256,3072]{1,0:T(8,128)(2,1)} %collective-permute-done.m_ref), channel_id=1, source_target_pairs={{8,16},{16,24},{17,9},{9,1},{10,18},{18,26},{19,11},{11,3},{12,20}... | collective-permute-start | bytes 4718600 | tf_op jit(solution)/shard_map/ppermute | solution.py:392
  89.7 21.7 %collective-permute-start.25 = (bf16[2,2,256,128]{3,2,1,0:T(8,128)(2,1)S(1)}, bf16[2,2,256,128]{3,2,1,0:T(8,128)(2,1)S(1)}, u32[]{:S(2)}, u32[]{:S(2)}) collective-permute-start(bf16[2,2,256,128]{3,2,1,0:T(8,128)(2,1)S(1)} %get-tuple-element.93), channel_id=1, source_target_pairs={{8,0},{16,8},{17,25},{9,17},{10,2},{18,10},{19,27},{11,19},{12,4},... | collective-permute-start | bytes 786440 | tf_op jit(solution)/shard_map/ppermute | solution.py:392
  91.1 27.5 %collective-permute-start.26 = (bf16[2,2,256,128]{3,2,1,0:T(8,128)(2,1)S(1)}, bf16[2,2,256,128]{3,2,1,0:T(8,128)(2,1)S(1)}, u32[]{:S(2)}, u32[]{:S(2)}) collective-permute-start(bf16[2,2,256,128]{3,2,1,0:T(8,128)(2,1)S(1)} %get-tuple-element.94), channel_id=1, source_target_pairs={{16,0},{24,8},{9,25},{1,17},{18,2},{26,10},{11,27},{3,19},{20,4},{... | collective-permute-start | bytes 786440 | tf_op jit(solution)/shard_map/ppermute | solution.py:392
  92.5 45.9 %collective-permute-start.27 = (bf16[2,2,2,256,128]{4,3,2,1,0:T(8,128)(2,1)S(1)}, bf16[2,2,2,256,128]{4,3,2,1,0:T(8,128)(2,1)S(1)}, u32[]{:S(2)}, u32[]{:S(2)}) collective-permute-start(bf16[2,2,2,256,128]{4,3,2,1,0:T(8,128)(2,1)S(1)} %get-tuple-element.97), channel_id=1, source_target_pairs={{16,24},{9,1},{18,26},{11,3},{20,28},{13,5},{22,30},{15,7}} | collective-permute-start | bytes 1572872 | tf_op jit(solution)/shard_map/ppermute | solution.py:392
  93.2 42.7 %collective-permute-start.28 = (bf16[2,2,256,128]{3,2,1,0:T(8,128)(2,1)S(1)}, bf16[2,2,256,128]{3,2,1,0:T(8,128)(2,1)S(1)}, u32[]{:S(2)}, u32[]{:S(2)}) collective-permute-start(bf16[2,2,256,128]{3,2,1,0:T(8,128)(2,1)S(1)} %get-tuple-element.98), channel_id=1, source_target_pairs={{16,0},{9,25},{18,2},{11,27},{20,4},{13,29},{22,6},{15,31}} | collective-permute-start | bytes 786440 | tf_op jit(solution)/shard_map/ppermute | solution.py:392
  94.8 63.3 %collective-permute-start.6 = (bf16[2,2,2,256,128]{4,3,2,1,0:T(8,128)(2,1)S(1)}, bf16[2,2,2,256,128]{4,3,2,1,0:T(8,128)(2,1)S(1)}, u32[]{:S(2)}, u32[]{:S(2)}) collective-permute-start(bf16[2,2,2,256,128]{4,3,2,1,0:T(8,128)(2,1)S(1)} %get-tuple-element.70), channel_id=1, source_target_pairs={{16,24},{9,1},{18,26},{11,3},{20,28},{13,5},{22,30},{15,7}} | collective-permute-start | bytes 1572872 | tf_op jit(solution)/shard_map/ppermute | solution.py:392
  111.4 31.0 %collective-permute-start.3 = (bf16[2,2,256,128]{3,2,1,0:T(8,128)(2,1)S(1)}, bf16[2,2,256,128]{3,2,1,0:T(8,128)(2,1)S(1)}, u32[]{:S(2)}, u32[]{:S(2)}) collective-permute-start(bf16[2,2,256,128]{3,2,1,0:T(8,128)(2,1)S(1)} %get-tuple-element.64), channel_id=1, source_target_pairs={{8,0},{16,8},{17,25},{9,17},{10,2},{18,10},{19,27},{11,19},{12,4},... | collective-permute-start | bytes 786440 | tf_op jit(solution)/shard_map/ppermute | solution.py:392
  118.6 35.2 %collective-permute-start.4 = (bf16[2,2,256,128]{3,2,1,0:T(8,128)(2,1)S(1)}, bf16[2,2,256,128]{3,2,1,0:T(8,128)(2,1)S(1)}, u32[]{:S(2)}, u32[]{:S(2)}) collective-permute-start(bf16[2,2,256,128]{3,2,1,0:T(8,128)(2,1)S(1)} %get-tuple-element.65), channel_id=1, source_target_pairs={{16,0},{24,8},{9,25},{1,17},{18,2},{26,10},{11,27},{3,19},{20,4},{... | collective-permute-start | bytes 786440 | tf_op jit(solution)/shard_map/ppermute | solution.py:392
  135.8 20.8 %collective-permute-start.7 = (bf16[2,2,256,128]{3,2,1,0:T(8,128)(2,1)S(1)}, bf16[2,2,256,128]{3,2,1,0:T(8,128)(2,1)S(1)}, u32[]{:S(2)}, u32[]{:S(2)}) collective-permute-start(bf16[2,2,256,128]{3,2,1,0:T(8,128)(2,1)S(1)} %get-tuple-element.71), channel_id=1, source_target_pairs={{16,0},{9,25},{18,2},{11,27},{20,4},{13,29},{22,6},{15,31}} | collective-permute-start | bytes 786440 | tf_op jit(solution)/shard_map/ppermute | solution.py:392
  138.6 19.8 %collective-permute-start.29 = (bf16[2,256,128]{2,1,0:T(8,128)(2,1)S(1)}, bf16[2,256,128]{2,1,0:T(8,128)(2,1)S(1)}, u32[]{:S(2)}, u32[]{:S(2)}) collective-permute-start(bf16[2,256,128]{2,1,0:T(8,128)(2,1)S(1)} %get-tuple-element.100), channel_id=1, source_target_pairs={{0,1},{1,0},{2,3},{3,2},{4,5},{5,4},{6,7},{7,6},{8,9},{9,8},{10,11... | collective-permute-start | bytes 393224 | tf_op jit(solution)/shard_map/ppermute | solution.py:405
  142.4 17.8 %collective-permute-start.30 = (bf16[2,256,128]{2,1,0:T(8,128)(2,1)S(1)}, bf16[2,256,128]{2,1,0:T(8,128)(2,1)S(1)}, u32[]{:S(2)}, u32[]{:S(2)}) collective-permute-start(bf16[2,256,128]{2,1,0:T(8,128)(2,1)S(1)} %get-tuple-element.101), channel_id=1, source_target_pairs={{0,2},{1,3},{2,0},{3,1},{4,6},{5,7},{6,4},{7,5},{8,10},{9,11},{10,... | collective-permute-start | bytes 393224 | tf_op jit(solution)/shard_map/ppermute | solution.py:405
  153.8 8.8 %collective-permute-start.31 = (bf16[2,256,128]{2,1,0:T(8,128)(2,1)S(1)}, bf16[2,256,128]{2,1,0:T(8,128)(2,1)S(1)}, u32[]{:S(2)}, u32[]{:S(2)}) collective-permute-start(bf16[2,256,128]{2,1,0:T(8,128)(2,1)S(1)} %get-tuple-element.102), channel_id=1, source_target_pairs={{0,3},{1,2},{2,1},{3,0},{4,7},{5,6},{6,5},{7,4},{8,11},{9,10},{10,... | collective-permute-start | bytes 393224 | tf_op jit(solution)/shard_map/ppermute | solution.py:405
  156.6 6.0 %collective-permute-start.32 = (bf16[2,256,128]{2,1,0:T(8,128)(2,1)S(1)}, bf16[2,256,128]{2,1,0:T(8,128)(2,1)S(1)}, u32[]{:S(2)}, u32[]{:S(2)}) collective-permute-start(bf16[2,256,128]{2,1,0:T(8,128)(2,1)S(1)} %get-tuple-element.103), channel_id=1, source_target_pairs={{0,4},{1,5},{2,6},{3,7},{4,0},{5,1},{6,2},{7,3},{8,12},{9,13},{10,... | collective-permute-start | bytes 393224 | tf_op jit(solution)/shard_map/ppermute | solution.py:405
  158.1 11.5 %collective-permute-start.33 = (bf16[2,256,128]{2,1,0:T(8,128)(2,1)S(1)}, bf16[2,256,128]{2,1,0:T(8,128)(2,1)S(1)}, u32[]{:S(2)}, u32[]{:S(2)}) collective-permute-start(bf16[2,256,128]{2,1,0:T(8,128)(2,1)S(1)} %get-tuple-element.104), channel_id=1, source_target_pairs={{0,5},{1,4},{2,7},{3,6},{4,1},{5,0},{6,3},{7,2},{8,13},{9,12},{10,... | collective-permute-start | bytes 393224 | tf_op jit(solution)/shard_map/ppermute | solution.py:405
  158.4 11.9 %collective-permute-start.34 = (bf16[2,256,128]{2,1,0:T(8,128)(2,1)S(1)}, bf16[2,256,128]{2,1,0:T(8,128)(2,1)S(1)}, u32[]{:S(2)}, u32[]{:S(2)}) collective-permute-start(bf16[2,256,128]{2,1,0:T(8,128)(2,1)S(1)} %get-tuple-element.105), channel_id=1, source_target_pairs={{0,6},{1,7},{2,4},{3,5},{4,2},{5,3},{6,0},{7,1},{8,14},{9,15},{10,... | collective-permute-start | bytes 393224 | tf_op jit(solution)/shard_map/ppermute | solution.py:405
  160.2 10.1 %collective-permute-start.35 = (bf16[2,256,128]{2,1,0:T(8,128)(2,1)S(1)}, bf16[2,256,128]{2,1,0:T(8,128)(2,1)S(1)}, u32[]{:S(2)}, u32[]{:S(2)}) collective-permute-start(bf16[2,256,128]{2,1,0:T(8,128)(2,1)S(1)} %get-tuple-element.106), channel_id=1, source_target_pairs={{0,7},{1,6},{2,5},{3,4},{4,3},{5,2},{6,1},{7,0},{8,15},{9,14},{10,... | collective-permute-start | bytes 393224 | tf_op jit(solution)/shard_map/ppermute | solution.py:405
  162.6 9.1 %collective-permute-start.8 = (bf16[2,256,128]{2,1,0:T(8,128)(2,1)S(1)}, bf16[2,256,128]{2,1,0:T(8,128)(2,1)S(1)}, u32[]{:S(2)}, u32[]{:S(2)}) collective-permute-start(bf16[2,256,128]{2,1,0:T(8,128)(2,1)S(1)} %get-tuple-element.73), channel_id=1, source_target_pairs={{0,1},{1,0},{2,3},{3,2},{4,5},{5,4},{6,7},{7,6},{8,9},{9,8},{10,11... | collective-permute-start | bytes 393224 | tf_op jit(solution)/shard_map/ppermute | solution.py:405
  162.6 10.7 %collective-permute-start.9 = (bf16[2,256,128]{2,1,0:T(8,128)(2,1)S(1)}, bf16[2,256,128]{2,1,0:T(8,128)(2,1)S(1)}, u32[]{:S(2)}, u32[]{:S(2)}) collective-permute-start(bf16[2,256,128]{2,1,0:T(8,128)(2,1)S(1)} %get-tuple-element.74), channel_id=1, source_target_pairs={{0,2},{1,3},{2,0},{3,1},{4,6},{5,7},{6,4},{7,5},{8,10},{9,11},{10,... | collective-permute-start | bytes 393224 | tf_op jit(solution)/shard_map/ppermute | solution.py:405
  169.6 5.1 %collective-permute-start.10 = (bf16[2,256,128]{2,1,0:T(8,128)(2,1)S(1)}, bf16[2,256,128]{2,1,0:T(8,128)(2,1)S(1)}, u32[]{:S(2)}, u32[]{:S(2)}) collective-permute-start(bf16[2,256,128]{2,1,0:T(8,128)(2,1)S(1)} %get-tuple-element.75), channel_id=1, source_target_pairs={{0,3},{1,2},{2,1},{3,0},{4,7},{5,6},{6,5},{7,4},{8,11},{9,10},{10,... | collective-permute-start | bytes 393224 | tf_op jit(solution)/shard_map/ppermute | solution.py:405
  170.3 12.0 %collective-permute-start.11 = (bf16[2,256,128]{2,1,0:T(8,128)(2,1)S(1)}, bf16[2,256,128]{2,1,0:T(8,128)(2,1)S(1)}, u32[]{:S(2)}, u32[]{:S(2)}) collective-permute-start(bf16[2,256,128]{2,1,0:T(8,128)(2,1)S(1)} %get-tuple-element.76), channel_id=1, source_target_pairs={{0,4},{1,5},{2,6},{3,7},{4,0},{5,1},{6,2},{7,3},{8,12},{9,13},{10,... | collective-permute-start | bytes 393224 | tf_op jit(solution)/shard_map/ppermute | solution.py:405
  170.3 13.0 %collective-permute-start.12 = (bf16[2,256,128]{2,1,0:T(8,128)(2,1)S(1)}, bf16[2,256,128]{2,1,0:T(8,128)(2,1)S(1)}, u32[]{:S(2)}, u32[]{:S(2)}) collective-permute-start(bf16[2,256,128]{2,1,0:T(8,128)(2,1)S(1)} %get-tuple-element.77), channel_id=1, source_target_pairs={{0,5},{1,4},{2,7},{3,6},{4,1},{5,0},{6,3},{7,2},{8,13},{9,12},{10,... | collective-permute-start | bytes 393224 | tf_op jit(solution)/shard_map/ppermute | solution.py:405
  171.7 11.6 %collective-permute-start.13 = (bf16[2,256,128]{2,1,0:T(8,128)(2,1)S(1)}, bf16[2,256,128]{2,1,0:T(8,128)(2,1)S(1)}, u32[]{:S(2)}, u32[]{:S(2)}) collective-permute-start(bf16[2,256,128]{2,1,0:T(8,128)(2,1)S(1)} %get-tuple-element.78), channel_id=1, source_target_pairs={{0,6},{1,7},{2,4},{3,5},{4,2},{5,3},{6,0},{7,1},{8,14},{9,15},{10,... | collective-permute-start | bytes 393224 | tf_op jit(solution)/shard_map/ppermute | solution.py:405
  173.3 10.0 %collective-permute-start.14 = (bf16[2,256,128]{2,1,0:T(8,128)(2,1)S(1)}, bf16[2,256,128]{2,1,0:T(8,128)(2,1)S(1)}, u32[]{:S(2)}, u32[]{:S(2)}) collective-permute-start(bf16[2,256,128]{2,1,0:T(8,128)(2,1)S(1)} %get-tuple-element.79), channel_id=1, source_target_pairs={{0,7},{1,6},{2,5},{3,4},{4,3},{5,2},{6,1},{7,0},{8,15},{9,14},{10,... | collective-permute-start | bytes 393224 | tf_op jit(solution)/shard_map/ppermute | solution.py:405
where the time goes:
time: 185 us
  waiting for transfers between devices  103 us (56%)
  starting transfers between devices  49.7 us (27%)
  Pallas kernels  28.1 us (15%)
  local copies, waits for them, and re-layouts  2.98 us (2%)
    ppermute x13, waiting for transfers between devices, send(): return lax.ppermute(x, ('ri', 'orb'), flat)  52.6 us
    ppermute x21, waiting for transfers between devices, xors(): out.append(lax.ppermute(pieces[k], ('ri', 'orb'), pairs))  39.5 us
    ppermute x21, starting transfers between devices, xors(): out.append(lax.ppermute(pieces[k], ('ri', 'orb'), pairs))  18.1 us
    ppermute x13, starting transfers between devices, send(): return lax.ppermute(x, ('ri', 'orb'), flat)  17.3 us
    all_to_all x2, waiting for transfers between devices, swap(): return lax.all_to_all(x, 'orb', split_axis=0, concat_axis=0, tiled=True)  11.3 us
    pallas_call x2, Pallas kernels, prep(): pl.pallas_call(functools.partial(prep_kernel, groups, blocks, c, per), ou...  9.86 us
    all_to_all x2, starting transfers between devices, swap(): return lax.all_to_all(x, 'orb', split_axis=0, concat_axis=0, tiled=True)  9.49 us
    pallas_call x1, Pallas kernels, green(): pl.pallas_call(green_kernel, out_shape=(jax.ShapeDtypeStruct((2, rows, 30...  5.96 us
  transfers between devices with their start and end apart: 38, of which 14 were waited for; matrix products, arithmetic and copies ran while one was open for 0% of the time, Pallas kernels for 12%

commit v1 on v0

--- a/solution.py
+++ b/solution.py
@@ -36,8 +36,11 @@
     return pl.CostEstimate(flops=int(flops), bytes_accessed=int(moved), transcendentals=0)
 
 
-def prep_kernel(groups, blocks, c, per, screen_ref, x_ref, out_ref, *refs):
-    lanes_ref = refs[-1]
+def prep_kernel(groups, blocks, c, per, apart, screen_ref, x_ref, *refs):
+    if apart:
+        *outs, lanes_ref, out_ref = refs
+    else:
+        out_ref, lanes_ref = refs
     rows, first = per * groups, c * (per // RB)
     lane, row = iota((1536, 128), 1), iota((1536, 128), 0)
     base = row - (lane // 8) * 96 - lane % 8
@@ -63,22 +66,30 @@
     zeros = jnp.zeros((per, 1024), BF16)
     out_ref[0, :, :1024] = zeros
     out_ref[groups - 1, :, 2048:] = zeros
-    for odd, half_ref in enumerate(refs[:-1]):
-        for k in range(groups // 2):
-            half_ref[k] = out_ref[2 * k + odd]
-
-
-def prep(c, x, screen, groups, per, halves):
+    if apart:
+        me = lax.axis_index("orb")
+        for k in range(groups):
+            outs[k][...] = out_ref[me ^ k]
+        for odd, half_ref in enumerate(outs[groups:]):
+            for k in range(groups // 2):
+                half_ref[k] = out_ref[2 * k + odd]
+
+
+def prep(c, x, screen, groups, per, apart):
     blocks = screen.shape[0] // (groups * 3)
     rows = per * groups
     shapes = [jax.ShapeDtypeStruct((groups, per, 3072), BF16)]
-    shapes += [jax.ShapeDtypeStruct((groups // 2, per, 3072), BF16)] * (2 * halves)
-    return pl.pallas_call(
-        functools.partial(prep_kernel, groups, blocks, c, per),
+    scratch = [pltpu.VMEM((1536, 1536), BF16)]
+    if apart:
+        scratch.append(pltpu.VMEM((groups, per, 3072), BF16))
+        shapes = [jax.ShapeDtypeStruct((per, 3072), BF16)] * groups
+        shapes += [jax.ShapeDtypeStruct((groups // 2, per, 3072), BF16)] * 2
+    return pl.pallas_call(
+        functools.partial(prep_kernel, groups, blocks, c, per, apart),
         out_shape=shapes,
         in_specs=[SMEM, VMEM],
         out_specs=[VMEM] * len(shapes),
-        scratch_shapes=[pltpu.VMEM((1536, 1536), BF16)],
+        scratch_shapes=scratch,
         compiler_params=pltpu.CompilerParams(vmem_limit_bytes=24 * MIB),
         cost_estimate=cost(4 * rows * 1536 * 1536, rows * 3072 * 4),
     )(screen, x[c * rows : (c + 1) * rows])
@@ -179,19 +190,25 @@
                 out_ref[:, col : col + 128] = z[:, j * 128 : (j + 1) * 128]
 
 
-def green_kernel(m0_ref, m1_ref, w1_ref, w2_ref, out_ref, kept_ref, y_ref):
-    kept_ref[0] = m0_ref[...]
-    kept_ref[1] = m1_ref[...]
-
-    @pl.loop(0, 2)
-    def _(c):
-        apply_green(kept_ref.at[c], w1_ref, w2_ref, y_ref, out_ref.at[c])
-
-
-def green(ms, w1, w2):
+def green_kernel(far, m0_ref, m1_ref, w1_ref, w2_ref, out_ref, kept_ref, y_ref):
+    def run():
+        kept_ref[0] = m0_ref[...]
+        kept_ref[1] = m1_ref[...]
+
+        @pl.loop(0, 2)
+        def _(c):
+            apply_green(kept_ref.at[c], w1_ref, w2_ref, y_ref, out_ref.at[c])
+
+    if far:
+        pl.when(place()[0] == 2)(run)
+    else:
+        run()
+
+
+def green(ms, w1, w2, far):
     rows = ms[0].shape[0]
     return pl.pallas_call(
-        green_kernel,
+        functools.partial(green_kernel, far),
         out_shape=(jax.ShapeDtypeStruct((2, rows, 3072), BF16),) * 2,
         in_specs=[VMEM] * 4,
         out_specs=(VMEM,) * 2,
@@ -227,7 +244,7 @@
     )(b, m)
 
 
-USERS = {"f1": (1, 2), "f2": (2, 3), "g": (2, 2)}
+USERS = {"f1": (1, 3), "f2": (2, 3)}
 
 
 def place():
@@ -251,60 +268,59 @@
 
 def pair(kind, m, w1, w2, kept, b):
     rows = m.shape[0]
+    keep = kind == "f2"
     block = jax.ShapeDtypeStruct((2, 2, rows, rows // 2), BF16)
     return pl.pallas_call(
         functools.partial(pair_kernel, kind),
-        out_shape=(block, block, jax.ShapeDtypeStruct(m.shape, BF16)),
+        out_shape=(block, block) + (jax.ShapeDtypeStruct(m.shape, BF16),) * keep,
         in_specs=[VMEM] * 5,
-        out_specs=(VMEM,) * 3,
-        scratch_shapes=[pltpu.VMEM((rows, 3072), BF16)],
+        out_specs=(VMEM,) * (2 + keep),
+        scratch_shapes=[pltpu.VMEM((rows, 3072), BF16)] * (2 - keep),
         compiler_params=pltpu.CompilerParams(vmem_limit_bytes=12 * MIB),
         cost_estimate=cost(rows * 7e6 + 8 * rows * rows * 3072, 5 * rows * 3072 * 2),
     )(m, w1, w2, kept, b)
 
 
-def cross_kernel(m_ref, b_ref, m0_ref, m1_ref, b0_ref, b1_ref, held_ref, up_ref, down_ref):
+def cross_kernel(m_ref, b_ref, kept_ref, green_ref, up_ref, down_ref):
     @pl.when(place()[0] == 2)
     def _():
-        for i, (far_m_ref, far_b_ref) in enumerate(((m0_ref, b0_ref), (m1_ref, b1_ref))):
-            halves_to(dot_t(b_ref[...], far_m_ref[...]), down_ref, i)
-            halves_to(dot_t(far_b_ref[...], m_ref[...]), up_ref.at[1], i)
-        up_ref[0] = held_ref[...]
-
-
-def cross(m, b, ms, bs, held):
+        @pl.loop(0, 2)
+        def _(i):
+            halves_to(dot_t(b_ref[...], kept_ref[i]), down_ref, i)
+            halves_to(dot_t(green_ref[i], m_ref[...]), up_ref, i)
+
+
+def cross(m, b, kept, far_b):
     rows = m.shape[0]
     return pl.pallas_call(
         cross_kernel,
-        out_shape=(jax.ShapeDtypeStruct((2,) + held.shape, BF16), jax.ShapeDtypeStruct(held.shape, BF16)),
-        in_specs=[VMEM] * 7,
+        out_shape=(jax.ShapeDtypeStruct((2, 2, rows, rows // 2), BF16),) * 2,
+        in_specs=[VMEM] * 4,
         out_specs=(VMEM,) * 2,
         compiler_params=pltpu.CompilerParams(vmem_limit_bytes=12 * MIB),
         cost_estimate=cost(8 * rows * rows * 3072, 5 * rows * 3072 * 2),
         name="cross",
-    )(m, b, *ms, *bs, held)
-
-
-def select_kernel(own_ref, m1_ref, m2_ref, mg_ref, t1_ref, t2_ref, up_ref, down_ref, *refs):
+    )(m, b, kept, far_b)
+
+
+def select_kernel(own_ref, m1_ref, m2_ref, t1_ref, t2_ref, up_ref, down_ref, *refs):
     outs, all_ref = refs[:-1], refs[-1]
     p, odd = place()
     me = lax.axis_index("orb")
 
-    def put(used, at, x_ref, *index):
+    def put(used, at, x_ref):
         @pl.when(used)
         def _():
             q = jnp.where(odd == 1, 3 - at, at)
             for h in range(2):
-                all_ref[(q * 2 + h) ^ me] = x_ref[(*index, h)]
+                all_ref[(q * 2 + h) ^ me] = x_ref[h]
 
     put(p >= 0, p, own_ref)
-    put((p == 1) | (p == 2), p - 1, m1_ref)
+    put(p >= 1, p - 1, m1_ref)
     put(p >= 2, p - 2, m2_ref)
-    put(p == 2, 3, mg_ref)
-    put(p <= 1, p + 1, t1_ref)
+    put(p <= 2, p + 1, t1_ref)
     put(p <= 1, p + 2, t2_ref)
-    put(p == 3, 2, up_ref, 0)
-    put(p == 3, 0, up_ref, 1)
+    put(p == 3, 0, up_ref)
     put(p == 0, 3, down_ref)
     for k, out_ref in enumerate(outs):
         out_ref[...] = all_ref[k]
@@ -333,7 +349,7 @@
     for other in range(2):
         odd = (me + other) % 2
         p, t = jnp.where(odd == 1, 3 - r, r), jnp.where(odd == 1, 3 - q, q)
-        straight.append((p == t) | ((t < p) & (t < 2)) | ((t > p) & (p >= 2)))
+        straight.append(t <= p)
     blocks = width // per
     lane = iota((per, width), 1) // per
     for o in range(rows // per):
@@ -405,31 +421,33 @@
             out.append(lax.ppermute(pieces[k], ("ri", "orb"), pairs))
         return out
 
-    ms = []
-    for c in range(CHUNKS):
-        m, *halves = prep(c, x, screen, groups, per, c > 0)
-        ms.append(swap(m).reshape(orbs * per, 3072))
-    b, kept = green(ms, w1, w2)
-    even = lax.ppermute(halves[0], "ri", [(0, 1), (1, 2)])
-    odd = lax.ppermute(halves[1], "ri", [(3, 2), (2, 1)])
+    (m,) = prep(0, x, screen, groups, per, False)
+    ms = [swap(m).reshape(orbs * per, 3072)]
+    pieces = prep(1, x, screen, groups, per, True)
+    pieces, halves = pieces[:orbs], pieces[orbs:]
+    pieces = xors(pieces)
+    ms.append(assemble(pieces))
+    b, kept = green(ms, w1, w2, False)
+    even = lax.ppermute(halves[0], "ri", [(0, 1), (1, 2), (2, 3)])
+    odd = lax.ppermute(halves[1], "ri", [(3, 2), (2, 1), (1, 0)])
     pieces = unpack(even, odd)
     pieces = xors(pieces)
     hopped = assemble(pieces)
 
     mine, theirs, b_of, got = {}, {}, {}, {}
     for c in range(CHUNKS):
-        got["f1", c] = send(ms[c], [(0, 1), (1, 2)]) if c == 0 else hopped
+        got["f1", c] = send(ms[c], [(0, 1), (1, 2), (2, 3)]) if c == 0 else hopped
         got["f2", c] = send(got["f1", c], [(1, 2), (2, 3)])
         got["g", c] = send(ms[c], [(3, 2)])
         for kind in USERS:
-            mine[kind, c], theirs[kind, c], b_of[kind, c] = pair(kind, got[kind, c], w1, w2, kept, b)
+            mine[kind, c], theirs[kind, c], *b_of[kind, c] = pair(kind, got[kind, c], w1, w2, kept, b)
+    far_b, far_kept = green([got["g", c] for c in range(CHUNKS)], w1, w2, True)
     sums = []
     for c in range(CHUNKS):
         own_block = own(b, kept, c)
-        far = [[x["g", i] for i in range(CHUNKS)] for x in (got, b_of)]
-        up, down = cross(got["f2", c], b_of["f2", c], *far, theirs["g", c])
+        up, down = cross(got["f2", c], b_of["f2", c][0], far_kept, far_b)
         back = [
-            send(theirs["f1", c], [(1, 0), (2, 1)]),
+            send(theirs["f1", c], [(1, 0), (2, 1), (3, 2)]),
             send(theirs["f2", c], [(2, 0), (3, 1)]),
             send(up, [(2, 3)]),
             send(down, [(2, 0)]),

time: 185 us -> 192 us (1.038)
  starting transfers between devices: 49.7 us -> 63.6 us
  Pallas kernels: 28.1 us -> 20 us
  local copies, waits for them, and re-layouts: 2.98 us -> 7.1 us
  waiting for transfers between devices: 103 us -> 100 us
    ppermute x21 -> x28, starting transfers between devices: 18.1 us -> 37.6 us  [xors(): out.append(lax.ppermute(pieces[k], ('ri', 'orb'), pairs))]
    ppermute x2, waiting for transfers between devices: 0.01 us -> 10.6 us  [the longest x1 5.85 us: local(): even = lax.ppermute(halves[0], 'ri', [(0, 1), (1, 2), (2, 3)])]
    ppermute x13, waiting for transfers between devices: 52.6 us -> 42.5 us  [send(): return lax.ppermute(x, ('ri', 'orb'), flat)]
    pallas_call x6 -> x4, Pallas kernels: 5.48 us -> 0.09 us  [pair(): pl.pallas_call(functools.partial(pair_kernel, kind), out_shape=(block, bl...]
    all_to_all x2 -> x1, starting transfers between devices: 9.49 us -> 5.2 us  [swap(): return lax.all_to_all(x, 'orb', split_axis=0, concat_axis=0, tiled=True)]
    all_to_all x2 -> x1, waiting for transfers between devices: 11.3 us -> 6.99 us  [swap(): return lax.all_to_all(x, 'orb', split_axis=0, concat_axis=0, tiled=True)]
    unnamed x5 -> x29, local copies, waits for them, and re-layouts: 0.79 us -> 4.91 us
    pallas_call x5 -> x6, Pallas kernels: 15.9 us -> 14.4 us  [the longest x2 10 us: prep(): pl.pallas_call(functools.partial(prep_kernel, groups, blocks, c, per, apa...]
  transfers between devices with their start and end apart: 38 -> 44, of which waited for: 14 -> 18; matrix products, arithmetic and copies ran while one was open for 0% -> 0% of each run, Pallas kernels for 12% -> 7%
where the time goes in v1:
time: 192 us; the launch traced here: 191 us
  waiting for transfers between devices  100 us (52%)
  starting transfers between devices  63.6 us (33%)
  Pallas kernels  20 us (10%)
  local copies, waits for them, and re-layouts  7.1 us (4%)
    ppermute x13, waiting for transfers between devices, send(): return lax.ppermute(x, ('ri', 'orb'), flat)  42.5 us
    ppermute x28, waiting for transfers between devices, xors(): out.append(lax.ppermute(pieces[k], ('ri', 'orb'), pairs))  39.9 us
    ppermute x28, starting transfers between devices, xors(): out.append(lax.ppermute(pieces[k], ('ri', 'orb'), pairs))  37.6 us
    ppermute x13, starting transfers between devices, send(): return lax.ppermute(x, ('ri', 'orb'), flat)  16 us
    pallas_call x2, Pallas kernels, prep(): pl.pallas_call(functools.partial(prep_kernel, groups, blocks, c, per, apa...  10 us
    all_to_all x1, waiting for transfers between devices, swap(): return lax.all_to_all(x, 'orb', split_axis=0, concat_axis=0, tiled=True)  6.99 us
    ppermute x1, waiting for transfers between devices, local(): even = lax.ppermute(halves[0], 'ri', [(0, 1), (1, 2), (2, 3)])  5.85 us
    all_to_all x1, starting transfers between devices, swap(): return lax.all_to_all(x, 'orb', split_axis=0, concat_axis=0, tiled=True)  5.2 us
  transfers between devices with their start and end apart: 44, of which 18 were waited for; matrix products, arithmetic and copies ran while one was open for 0% of the time, Pallas kernels for 7%

profile of v1, /device:TPU:0, one launch (start us, length us, event | category | flops | bytes accessed | tf_op | source)
XLA Modules:
  0.0 191.3 jit_solution(12088790661113086935)
XLA Ops:
  0.0 0.8 copy.6
  0.9 2.1 %slice_bitcast_fusion = (bf16[256,3072]{1,0:T(8,128)(2,1)S(1)}, bf16[256,3072]{1,0:T(8,128)(2,1)S(1)}) fusion(bf16[64,8,3072]{2,1,0:T(8,128)(2,1)} %param.4), kind=kLoop, calls=%fused_computation | loop fusion | bytes 6291456 | tf_op jit(solution)/shard_map/slice | solution.py:95
  3.0 4.9 %shard_map.46 = bf16[8,32,3072]{2,1,0:T(8,128)(2,1)} custom-call(s32[96]{0:T(128)S(1)} %reshape.9.screen_ref, bf16[256,3072]{1,0:T(8,128)(2,1)S(1)} %get-tuple-element.114.x_ref), custom_call_target="tpu_custom_call" | custom-call | flops 2415919104 | bytes 3145728 | tf_op jit(solution)/shard_map/pallas_call | solution.py:87
  7.9 5.2 %all-to-all-start = ((bf16[8,32,3072]{2,1,0:T(8,128)(2,1)}), bf16[8,32,3072]{2,1,0:T(8,128)(2,1)S(1)}, u32[]{:S(2)}, u32[]{:S(2)}) async-start(bf16[8,32,3072]{2,1,0:T(8,128)(2,1)} %shard_map.46), calls=%async_computation | async-start | bytes 3145728 | tf_op jit(solution)/shard_map/all_to_all | solution.py:411
  13.1 5.1 %shard_map.47 = (bf16[32,3072]{1,0:T(8,128)(2,1)S(1)}, bf16[32,3072]{1,0:T(8,128)(2,1)S(1)}, bf16[32,3072]{1,0:T(8,128)(2,1)S(1)}, bf16[32,3072]{1,0:T(8,128)(2,...) custom-call(s32[96]{0:T(128)S(1)} %reshape.9.screen_ref, ...), custom_call_target="tpu_custom_call" | custom-call | flops 2415919104 | bytes 3145728 | tf_op jit(solution)/shard_map/pallas_call | solution.py:87
  18.2 0.7 copy-done.1
  19.5 0.7 copy-done.5
  20.2 0.7 copy-done.7
  20.9 0.7 copy-done.9
  22.3 3.5 %collective-permute-start.22 = (bf16[4,32,3072]{2,1,0:T(8,128)(2,1)}, bf16[4,32,3072]{2,1,0:T(8,128)(2,1)S(1)}, u32[]{:S(2)}, u32[]{:S(2)}) collective-permute-start(bf16[4,32,3072]{2,1,0:T(8,128)(2,1)} %get-tuple-element.88), channel_id=1, source_target_pairs={{0,8},{8,16},{16,24},{1,9},{9,17},{17,25},{2,10},{10,18},{18,26},{... | collective-permute-start | bytes 2359304 | tf_op jit(solution)/shard_map/ppermute | solution.py:431
  25.8 1.3 collective-permute-start.23
  27.1 7.0 %all-to-all-done = bf16[8,32,3072]{2,1,0:T(8,128)(2,1)S(1)} async-done(((bf16[8,32,3072]{2,1,0:T(8,128)(2,1)}), bf16[8,32,3072]{2,1,0:T(8,128)(2,1)S(1)}, u32[]{:S(2)}, u32[]{:S(2)}) %all-to-all-start) | async-done | bytes 1572896 | tf_op jit(solution)/shard_map/all_to_all | solution.py:411
  34.1 3.6 %collective-permute-start.7 = (bf16[256,3072]{1,0:T(8,128)(2,1)S(1)}, bf16[256,3072]{1,0:T(8,128)(2,1)S(1)}, u32[]{:S(2)}, u32[]{:S(2)}) collective-permute-start(bf16[256,3072]{1,0:T(8,128)(2,1)S(1)} %bitcast.5), channel_id=1, source_target_pairs={{0,8},{8,16},{16,24},{25,17},{17,9},{9,1},{2,10},{10,18},{18,26},{... | collective-permute-start | bytes 4718600 | tf_op jit(solution)/shard_map/ppermute | solution.py:408
  37.7 5.9 %collective-permute-done.22.even_ref = bf16[4,32,3072]{2,1,0:T(8,128)(2,1)S(1)} collective-permute-done((bf16[4,32,3072]{2,1,0:T(8,128)(2,1)}, bf16[4,32,3072]{2,1,0:T(8,128)(2,1)S(1)}, u32[]{:S(2)}, u32[]{:S(2)}) %collective-permute-start.22) | collective-permute-done | bytes 786464 | tf_op jit(solution)/shard_map/ppermute | solution.py:431
  43.5 4.8 %collective-permute-done.23.odd_ref = bf16[4,32,3072]{2,1,0:T(8,128)(2,1)S(1)} collective-permute-done((bf16[4,32,3072]{2,1,0:T(8,128)(2,1)}, bf16[4,32,3072]{2,1,0:T(8,128)(2,1)S(1)}, u32[]{:S(2)}, u32[]{:S(2)}) %collective-permute-start.23) | collective-permute-done | bytes 786464 | tf_op jit(solution)/shard_map/ppermute | solution.py:432
  48.6 2.1 %collective-permute-start.25 = (bf16[32,3072]{1,0:T(8,128)(2,1)S(1)}, bf16[32,3072]{1,0:T(8,128)(2,1)S(1)}, u32[]{:S(2)}, u32[]{:S(2)}) collective-permute-start(bf16[32,3072]{1,0:T(8,128)(2,1)S(1)} %get-tuple-element.92), channel_id=1, source_target_pairs={{0,2},{1,3},{2,0},{3,1},{4,6},{5,7},{6,4},{7,5},{8,10},{9,11},{10,... | collective-permute-start | bytes 589832 | tf_op jit(solution)/shard_map/ppermute | solution.py:421
  50.8 1.7 collective-permute-start.27
  52.5 4.0 %collective-permute-done.25.refs_2_ = bf16[32,3072]{1,0:T(8,128)(2,1)S(1)} collective-permute-done((bf16[32,3072]{1,0:T(8,128)(2,1)S(1)}, bf16[32,3072]{1,0:T(8,128)(2,1)S(1)}, u32[]{:S(2)}, u32[]{:S(2)}) %collective-permute-start.25) | collective-permute-done | bytes 196640 | tf_op jit(solution)/shard_map/ppermute | solution.py:421
  56.5 2.9 %collective-permute-start.29 = (bf16[32,3072]{1,0:T(8,128)(2,1)S(1)}, bf16[32,3072]{1,0:T(8,128)(2,1)S(1)}, u32[]{:S(2)}, u32[]{:S(2)}) collective-permute-start(bf16[32,3072]{1,0:T(8,128)(2,1)S(1)} %get-tuple-element.96), channel_id=1, source_target_pairs={{0,6},{1,7},{2,4},{3,5},{4,2},{5,3},{6,0},{7,1},{8,14},{9,15},{10,... | collective-permute-start | bytes 589832 | tf_op jit(solution)/shard_map/ppermute | solution.py:421
  59.4 0.8 collective-permute-done.26.refs_3_
  60.2 3.1 %collective-permute-start.30 = (bf16[32,3072]{1,0:T(8,128)(2,1)S(1)}, bf16[32,3072]{1,0:T(8,128)(2,1)S(1)}, u32[]{:S(2)}, u32[]{:S(2)}) collective-permute-start(bf16[32,3072]{1,0:T(8,128)(2,1)S(1)} %get-tuple-element.97), channel_id=1, source_target_pairs={{0,7},{1,6},{2,5},{3,4},{4,3},{5,2},{6,1},{7,0},{8,15},{9,14},{10,... | collective-permute-start | bytes 589832 | tf_op jit(solution)/shard_map/ppermute | solution.py:421
  63.3 6.5 %collective-permute-done.28.refs_5_ = bf16[32,3072]{1,0:T(8,128)(2,1)S(1)} collective-permute-done((bf16[32,3072]{1,0:T(8,128)(2,1)S(1)}, bf16[32,3072]{1,0:T(8,128)(2,1)S(1)}, u32[]{:S(2)}, u32[]{:S(2)}) %collective-permute-start.28) | collective-permute-done | bytes 196640 | tf_op jit(solution)/shard_map/ppermute | solution.py:421
  70.0 0.9 collective-permute-start.31
  70.9 1.2 collective-permute-start
  72.1 1.7 collective-permute-start.1
  73.9 1.5 collective-permute-start.3
  75.4 4.5 %collective-permute-done.1.refs_2_ = bf16[32,3072]{1,0:T(8,128)(2,1)S(1)} collective-permute-done((bf16[32,3072]{1,0:T(8,128)(2,1)S(1)}, bf16[32,3072]{1,0:T(8,128)(2,1)S(1)}, u32[]{:S(2)}, u32[]{:S(2)}) %collective-permute-start.1) | collective-permute-done | bytes 196640 | tf_op jit(solution)/shard_map/ppermute | solution.py:421
  79.9 2.6 %collective-permute-done.2.refs_3_ = bf16[32,3072]{1,0:T(8,128)(2,1)S(1)} collective-permute-done((bf16[32,3072]{1,0:T(8,128)(2,1)S(1)}, bf16[32,3072]{1,0:T(8,128)(2,1)S(1)}, u32[]{:S(2)}, u32[]{:S(2)}) %collective-permute-start.2) | collective-permute-done | bytes 196640 | tf_op jit(solution)/shard_map/ppermute | solution.py:421
  82.5 2.5 %collective-permute-start.5 = (bf16[32,3072]{1,0:T(8,128)(2,1)S(1)}, bf16[32,3072]{1,0:T(8,128)(2,1)S(1)}, u32[]{:S(2)}, u32[]{:S(2)}) collective-permute-start(bf16[32,3072]{1,0:T(8,128)(2,1)S(1)} %copy-done.2), channel_id=1, source_target_pairs={{0,6},{1,7},{2,4},{3,5},{4,2},{5,3},{6,0},{7,1},{8,14},{9,15},{10,... | collective-permute-start | bytes 589832 | tf_op jit(solution)/shard_map/ppermute | solution.py:421
  85.0 0.7 collective-permute-start.6
  85.6 1.1 collective-permute-done.4.refs_5_
  86.8 4.5 %collective-permute-done.5.refs_6_ = bf16[32,3072]{1,0:T(8,128)(2,1)S(1)} collective-permute-done((bf16[32,3072]{1,0:T(8,128)(2,1)S(1)}, bf16[32,3072]{1,0:T(8,128)(2,1)S(1)}, u32[]{:S(2)}, u32[]{:S(2)}) %collective-permute-start.5) | collective-permute-done | bytes 196640 | tf_op jit(solution)/shard_map/ppermute | solution.py:421
  91.2 4.0 %collective-permute-done.6.refs_7_ = bf16[32,3072]{1,0:T(8,128)(2,1)S(1)} collective-permute-done((bf16[32,3072]{1,0:T(8,128)(2,1)S(1)}, bf16[32,3072]{1,0:T(8,128)(2,1)S(1)}, u32[]{:S(2)}, u32[]{:S(2)}) %collective-permute-start.6) | collective-permute-done | bytes 196640 | tf_op jit(solution)/shard_map/ppermute | solution.py:421
  95.3 0.8 collective-permute-start.12
  96.1 0.8 collective-permute-start.11
  96.9 1.1 weights.1
  98.0 0.9 collective-permute-start.8
  98.9 4.1 %green.2 = (bf16[2,256,3072]{2,1,0:T(8,128)(2,1)S(1)}, bf16[2,256,3072]{2,1,0:T(8,128)(2,1)S(1)}) custom-call(bf16[256,3072]{1,0:T(8,128)(2,1)S(1)} %bitcast.7, bf16[256,3072]{1,0:T(8,128)(2,1)S(1)} %assemble.2.m1_ref, bf16[768,768]{1,0:T(8,128)(2,1)S(1)} %get-tuple-element.67.w1_ref, bf16[512,512]{1,0:T(8,128)(2,1)S(1)} %get-tuple-element.68.w2_ref), custom_call_target="tpu_custom_call" | custom-call | flops 3584000000 | bytes 9437184 | tf_op jit(solution)/shard_map/green/pallas_call | solution.py:210
  103.0 1.3 collective-permute-start.32
  104.4 1.3 collective-permute-start.33
  105.7 1.3 collective-permute-start.9
  107.3 0.7 collective-permute-start.34
  108.0 1.3 collective-permute-start.35
  109.4 13.0 %collective-permute-done.32.t1_ref = bf16[2,2,256,128]{3,2,1,0:T(8,128)(2,1)S(1)} collective-permute-done((bf16[2,2,256,128]{3,2,1,0:T(8,128)(2,1)S(1)}, bf16[2,2,256,128]{3,2,1,0:T(8,128)(2,1)S(1)}, u32[]{:S(2)}, u32[]{:S(2)}) %collective-permute-start.32) | collective-permute-done | bytes 262176 | tf_op jit(solution)/shard_map/ppermute | solution.py:408
  122.4 1.3 collective-permute-start.10
  123.6 5.5 %collective-permute-done.33.t2_ref = bf16[2,2,256,128]{3,2,1,0:T(8,128)(2,1)S(1)} collective-permute-done((bf16[2,2,256,128]{3,2,1,0:T(8,128)(2,1)S(1)}, bf16[2,2,256,128]{3,2,1,0:T(8,128)(2,1)S(1)}, u32[]{:S(2)}, u32[]{:S(2)}) %collective-permute-start.33) | collective-permute-done | bytes 262176 | tf_op jit(solution)/shard_map/ppermute | solution.py:408
  129.9 1.3 collective-permute-start.14
  131.2 1.2 own.3.own_ref
  132.4 19.0 %collective-permute-done.35.down_ref = bf16[2,2,256,128]{3,2,1,0:T(8,128)(2,1)S(1)} collective-permute-done((bf16[2,2,256,128]{3,2,1,0:T(8,128)(2,1)S(1)}, bf16[2,2,256,128]{3,2,1,0:T(8,128)(2,1)S(1)}, u32[]{:S(2)}, u32[]{:S(2)}) %collective-permute-start.35) | collective-permute-done | bytes 262176 | tf_op jit(solution)/shard_map/ppermute | solution.py:408
  151.7 2.1 %collective-permute-start.37 = (bf16[2,256,128]{2,1,0:T(8,128)(2,1)S(1)}, bf16[2,256,128]{2,1,0:T(8,128)(2,1)S(1)}, u32[]{:S(2)}, u32[]{:S(2)}) collective-permute-start(bf16[2,256,128]{2,1,0:T(8,128)(2,1)S(1)} %get-tuple-element.107), channel_id=1, source_target_pairs={{0,2},{1,3},{2,0},{3,1},{4,6},{5,7},{6,4},{7,5},{8,10},{9,11},{10,... | collective-permute-start | bytes 393224 | tf_op jit(solution)/shard_map/ppermute | solution.py:421
  153.8 4.9 %collective-permute-done.10.t2_ref = bf16[2,2,256,128]{3,2,1,0:T(8,128)(2,1)S(1)} collective-permute-done((bf16[2,2,256,128]{3,2,1,0:T(8,128)(2,1)S(1)}, bf16[2,2,256,128]{3,2,1,0:T(8,128)(2,1)S(1)}, u32[]{:S(2)}, u32[]{:S(2)}) %collective-permute-start.10) | collective-permute-done | bytes 262176 | tf_op jit(solution)/shard_map/ppermute | solution.py:408
  158.7 1.7 collective-permute-start.39
  160.4 1.2 own.2.own_ref
  161.7 5.0 %collective-permute-start.40 = (bf16[2,256,128]{2,1,0:T(8,128)(2,1)S(1)}, bf16[2,256,128]{2,1,0:T(8,128)(2,1)S(1)}, u32[]{:S(2)}, u32[]{:S(2)}) collective-permute-start(bf16[2,256,128]{2,1,0:T(8,128)(2,1)S(1)} %get-tuple-element.110), channel_id=1, source_target_pairs={{0,5},{1,4},{2,7},{3,6},{4,1},{5,0},{6,3},{7,2},{8,13},{9,12},{10,... | collective-permute-start | bytes 393224 | tf_op jit(solution)/shard_map/ppermute | solution.py:421
  166.9 2.4 %collective-permute-start.41 = (bf16[2,256,128]{2,1,0:T(8,128)(2,1)S(1)}, bf16[2,256,128]{2,1,0:T(8,128)(2,1)S(1)}, u32[]{:S(2)}, u32[]{:S(2)}) collective-permute-start(bf16[2,256,128]{2,1,0:T(8,128)(2,1)S(1)} %get-tuple-element.111), channel_id=1, source_target_pairs={{0,6},{1,7},{2,4},{3,5},{4,2},{5,3},{6,0},{7,1},{8,14},{9,15},{10,... | collective-permute-start | bytes 393224 | tf_op jit(solution)/shard_map/ppermute | solution.py:421
  170.0 1.7 collective-permute-start.16
  171.7 4.0 %collective-permute-done.40.refs_13_ = bf16[2,256,128]{2,1,0:T(8,128)(2,1)S(1)} collective-permute-done((bf16[2,256,128]{2,1,0:T(8,128)(2,1)S(1)}, bf16[2,256,128]{2,1,0:T(8,128)(2,1)S(1)}, u32[]{:S(2)}, u32[]{:S(2)}) %collective-permute-start.40) | collective-permute-done | bytes 131104 | tf_op jit(solution)/shard_map/ppermute | solution.py:421
  175.8 1.9 collective-permute-start.17
  177.6 0.9 collective-permute-start.18
  178.6 1.9 collective-permute-start.20
  180.5 1.6 collective-permute-start.21
  182.0 7.2 %collective-permute-done.18.refs_4_ = bf16[2,256,128]{2,1,0:T(8,128)(2,1)S(1)} collective-permute-done((bf16[2,256,128]{2,1,0:T(8,128)(2,1)S(1)}, bf16[2,256,128]{2,1,0:T(8,128)(2,1)S(1)}, u32[]{:S(2)}, u32[]{:S(2)}) %collective-permute-start.18) | collective-permute-done | bytes 131104 | tf_op jit(solution)/shard_map/ppermute | solution.py:421
  189.3 0.7 collective-permute-done.19.refs_5_
  190.0 1.3 total.1
  (74 shorter events, 4.3 us)
Async XLA Ops:
  7.9 26.2 %all-to-all-start = ((bf16[8,32,3072]{2,1,0:T(8,128)(2,1)}), bf16[8,32,3072]{2,1,0:T(8,128)(2,1)S(1)}, u32[]{:S(2)}, u32[]{:S(2)}) async-start(bf16[8,32,3072]{2,1,0:T(8,128)(2,1)} %shard_map.46), calls=%async_computation | async-start | bytes 3145728 | tf_op jit(solution)/shard_map/all_to_all | solution.py:411
  18.2 0.7 copy-start.1
  18.9 0.7 copy-start.3
  19.5 0.7 copy-start.5
  20.2 0.7 copy-start.7
  20.9 0.7 copy-start.9
  21.6 0.7 copy-start.11
  22.3 21.2 %collective-permute-start.22 = (bf16[4,32,3072]{2,1,0:T(8,128)(2,1)}, bf16[4,32,3072]{2,1,0:T(8,128)(2,1)S(1)}, u32[]{:S(2)}, u32[]{:S(2)}) collective-permute-start(bf16[4,32,3072]{2,1,0:T(8,128)(2,1)} %get-tuple-element.88), channel_id=1, source_target_pairs={{0,8},{8,16},{16,24},{1,9},{9,17},{17,25},{2,10},{10,18},{18,26},{... | collective-permute-start | bytes 2359304 | tf_op jit(solution)/shard_map/ppermute | solution.py:431
  25.8 22.5 %collective-permute-start.23 = (bf16[4,32,3072]{2,1,0:T(8,128)(2,1)}, bf16[4,32,3072]{2,1,0:T(8,128)(2,1)S(1)}, u32[]{:S(2)}, u32[]{:S(2)}) collective-permute-start(bf16[4,32,3072]{2,1,0:T(8,128)(2,1)} %get-tuple-element.89), channel_id=1, source_target_pairs={{24,16},{16,8},{8,0},{25,17},{17,9},{9,1},{26,18},{18,10},{10,2},{... | collective-permute-start | bytes 2359304 | tf_op jit(solution)/shard_map/ppermute | solution.py:432
  34.1 63.9 %collective-permute-start.7 = (bf16[256,3072]{1,0:T(8,128)(2,1)S(1)}, bf16[256,3072]{1,0:T(8,128)(2,1)S(1)}, u32[]{:S(2)}, u32[]{:S(2)}) collective-permute-start(bf16[256,3072]{1,0:T(8,128)(2,1)S(1)} %bitcast.5), channel_id=1, source_target_pairs={{0,8},{8,16},{16,24},{25,17},{17,9},{9,1},{2,10},{10,18},{18,26},{... | collective-permute-start | bytes 4718600 | tf_op jit(solution)/shard_map/ppermute | solution.py:408
  48.6 4.0 %collective-permute-start.24 = (bf16[32,3072]{1,0:T(8,128)(2,1)S(1)}, bf16[32,3072]{1,0:T(8,128)(2,1)S(1)}, u32[]{:S(2)}, u32[]{:S(2)}) collective-permute-start(bf16[32,3072]{1,0:T(8,128)(2,1)S(1)} %get-tuple-element.91), channel_id=1, source_target_pairs={{0,1},{1,0},{2,3},{3,2},{4,5},{5,4},{6,7},{7,6},{8,9},{9,8},{10,11... | collective-permute-start | bytes 589832 | tf_op jit(solution)/shard_map/ppermute | solution.py:421
  48.6 7.8 %collective-permute-start.25 = (bf16[32,3072]{1,0:T(8,128)(2,1)S(1)}, bf16[32,3072]{1,0:T(8,128)(2,1)S(1)}, u32[]{:S(2)}, u32[]{:S(2)}) collective-permute-start(bf16[32,3072]{1,0:T(8,128)(2,1)S(1)} %get-tuple-element.92), channel_id=1, source_target_pairs={{0,2},{1,3},{2,0},{3,1},{4,6},{5,7},{6,4},{7,5},{8,10},{9,11},{10,... | collective-permute-start | bytes 589832 | tf_op jit(solution)/shard_map/ppermute | solution.py:421
  50.7 9.5 %collective-permute-start.26 = (bf16[32,3072]{1,0:T(8,128)(2,1)S(1)}, bf16[32,3072]{1,0:T(8,128)(2,1)S(1)}, u32[]{:S(2)}, u32[]{:S(2)}) collective-permute-start(bf16[32,3072]{1,0:T(8,128)(2,1)S(1)} %get-tuple-element.93), channel_id=1, source_target_pairs={{0,3},{1,2},{2,1},{3,0},{4,7},{5,6},{6,5},{7,4},{8,11},{9,10},{10,... | collective-permute-start | bytes 589832 | tf_op jit(solution)/shard_map/ppermute | solution.py:421
  50.8 12.6 %collective-permute-start.27 = (bf16[32,3072]{1,0:T(8,128)(2,1)S(1)}, bf16[32,3072]{1,0:T(8,128)(2,1)S(1)}, u32[]{:S(2)}, u32[]{:S(2)}) collective-permute-start(bf16[32,3072]{1,0:T(8,128)(2,1)S(1)} %get-tuple-element.94), channel_id=1, source_target_pairs={{0,4},{1,5},{2,6},{3,7},{4,0},{5,1},{6,2},{7,3},{8,12},{9,13},{10,... | collective-permute-start | bytes 589832 | tf_op jit(solution)/shard_map/ppermute | solution.py:421
  52.5 17.3 %collective-permute-start.28 = (bf16[32,3072]{1,0:T(8,128)(2,1)S(1)}, bf16[32,3072]{1,0:T(8,128)(2,1)S(1)}, u32[]{:S(2)}, u32[]{:S(2)}) collective-permute-start(bf16[32,3072]{1,0:T(8,128)(2,1)S(1)} %get-tuple-element.95), channel_id=1, source_target_pairs={{0,5},{1,4},{2,7},{3,6},{4,1},{5,0},{6,3},{7,2},{8,13},{9,12},{10,... | collective-permute-start | bytes 589832 | tf_op jit(solution)/shard_map/ppermute | solution.py:421
  56.5 13.4 %collective-permute-start.29 = (bf16[32,3072]{1,0:T(8,128)(2,1)S(1)}, bf16[32,3072]{1,0:T(8,128)(2,1)S(1)}, u32[]{:S(2)}, u32[]{:S(2)}) collective-permute-start(bf16[32,3072]{1,0:T(8,128)(2,1)S(1)} %get-tuple-element.96), channel_id=1, source_target_pairs={{0,6},{1,7},{2,4},{3,5},{4,2},{5,3},{6,0},{7,1},{8,14},{9,15},{10,... | collective-permute-start | bytes 589832 | tf_op jit(solution)/shard_map/ppermute | solution.py:421
  60.2 9.6 %collective-permute-start.30 = (bf16[32,3072]{1,0:T(8,128)(2,1)S(1)}, bf16[32,3072]{1,0:T(8,128)(2,1)S(1)}, u32[]{:S(2)}, u32[]{:S(2)}) collective-permute-start(bf16[32,3072]{1,0:T(8,128)(2,1)S(1)} %get-tuple-element.97), channel_id=1, source_target_pairs={{0,7},{1,6},{2,5},{3,4},{4,3},{5,2},{6,1},{7,0},{8,15},{9,14},{10,... | collective-permute-start | bytes 589832 | tf_op jit(solution)/shard_map/ppermute | solution.py:421
  69.8 1.1 copy-start.12
  69.8 2.2 %copy-start.10 = (bf16[32,3072]{1,0:T(8,128)(2,1)S(1)}, bf16[32,3072]{1,0:T(8,128)(2,1)}, u32[]{:S(2)}) copy-start(bf16[32,3072]{1,0:T(8,128)(2,1)} %copy-done.9) | copy-start | bytes 589828
  69.9 4.0 %copy-start.8 = (bf16[32,3072]{1,0:T(8,128)(2,1)S(1)}, bf16[32,3072]{1,0:T(8,128)(2,1)}, u32[]{:S(2)}) copy-start(bf16[32,3072]{1,0:T(8,128)(2,1)} %copy-done.7) | copy-start | bytes 589828
  69.9 4.0 %copy-start.6 = (bf16[32,3072]{1,0:T(8,128)(2,1)S(1)}, bf16[32,3072]{1,0:T(8,128)(2,1)}, u32[]{:S(2)}) copy-start(bf16[32,3072]{1,0:T(8,128)(2,1)} %copy-done.5) | copy-start | bytes 589828
  69.9 10.0 %copy-start.4 = (bf16[32,3072]{1,0:T(8,128)(2,1)S(1)}, bf16[32,3072]{1,0:T(8,128)(2,1)}, u32[]{:S(2)}) copy-start(bf16[32,3072]{1,0:T(8,128)(2,1)} %copy-done.3) | copy-start | bytes 589828
  69.9 12.6 %copy-start.2 = (bf16[32,3072]{1,0:T(8,128)(2,1)S(1)}, bf16[32,3072]{1,0:T(8,128)(2,1)}, u32[]{:S(2)}) copy-start(bf16[32,3072]{1,0:T(8,128)(2,1)} %copy-done.1) | copy-start | bytes 589828
  70.0 34.3 %collective-permute-start.31 = (bf16[256,3072]{1,0:T(8,128)(2,1)S(1)}, bf16[256,3072]{1,0:T(8,128)(2,1)S(1)}, u32[]{:S(2)}, u32[]{:S(2)}) collective-permute-start(bf16[256,3072]{1,0:T(8,128)(2,1)S(1)} %assemble.3.m_ref), channel_id=1, source_target_pairs={{8,16},{16,24},{17,9},{9,1},{10,18},{18,26},{19,11},{11,3},{12,20}... | collective-permute-start | bytes 4718600 | tf_op jit(solution)/shard_map/ppermute | solution.py:408
  70.9 2.9 %collective-permute-start = (bf16[32,3072]{1,0:T(8,128)(2,1)S(1)}, bf16[32,3072]{1,0:T(8,128)(2,1)S(1)}, u32[]{:S(2)}, u32[]{:S(2)}) collective-permute-start(bf16[32,3072]{1,0:T(8,128)(2,1)S(1)} %copy-done.12), channel_id=1, source_target_pairs={{0,1},{1,0},{2,3},{3,2},{4,5},{5,4},{6,7},{7,6},{8,9},{9,8},{10,11... | collective-permute-start | bytes 589832 | tf_op jit(solution)/shard_map/ppermute | solution.py:421
  72.1 7.8 %collective-permute-start.1 = (bf16[32,3072]{1,0:T(8,128)(2,1)S(1)}, bf16[32,3072]{1,0:T(8,128)(2,1)S(1)}, u32[]{:S(2)}, u32[]{:S(2)}) collective-permute-start(bf16[32,3072]{1,0:T(8,128)(2,1)S(1)} %copy-done.10), channel_id=1, source_target_pairs={{0,2},{1,3},{2,0},{3,1},{4,6},{5,7},{6,4},{7,5},{8,10},{9,11},{10,... | collective-permute-start | bytes 589832 | tf_op jit(solution)/shard_map/ppermute | solution.py:421
  73.8 8.6 %collective-permute-start.2 = (bf16[32,3072]{1,0:T(8,128)(2,1)S(1)}, bf16[32,3072]{1,0:T(8,128)(2,1)S(1)}, u32[]{:S(2)}, u32[]{:S(2)}) collective-permute-start(bf16[32,3072]{1,0:T(8,128)(2,1)S(1)} %copy-done.8), channel_id=1, source_target_pairs={{0,3},{1,2},{2,1},{3,0},{4,7},{5,6},{6,5},{7,4},{8,11},{9,10},{10,... | collective-permute-start | bytes 589832 | tf_op jit(solution)/shard_map/ppermute | solution.py:421
  73.9 11.1 %collective-permute-start.3 = (bf16[32,3072]{1,0:T(8,128)(2,1)S(1)}, bf16[32,3072]{1,0:T(8,128)(2,1)S(1)}, u32[]{:S(2)}, u32[]{:S(2)}) collective-permute-start(bf16[32,3072]{1,0:T(8,128)(2,1)S(1)} %copy-done.6), channel_id=1, source_target_pairs={{0,4},{1,5},{2,6},{3,7},{4,0},{5,1},{6,2},{7,3},{8,12},{9,13},{10,... | collective-permute-start | bytes 589832 | tf_op jit(solution)/shard_map/ppermute | solution.py:421
  79.9 6.9 %collective-permute-start.4 = (bf16[32,3072]{1,0:T(8,128)(2,1)S(1)}, bf16[32,3072]{1,0:T(8,128)(2,1)S(1)}, u32[]{:S(2)}, u32[]{:S(2)}) collective-permute-start(bf16[32,3072]{1,0:T(8,128)(2,1)S(1)} %copy-done.4), channel_id=1, source_target_pairs={{0,5},{1,4},{2,7},{3,6},{4,1},{5,0},{6,3},{7,2},{8,13},{9,12},{10,... | collective-permute-start | bytes 589832 | tf_op jit(solution)/shard_map/ppermute | solution.py:421
  82.5 8.8 %collective-permute-start.5 = (bf16[32,3072]{1,0:T(8,128)(2,1)S(1)}, bf16[32,3072]{1,0:T(8,128)(2,1)S(1)}, u32[]{:S(2)}, u32[]{:S(2)}) collective-permute-start(bf16[32,3072]{1,0:T(8,128)(2,1)S(1)} %copy-done.2), channel_id=1, source_target_pairs={{0,6},{1,7},{2,4},{3,5},{4,2},{5,3},{6,0},{7,1},{8,14},{9,15},{10,... | collective-permute-start | bytes 589832 | tf_op jit(solution)/shard_map/ppermute | solution.py:421
  85.0 10.3 %collective-permute-start.6 = (bf16[32,3072]{1,0:T(8,128)(2,1)S(1)}, bf16[32,3072]{1,0:T(8,128)(2,1)S(1)}, u32[]{:S(2)}, u32[]{:S(2)}) collective-permute-start(bf16[32,3072]{1,0:T(8,128)(2,1)S(1)} %get-tuple-element.66), channel_id=1, source_target_pairs={{0,7},{1,6},{2,5},{3,4},{4,3},{5,2},{6,1},{7,0},{8,15},{9,14},{10,... | collective-permute-start | bytes 589832 | tf_op jit(solution)/shard_map/ppermute | solution.py:421
  95.2 1.7 copy-start
  95.2 1.7 copy-start.13
  95.3 10.4 %collective-permute-start.12 = (bf16[256,3072]{1,0:T(8,128)(2,1)S(1)}, bf16[256,3072]{1,0:T(8,128)(2,1)S(1)}, u32[]{:S(2)}, u32[]{:S(2)}) collective-permute-start(bf16[256,3072]{1,0:T(8,128)(2,1)S(1)} %assemble.2.m1_ref), channel_id=1, source_target_pairs={{24,16},{1,9},{26,18},{3,11},{28,20},{5,13},{30,22},{7,15}} | collective-permute-start | bytes 4718600 | tf_op jit(solution)/shard_map/ppermute | solution.py:408
  96.1 10.9 %collective-permute-start.11 = (bf16[256,3072]{1,0:T(8,128)(2,1)S(1)}, bf16[256,3072]{1,0:T(8,128)(2,1)S(1)}, u32[]{:S(2)}, u32[]{:S(2)}) collective-permute-start(bf16[256,3072]{1,0:T(8,128)(2,1)S(1)} %bitcast.6), channel_id=1, source_target_pairs={{24,16},{1,9},{26,18},{3,11},{28,20},{5,13},{30,22},{7,15}} | collective-permute-start | bytes 4718600 | tf_op jit(solution)/shard_map/ppermute | solution.py:408
  98.0 10.0 %collective-permute-start.8 = (bf16[256,3072]{1,0:T(8,128)(2,1)S(1)}, bf16[256,3072]{1,0:T(8,128)(2,1)S(1)}, u32[]{:S(2)}, u32[]{:S(2)}) collective-permute-start(bf16[256,3072]{1,0:T(8,128)(2,1)S(1)} %collective-permute-done.7.m_ref), channel_id=1, source_target_pairs={{8,16},{16,24},{17,9},{9,1},{10,18},{18,26},{19,11},{11,3},{12,20}... | collective-permute-start | bytes 4718600 | tf_op jit(solution)/shard_map/ppermute | solution.py:408
  103.0 19.3 %collective-permute-start.32 = (bf16[2,2,256,128]{3,2,1,0:T(8,128)(2,1)S(1)}, bf16[2,2,256,128]{3,2,1,0:T(8,128)(2,1)S(1)}, u32[]{:S(2)}, u32[]{:S(2)}) collective-permute-start(bf16[2,2,256,128]{3,2,1,0:T(8,128)(2,1)S(1)} %get-tuple-element.100), channel_id=1, source_target_pairs={{8,0},{16,8},{24,16},{17,25},{9,17},{1,9},{10,2},{18,10},{26,18},{... | collective-permute-start | bytes 786440 | tf_op jit(solution)/shard_map/ppermute | solution.py:408
  104.4 24.8 %collective-permute-start.33 = (bf16[2,2,256,128]{3,2,1,0:T(8,128)(2,1)S(1)}, bf16[2,2,256,128]{3,2,1,0:T(8,128)(2,1)S(1)}, u32[]{:S(2)}, u32[]{:S(2)}) collective-permute-start(bf16[2,2,256,128]{3,2,1,0:T(8,128)(2,1)S(1)} %get-tuple-element.101), channel_id=1, source_target_pairs={{16,0},{24,8},{9,25},{1,17},{18,2},{26,10},{11,27},{3,19},{20,4},{... | collective-permute-start | bytes 786440 | tf_op jit(solution)/shard_map/ppermute | solution.py:408
  105.7 46.0 %collective-permute-start.9 = (bf16[2,2,256,128]{3,2,1,0:T(8,128)(2,1)S(1)}, bf16[2,2,256,128]{3,2,1,0:T(8,128)(2,1)S(1)}, u32[]{:S(2)}, u32[]{:S(2)}) collective-permute-start(bf16[2,2,256,128]{3,2,1,0:T(8,128)(2,1)S(1)} %get-tuple-element.73), channel_id=1, source_target_pairs={{8,0},{16,8},{24,16},{17,25},{9,17},{1,9},{10,2},{18,10},{26,18},{... | collective-permute-start | bytes 786440 | tf_op jit(solution)/shard_map/ppermute | solution.py:408
  107.3 22.5 %collective-permute-start.34 = (bf16[2,2,256,128]{3,2,1,0:T(8,128)(2,1)S(1)}, bf16[2,2,256,128]{3,2,1,0:T(8,128)(2,1)S(1)}, u32[]{:S(2)}, u32[]{:S(2)}) collective-permute-start(bf16[2,2,256,128]{3,2,1,0:T(8,128)(2,1)S(1)} %get-tuple-element.103), channel_id=1, source_target_pairs={{16,24},{9,1},{18,26},{11,3},{20,28},{13,5},{22,30},{15,7}} | collective-permute-start | bytes 786440 | tf_op jit(solution)/shard_map/ppermute | solution.py:408
  108.0 43.4 %collective-permute-start.35 = (bf16[2,2,256,128]{3,2,1,0:T(8,128)(2,1)S(1)}, bf16[2,2,256,128]{3,2,1,0:T(8,128)(2,1)S(1)}, u32[]{:S(2)}, u32[]{:S(2)}) collective-permute-start(bf16[2,2,256,128]{3,2,1,0:T(8,128)(2,1)S(1)} %get-tuple-element.104), channel_id=1, source_target_pairs={{16,0},{9,25},{18,2},{11,27},{20,4},{13,29},{22,6},{15,31}} | collective-permute-start | bytes 786440 | tf_op jit(solution)/shard_map/ppermute | solution.py:408
  122.4 36.4 %collective-permute-start.10 = (bf16[2,2,256,128]{3,2,1,0:T(8,128)(2,1)S(1)}, bf16[2,2,256,128]{3,2,1,0:T(8,128)(2,1)S(1)}, u32[]{:S(2)}, u32[]{:S(2)}) collective-permute-start(bf16[2,2,256,128]{3,2,1,0:T(8,128)(2,1)S(1)} %get-tuple-element.74), channel_id=1, source_target_pairs={{16,0},{24,8},{9,25},{1,17},{18,2},{26,10},{11,27},{3,19},{20,4},{... | collective-permute-start | bytes 786440 | tf_op jit(solution)/shard_map/ppermute | solution.py:408
  129.2 29.5 %collective-permute-start.13 = (bf16[2,2,256,128]{3,2,1,0:T(8,128)(2,1)S(1)}, bf16[2,2,256,128]{3,2,1,0:T(8,128)(2,1)S(1)}, u32[]{:S(2)}, u32[]{:S(2)}) collective-permute-start(bf16[2,2,256,128]{3,2,1,0:T(8,128)(2,1)S(1)} %get-tuple-element.78), channel_id=1, source_target_pairs={{16,24},{9,1},{18,26},{11,3},{20,28},{13,5},{22,30},{15,7}} | collective-permute-start | bytes 786440 | tf_op jit(solution)/shard_map/ppermute | solution.py:408
  129.9 31.8 %collective-permute-start.14 = (bf16[2,2,256,128]{3,2,1,0:T(8,128)(2,1)S(1)}, bf16[2,2,256,128]{3,2,1,0:T(8,128)(2,1)S(1)}, u32[]{:S(2)}, u32[]{:S(2)}) collective-permute-start(bf16[2,2,256,128]{3,2,1,0:T(8,128)(2,1)S(1)} %get-tuple-element.79), channel_id=1, source_target_pairs={{16,0},{9,25},{18,2},{11,27},{20,4},{13,29},{22,6},{15,31}} | collective-permute-start | bytes 786440 | tf_op jit(solution)/shard_map/ppermute | solution.py:408
  151.6 15.3 %collective-permute-start.36 = (bf16[2,256,128]{2,1,0:T(8,128)(2,1)S(1)}, bf16[2,256,128]{2,1,0:T(8,128)(2,1)S(1)}, u32[]{:S(2)}, u32[]{:S(2)}) collective-permute-start(bf16[2,256,128]{2,1,0:T(8,128)(2,1)S(1)} %get-tuple-element.106), channel_id=1, source_target_pairs={{0,1},{1,0},{2,3},{3,2},{4,5},{5,4},{6,7},{7,6},{8,9},{9,8},{10,11... | collective-permute-start | bytes 393224 | tf_op jit(solution)/shard_map/ppermute | solution.py:421
  151.7 17.6 %collective-permute-start.37 = (bf16[2,256,128]{2,1,0:T(8,128)(2,1)S(1)}, bf16[2,256,128]{2,1,0:T(8,128)(2,1)S(1)}, u32[]{:S(2)}, u32[]{:S(2)}) collective-permute-start(bf16[2,256,128]{2,1,0:T(8,128)(2,1)S(1)} %get-tuple-element.107), channel_id=1, source_target_pairs={{0,2},{1,3},{2,0},{3,1},{4,6},{5,7},{6,4},{7,5},{8,10},{9,11},{10,... | collective-permute-start | bytes 393224 | tf_op jit(solution)/shard_map/ppermute | solution.py:421
  158.7 10.7 %collective-permute-start.38 = (bf16[2,256,128]{2,1,0:T(8,128)(2,1)S(1)}, bf16[2,256,128]{2,1,0:T(8,128)(2,1)S(1)}, u32[]{:S(2)}, u32[]{:S(2)}) collective-permute-start(bf16[2,256,128]{2,1,0:T(8,128)(2,1)S(1)} %get-tuple-element.108), channel_id=1, source_target_pairs={{0,3},{1,2},{2,1},{3,0},{4,7},{5,6},{6,5},{7,4},{8,11},{9,10},{10,... | collective-permute-start | bytes 393224 | tf_op jit(solution)/shard_map/ppermute | solution.py:421
  158.7 11.3 %collective-permute-start.39 = (bf16[2,256,128]{2,1,0:T(8,128)(2,1)S(1)}, bf16[2,256,128]{2,1,0:T(8,128)(2,1)S(1)}, u32[]{:S(2)}, u32[]{:S(2)}) collective-permute-start(bf16[2,256,128]{2,1,0:T(8,128)(2,1)S(1)} %get-tuple-element.109), channel_id=1, source_target_pairs={{0,4},{1,5},{2,6},{3,7},{4,0},{5,1},{6,2},{7,3},{8,12},{9,13},{10,... | collective-permute-start | bytes 393224 | tf_op jit(solution)/shard_map/ppermute | solution.py:421
  161.7 14.1 %collective-permute-start.40 = (bf16[2,256,128]{2,1,0:T(8,128)(2,1)S(1)}, bf16[2,256,128]{2,1,0:T(8,128)(2,1)S(1)}, u32[]{:S(2)}, u32[]{:S(2)}) collective-permute-start(bf16[2,256,128]{2,1,0:T(8,128)(2,1)S(1)} %get-tuple-element.110), channel_id=1, source_target_pairs={{0,5},{1,4},{2,7},{3,6},{4,1},{5,0},{6,3},{7,2},{8,13},{9,12},{10,... | collective-permute-start | bytes 393224 | tf_op jit(solution)/shard_map/ppermute | solution.py:421
  166.9 10.8 %collective-permute-start.41 = (bf16[2,256,128]{2,1,0:T(8,128)(2,1)S(1)}, bf16[2,256,128]{2,1,0:T(8,128)(2,1)S(1)}, u32[]{:S(2)}, u32[]{:S(2)}) collective-permute-start(bf16[2,256,128]{2,1,0:T(8,128)(2,1)S(1)} %get-tuple-element.111), channel_id=1, source_target_pairs={{0,6},{1,7},{2,4},{3,5},{4,2},{5,3},{6,0},{7,1},{8,14},{9,15},{10,... | collective-permute-start | bytes 393224 | tf_op jit(solution)/shard_map/ppermute | solution.py:421
  169.3 9.2 %collective-permute-start.42 = (bf16[2,256,128]{2,1,0:T(8,128)(2,1)S(1)}, bf16[2,256,128]{2,1,0:T(8,128)(2,1)S(1)}, u32[]{:S(2)}, u32[]{:S(2)}) collective-permute-start(bf16[2,256,128]{2,1,0:T(8,128)(2,1)S(1)} %get-tuple-element.112), channel_id=1, source_target_pairs={{0,7},{1,6},{2,5},{3,4},{4,3},{5,2},{6,1},{7,0},{8,15},{9,14},{10,... | collective-permute-start | bytes 393224 | tf_op jit(solution)/shard_map/ppermute | solution.py:421
  169.4 9.2 %collective-permute-start.15 = (bf16[2,256,128]{2,1,0:T(8,128)(2,1)S(1)}, bf16[2,256,128]{2,1,0:T(8,128)(2,1)S(1)}, u32[]{:S(2)}, u32[]{:S(2)}) collective-permute-start(bf16[2,256,128]{2,1,0:T(8,128)(2,1)S(1)} %get-tuple-element.81), channel_id=1, source_target_pairs={{0,1},{1,0},{2,3},{3,2},{4,5},{5,4},{6,7},{7,6},{8,9},{9,8},{10,11... | collective-permute-start | bytes 393224 | tf_op jit(solution)/shard_map/ppermute | solution.py:421
  170.0 10.5 %collective-permute-start.16 = (bf16[2,256,128]{2,1,0:T(8,128)(2,1)S(1)}, bf16[2,256,128]{2,1,0:T(8,128)(2,1)S(1)}, u32[]{:S(2)}, u32[]{:S(2)}) collective-permute-start(bf16[2,256,128]{2,1,0:T(8,128)(2,1)S(1)} %get-tuple-element.82), channel_id=1, source_target_pairs={{0,2},{1,3},{2,0},{3,1},{4,6},{5,7},{6,4},{7,5},{8,10},{9,11},{10,... | collective-permute-start | bytes 393224 | tf_op jit(solution)/shard_map/ppermute | solution.py:421
  175.8 6.3 %collective-permute-start.17 = (bf16[2,256,128]{2,1,0:T(8,128)(2,1)S(1)}, bf16[2,256,128]{2,1,0:T(8,128)(2,1)S(1)}, u32[]{:S(2)}, u32[]{:S(2)}) collective-permute-start(bf16[2,256,128]{2,1,0:T(8,128)(2,1)S(1)} %get-tuple-element.83), channel_id=1, source_target_pairs={{0,3},{1,2},{2,1},{3,0},{4,7},{5,6},{6,5},{7,4},{8,11},{9,10},{10,... | collective-permute-start | bytes 393224 | tf_op jit(solution)/shard_map/ppermute | solution.py:421
  177.6 11.6 %collective-permute-start.18 = (bf16[2,256,128]{2,1,0:T(8,128)(2,1)S(1)}, bf16[2,256,128]{2,1,0:T(8,128)(2,1)S(1)}, u32[]{:S(2)}, u32[]{:S(2)}) collective-permute-start(bf16[2,256,128]{2,1,0:T(8,128)(2,1)S(1)} %get-tuple-element.84), channel_id=1, source_target_pairs={{0,4},{1,5},{2,6},{3,7},{4,0},{5,1},{6,2},{7,3},{8,12},{9,13},{10,... | collective-permute-start | bytes 393224 | tf_op jit(solution)/shard_map/ppermute | solution.py:421
  178.6 11.4 %collective-permute-start.19 = (bf16[2,256,128]{2,1,0:T(8,128)(2,1)S(1)}, bf16[2,256,128]{2,1,0:T(8,128)(2,1)S(1)}, u32[]{:S(2)}, u32[]{:S(2)}) collective-permute-start(bf16[2,256,128]{2,1,0:T(8,128)(2,1)S(1)} %get-tuple-element.85), channel_id=1, source_target_pairs={{0,5},{1,4},{2,7},{3,6},{4,1},{5,0},{6,3},{7,2},{8,13},{9,12},{10,... | collective-permute-start | bytes 393224 | tf_op jit(solution)/shard_map/ppermute | solution.py:421
  178.6 11.4 %collective-permute-start.20 = (bf16[2,256,128]{2,1,0:T(8,128)(2,1)S(1)}, bf16[2,256,128]{2,1,0:T(8,128)(2,1)S(1)}, u32[]{:S(2)}, u32[]{:S(2)}) collective-permute-start(bf16[2,256,128]{2,1,0:T(8,128)(2,1)S(1)} %get-tuple-element.86), channel_id=1, source_target_pairs={{0,6},{1,7},{2,4},{3,5},{4,2},{5,3},{6,0},{7,1},{8,14},{9,15},{10,... | collective-permute-start | bytes 393224 | tf_op jit(solution)/shard_map/ppermute | solution.py:421
  180.5 9.5 %collective-permute-start.21 = (bf16[2,256,128]{2,1,0:T(8,128)(2,1)S(1)}, bf16[2,256,128]{2,1,0:T(8,128)(2,1)S(1)}, u32[]{:S(2)}, u32[]{:S(2)}) collective-permute-start(bf16[2,256,128]{2,1,0:T(8,128)(2,1)S(1)} %get-tuple-element.87), channel_id=1, source_target_pairs={{0,7},{1,6},{2,5},{3,4},{4,3},{5,2},{6,1},{7,0},{8,15},{9,14},{10,... | collective-permute-start | bytes 393224 | tf_op jit(solution)/shard_map/ppermute | solution.py:421

commit v2 on v1

--- a/solution.py
+++ b/solution.py
@@ -37,10 +37,11 @@
 
 
 def prep_kernel(groups, blocks, c, per, apart, screen_ref, x_ref, *refs):
-    if apart:
-        *outs, lanes_ref, out_ref = refs
-    else:
-        out_ref, lanes_ref = refs
+    *outs, lanes_ref = refs
+
+    def kept(d):
+        return outs[d % 2].at[d // 2] if apart else outs[0].at[d]
+
     rows, first = per * groups, c * (per // RB)
     lane, row = iota((1536, 128), 1), iota((1536, 128), 0)
     base = row - (lane // 8) * 96 - lane % 8
@@ -62,34 +63,24 @@
                     z = (y[at : at + RB] * keep).astype(BF16)
                     for j in range(4):
                         col = (2 - s) * 1024 + j * 256 + h * 128
-                        out_ref[d, b * RB : (b + 1) * RB, col : col + 128] = z[:, j * 128 : (j + 1) * 128]
+                        kept(d)[b * RB : (b + 1) * RB, col : col + 128] = z[:, j * 128 : (j + 1) * 128]
     zeros = jnp.zeros((per, 1024), BF16)
-    out_ref[0, :, :1024] = zeros
-    out_ref[groups - 1, :, 2048:] = zeros
-    if apart:
-        me = lax.axis_index("orb")
-        for k in range(groups):
-            outs[k][...] = out_ref[me ^ k]
-        for odd, half_ref in enumerate(outs[groups:]):
-            for k in range(groups // 2):
-                half_ref[k] = out_ref[2 * k + odd]
+    kept(0)[:, :1024] = zeros
+    kept(groups - 1)[:, 2048:] = zeros
 
 
 def prep(c, x, screen, groups, per, apart):
     blocks = screen.shape[0] // (groups * 3)
     rows = per * groups
     shapes = [jax.ShapeDtypeStruct((groups, per, 3072), BF16)]
-    scratch = [pltpu.VMEM((1536, 1536), BF16)]
     if apart:
-        scratch.append(pltpu.VMEM((groups, per, 3072), BF16))
-        shapes = [jax.ShapeDtypeStruct((per, 3072), BF16)] * groups
-        shapes += [jax.ShapeDtypeStruct((groups // 2, per, 3072), BF16)] * 2
+        shapes = [jax.ShapeDtypeStruct((groups // 2, per, 3072), BF16)] * 2
     return pl.pallas_call(
         functools.partial(prep_kernel, groups, blocks, c, per, apart),
         out_shape=shapes,
         in_specs=[SMEM, VMEM],
         out_specs=[VMEM] * len(shapes),
-        scratch_shapes=scratch,
+        scratch_shapes=[pltpu.VMEM((1536, 1536), BF16)],
         compiler_params=pltpu.CompilerParams(vmem_limit_bytes=24 * MIB),
         cost_estimate=cost(4 * rows * 1536 * 1536, rows * 3072 * 4),
     )(screen, x[c * rows : (c + 1) * rows])
@@ -422,9 +413,10 @@
         return out
 
     (m,) = prep(0, x, screen, groups, per, False)
+    x, m = lax.optimization_barrier((x, m))
     ms = [swap(m).reshape(orbs * per, 3072)]
-    pieces = prep(1, x, screen, groups, per, True)
-    pieces, halves = pieces[:orbs], pieces[orbs:]
+    halves = prep(1, x, screen, groups, per, True)
+    pieces = unpack(*halves)
     pieces = xors(pieces)
     ms.append(assemble(pieces))
     b, kept = green(ms, w1, w2, False)

time: 192 us -> 189 us (0.984)
  local copies, waits for them, and re-layouts: 7.1 us -> 3.92 us
    ppermute x1, waiting for transfers between devices: 5.85 us -> 1.62 us  [local(): even = lax.ppermute(halves[0], 'ri', [(0, 1), (1, 2), (2, 3)])]
    unnamed x29 -> x5, local copies, waits for them, and re-layouts: 4.91 us -> 0.79 us
    all_to_all x1, waiting for transfers between devices: 6.99 us -> 10.1 us  [swap(): return lax.all_to_all(x, 'orb', split_axis=0, concat_axis=0, tiled=True)]
  transfers between devices with their start and end apart: 44 -> 44, of which waited for: 18 -> 18; matrix products, arithmetic and copies ran while one was open for 0% -> 1% of each run, Pallas kernels for 7% -> 7%
where the time goes in v2:
time: 189 us; the launch traced here: 188 us
  waiting for transfers between devices  99.3 us (53%)
  starting transfers between devices  64.2 us (34%)
  Pallas kernels  20.3 us (11%)
  local copies, waits for them, and re-layouts  3.92 us (2%)
    ppermute x13, waiting for transfers between devices, send(): return lax.ppermute(x, ('ri', 'orb'), flat)  41.7 us
    ppermute x28, waiting for transfers between devices, xors(): out.append(lax.ppermute(pieces[k], ('ri', 'orb'), pairs))  40.1 us
    ppermute x28, starting transfers between devices, xors(): out.append(lax.ppermute(pieces[k], ('ri', 'orb'), pairs))  37.5 us
    ppermute x13, starting transfers between devices, send(): return lax.ppermute(x, ('ri', 'orb'), flat)  15.9 us
    all_to_all x1, waiting for transfers between devices, swap(): return lax.all_to_all(x, 'orb', split_axis=0, concat_axis=0, tiled=True)  10.1 us
    pallas_call x2, Pallas kernels, prep(): pl.pallas_call(functools.partial(prep_kernel, groups, blocks, c, per, apa...  8.64 us
    ppermute x1, waiting for transfers between devices, local(): odd = lax.ppermute(halves[1], 'ri', [(3, 2), (2, 1), (1, 0)])  5.84 us
    all_to_all x1, starting transfers between devices, swap(): return lax.all_to_all(x, 'orb', split_axis=0, concat_axis=0, tiled=True)  5.2 us
  transfers between devices with their start and end apart: 44, of which 18 were waited for; matrix products, arithmetic and copies ran while one was open for 1% of the time, Pallas kernels for 7%

profile of v2, /device:TPU:0, one launch (start us, length us, event | category | flops | bytes accessed | tf_op | source)
XLA Modules:
  0.0 188.1 jit_solution(14541819395140577660)
XLA Ops:
  0.0 0.8 copy.6
  0.9 1.5 slice_bitcast_fusion.x_ref
  2.4 4.9 %shard_map.46 = bf16[8,32,3072]{2,1,0:T(8,128)(2,1)} custom-call(s32[96]{0:T(128)S(1)} %reshape.11.screen_ref, bf16[256,3072]{1,0:T(8,128)(2,1)S(1)} %slice_bitcast_fusion.x_ref), custom_call_target="tpu_custom_call" | custom-call | flops 2415919104 | bytes 3145728 | tf_op jit(solution)/shard_map/pallas_call | solution.py:78
  7.3 5.2 %all-to-all-start = ((bf16[8,32,3072]{2,1,0:T(8,128)(2,1)}), bf16[8,32,3072]{2,1,0:T(8,128)(2,1)S(1)}, u32[]{:S(2)}, u32[]{:S(2)}) async-start(bf16[8,32,3072]{2,1,0:T(8,128)(2,1)} %shard_map.46), calls=%async_computation | async-start | bytes 3145728 | tf_op jit(solution)/shard_map/all_to_all | solution.py:402
  12.5 1.5 slice.11.x_ref
  14.0 3.7 %shard_map.47 = (bf16[4,32,3072]{2,1,0:T(8,128)(2,1)S(1)}, bf16[4,32,3072]{2,1,0:T(8,128)(2,1)S(1)}) custom-call(s32[96]{0:T(128)S(1)} %reshape.11.screen_ref, bf16[256,3072]{1,0:T(8,128)(2,1)S(1)} %slice.11.x_ref), custom_call_target="tpu_custom_call" | custom-call | flops 2415919104 | bytes 3145728 | tf_op jit(solution)/shard_map/pallas_call | solution.py:78
  17.8 4.4 %collective-permute-start.22 = (bf16[4,32,3072]{2,1,0:T(8,128)(2,1)S(1)}, bf16[4,32,3072]{2,1,0:T(8,128)(2,1)}, u32[]{:S(2)}, u32[]{:S(2)}) collective-permute-start(bf16[4,32,3072]{2,1,0:T(8,128)(2,1)S(1)} %get-tuple-element.63.even_ref), channel_id=1, source_target_pairs={{0,8},{8,16},{16,24},{1,9},{9,17},{17,25},{2,10},{10,18},{18,26},{... | collective-permute-start | bytes 2359304 | tf_op jit(solution)/shard_map/ppermute | solution.py:423
  22.1 1.3 collective-permute-start.23
  23.4 10.1 %all-to-all-done = bf16[8,32,3072]{2,1,0:T(8,128)(2,1)S(1)} async-done(((bf16[8,32,3072]{2,1,0:T(8,128)(2,1)}), bf16[8,32,3072]{2,1,0:T(8,128)(2,1)S(1)}, u32[]{:S(2)}, u32[]{:S(2)}) %all-to-all-start) | async-done | bytes 1572896 | tf_op jit(solution)/shard_map/all_to_all | solution.py:402
  33.5 3.6 %collective-permute-start.7 = (bf16[256,3072]{1,0:T(8,128)(2,1)S(1)}, bf16[256,3072]{1,0:T(8,128)(2,1)S(1)}, u32[]{:S(2)}, u32[]{:S(2)}) collective-permute-start(bf16[256,3072]{1,0:T(8,128)(2,1)S(1)} %bitcast.4), channel_id=1, source_target_pairs={{0,8},{8,16},{16,24},{25,17},{17,9},{9,1},{2,10},{10,18},{18,26},{... | collective-permute-start | bytes 4718600 | tf_op jit(solution)/shard_map/ppermute | solution.py:399
  37.1 1.6 collective-permute-done.22.even_ref
  38.7 5.8 %collective-permute-done.23.odd_ref = bf16[4,32,3072]{2,1,0:T(8,128)(2,1)} collective-permute-done((bf16[4,32,3072]{2,1,0:T(8,128)(2,1)S(1)}, bf16[4,32,3072]{2,1,0:T(8,128)(2,1)}, u32[]{:S(2)}, u32[]{:S(2)}) %collective-permute-start.23) | collective-permute-done | bytes 786464 | tf_op jit(solution)/shard_map/ppermute | solution.py:424
  44.5 1.6 unpack.3
  46.2 2.1 %collective-permute-start.25 = (bf16[32,3072]{1,0:T(8,128)(2,1)S(1)}, bf16[32,3072]{1,0:T(8,128)(2,1)S(1)}, u32[]{:S(2)}, u32[]{:S(2)}) collective-permute-start(bf16[32,3072]{1,0:T(8,128)(2,1)S(1)} %get-tuple-element.96), channel_id=1, source_target_pairs={{0,2},{1,3},{2,0},{3,1},{4,6},{5,7},{6,4},{7,5},{8,10},{9,11},{10,... | collective-permute-start | bytes 589832 | tf_op jit(solution)/shard_map/ppermute | solution.py:412
  48.4 1.7 collective-permute-start.27
  50.1 4.0 %collective-permute-done.25.refs_2_ = bf16[32,3072]{1,0:T(8,128)(2,1)S(1)} collective-permute-done((bf16[32,3072]{1,0:T(8,128)(2,1)S(1)}, bf16[32,3072]{1,0:T(8,128)(2,1)S(1)}, u32[]{:S(2)}, u32[]{:S(2)}) %collective-permute-start.25) | collective-permute-done | bytes 196640 | tf_op jit(solution)/shard_map/ppermute | solution.py:412
  54.1 2.9 %collective-permute-start.29 = (bf16[32,3072]{1,0:T(8,128)(2,1)S(1)}, bf16[32,3072]{1,0:T(8,128)(2,1)S(1)}, u32[]{:S(2)}, u32[]{:S(2)}) collective-permute-start(bf16[32,3072]{1,0:T(8,128)(2,1)S(1)} %get-tuple-element.100), channel_id=1, source_target_pairs={{0,6},{1,7},{2,4},{3,5},{4,2},{5,3},{6,0},{7,1},{8,14},{9,15},{10,... | collective-permute-start | bytes 589832 | tf_op jit(solution)/shard_map/ppermute | solution.py:412
  57.0 0.8 collective-permute-done.26.refs_3_
  57.8 3.1 %collective-permute-start.30 = (bf16[32,3072]{1,0:T(8,128)(2,1)S(1)}, bf16[32,3072]{1,0:T(8,128)(2,1)S(1)}, u32[]{:S(2)}, u32[]{:S(2)}) collective-permute-start(bf16[32,3072]{1,0:T(8,128)(2,1)S(1)} %get-tuple-element.101), channel_id=1, source_target_pairs={{0,7},{1,6},{2,5},{3,4},{4,3},{5,2},{6,1},{7,0},{8,15},{9,14},{10,... | collective-permute-start | bytes 589832 | tf_op jit(solution)/shard_map/ppermute | solution.py:412
  60.9 6.5 %collective-permute-done.28.refs_5_ = bf16[32,3072]{1,0:T(8,128)(2,1)S(1)} collective-permute-done((bf16[32,3072]{1,0:T(8,128)(2,1)S(1)}, bf16[32,3072]{1,0:T(8,128)(2,1)S(1)}, u32[]{:S(2)}, u32[]{:S(2)}) %collective-permute-start.28) | collective-permute-done | bytes 196640 | tf_op jit(solution)/shard_map/ppermute | solution.py:412
  67.6 0.8 collective-permute-start.31
  68.6 1.2 collective-permute-start
  69.8 1.7 collective-permute-start.1
  71.5 1.5 collective-permute-start.3
  73.0 4.6 %collective-permute-done.1.refs_2_ = bf16[32,3072]{1,0:T(8,128)(2,1)S(1)} collective-permute-done((bf16[32,3072]{1,0:T(8,128)(2,1)S(1)}, bf16[32,3072]{1,0:T(8,128)(2,1)S(1)}, u32[]{:S(2)}, u32[]{:S(2)}) %collective-permute-start.1) | collective-permute-done | bytes 196640 | tf_op jit(solution)/shard_map/ppermute | solution.py:412
  77.5 2.6 %collective-permute-done.2.refs_3_ = bf16[32,3072]{1,0:T(8,128)(2,1)S(1)} collective-permute-done((bf16[32,3072]{1,0:T(8,128)(2,1)S(1)}, bf16[32,3072]{1,0:T(8,128)(2,1)S(1)}, u32[]{:S(2)}, u32[]{:S(2)}) %collective-permute-start.2) | collective-permute-done | bytes 196640 | tf_op jit(solution)/shard_map/ppermute | solution.py:412
  80.1 2.5 %collective-permute-start.5 = (bf16[32,3072]{1,0:T(8,128)(2,1)S(1)}, bf16[32,3072]{1,0:T(8,128)(2,1)S(1)}, u32[]{:S(2)}, u32[]{:S(2)}) collective-permute-start(bf16[32,3072]{1,0:T(8,128)(2,1)S(1)} %get-tuple-element.71), channel_id=1, source_target_pairs={{0,6},{1,7},{2,4},{3,5},{4,2},{5,3},{6,0},{7,1},{8,14},{9,15},{10,... | collective-permute-start | bytes 589832 | tf_op jit(solution)/shard_map/ppermute | solution.py:412
  82.6 0.6 collective-permute-start.6
  83.2 1.2 collective-permute-done.4.refs_5_
  84.4 4.5 %collective-permute-done.5.refs_6_ = bf16[32,3072]{1,0:T(8,128)(2,1)S(1)} collective-permute-done((bf16[32,3072]{1,0:T(8,128)(2,1)S(1)}, bf16[32,3072]{1,0:T(8,128)(2,1)S(1)}, u32[]{:S(2)}, u32[]{:S(2)}) %collective-permute-start.5) | collective-permute-done | bytes 196640 | tf_op jit(solution)/shard_map/ppermute | solution.py:412
  88.9 4.0 %collective-permute-done.6.refs_7_ = bf16[32,3072]{1,0:T(8,128)(2,1)S(1)} collective-permute-done((bf16[32,3072]{1,0:T(8,128)(2,1)S(1)}, bf16[32,3072]{1,0:T(8,128)(2,1)S(1)}, u32[]{:S(2)}, u32[]{:S(2)}) %collective-permute-start.6) | collective-permute-done | bytes 196640 | tf_op jit(solution)/shard_map/ppermute | solution.py:412
  93.0 0.8 collective-permute-start.12
  93.8 0.8 collective-permute-start.11
  94.6 1.1 weights.1
  95.6 0.9 collective-permute-start.8
  96.6 4.1 %green.2 = (bf16[2,256,3072]{2,1,0:T(8,128)(2,1)S(1)}, bf16[2,256,3072]{2,1,0:T(8,128)(2,1)S(1)}) custom-call(bf16[256,3072]{1,0:T(8,128)(2,1)S(1)} %bitcast.6, bf16[256,3072]{1,0:T(8,128)(2,1)S(1)} %assemble.2.m1_ref, bf16[768,768]{1,0:T(8,128)(2,1)S(1)} %get-tuple-element.73.w1_ref, bf16[512,512]{1,0:T(8,128)(2,1)S(1)} %get-tuple-element.74.w2_ref), custom_call_target="tpu_custom_call" | custom-call | flops 3584000000 | bytes 9437184 | tf_op jit(solution)/shard_map/green/pallas_call | solution.py:201
  100.7 1.3 collective-permute-start.32
  102.0 1.3 collective-permute-start.33
  103.4 1.3 collective-permute-start.9
  105.0 0.7 collective-permute-start.34
  105.7 1.3 collective-permute-start.35
  107.0 12.1 %collective-permute-done.32.t1_ref = bf16[2,2,256,128]{3,2,1,0:T(8,128)(2,1)S(1)} collective-permute-done((bf16[2,2,256,128]{3,2,1,0:T(8,128)(2,1)S(1)}, bf16[2,2,256,128]{3,2,1,0:T(8,128)(2,1)S(1)}, u32[]{:S(2)}, u32[]{:S(2)}) %collective-permute-start.32) | collective-permute-done | bytes 262176 | tf_op jit(solution)/shard_map/ppermute | solution.py:399
  119.2 1.3 collective-permute-start.10
  120.5 5.5 %collective-permute-done.33.t2_ref = bf16[2,2,256,128]{3,2,1,0:T(8,128)(2,1)S(1)} collective-permute-done((bf16[2,2,256,128]{3,2,1,0:T(8,128)(2,1)S(1)}, bf16[2,2,256,128]{3,2,1,0:T(8,128)(2,1)S(1)}, u32[]{:S(2)}, u32[]{:S(2)}) %collective-permute-start.33) | collective-permute-done | bytes 262176 | tf_op jit(solution)/shard_map/ppermute | solution.py:399
  126.0 0.7 collective-permute-start.13
  126.7 1.3 collective-permute-start.14
  128.0 1.2 own.3.own_ref
  129.2 19.0 %collective-permute-done.35.down_ref = bf16[2,2,256,128]{3,2,1,0:T(8,128)(2,1)S(1)} collective-permute-done((bf16[2,2,256,128]{3,2,1,0:T(8,128)(2,1)S(1)}, bf16[2,2,256,128]{3,2,1,0:T(8,128)(2,1)S(1)}, u32[]{:S(2)}, u32[]{:S(2)}) %collective-permute-start.35) | collective-permute-done | bytes 262176 | tf_op jit(solution)/shard_map/ppermute | solution.py:399
  148.5 2.1 %collective-permute-start.37 = (bf16[2,256,128]{2,1,0:T(8,128)(2,1)S(1)}, bf16[2,256,128]{2,1,0:T(8,128)(2,1)S(1)}, u32[]{:S(2)}, u32[]{:S(2)}) collective-permute-start(bf16[2,256,128]{2,1,0:T(8,128)(2,1)S(1)} %get-tuple-element.111), channel_id=1, source_target_pairs={{0,2},{1,3},{2,0},{3,1},{4,6},{5,7},{6,4},{7,5},{8,10},{9,11},{10,... | collective-permute-start | bytes 393224 | tf_op jit(solution)/shard_map/ppermute | solution.py:412
  150.6 4.9 %collective-permute-done.10.t2_ref = bf16[2,2,256,128]{3,2,1,0:T(8,128)(2,1)S(1)} collective-permute-done((bf16[2,2,256,128]{3,2,1,0:T(8,128)(2,1)S(1)}, bf16[2,2,256,128]{3,2,1,0:T(8,128)(2,1)S(1)}, u32[]{:S(2)}, u32[]{:S(2)}) %collective-permute-start.10) | collective-permute-done | bytes 262176 | tf_op jit(solution)/shard_map/ppermute | solution.py:399
  155.5 1.7 collective-permute-start.39
  157.3 1.2 own.2.own_ref
  158.5 5.0 %collective-permute-start.40 = (bf16[2,256,128]{2,1,0:T(8,128)(2,1)S(1)}, bf16[2,256,128]{2,1,0:T(8,128)(2,1)S(1)}, u32[]{:S(2)}, u32[]{:S(2)}) collective-permute-start(bf16[2,256,128]{2,1,0:T(8,128)(2,1)S(1)} %get-tuple-element.114), channel_id=1, source_target_pairs={{0,5},{1,4},{2,7},{3,6},{4,1},{5,0},{6,3},{7,2},{8,13},{9,12},{10,... | collective-permute-start | bytes 393224 | tf_op jit(solution)/shard_map/ppermute | solution.py:412
  163.7 2.4 %collective-permute-start.41 = (bf16[2,256,128]{2,1,0:T(8,128)(2,1)S(1)}, bf16[2,256,128]{2,1,0:T(8,128)(2,1)S(1)}, u32[]{:S(2)}, u32[]{:S(2)}) collective-permute-start(bf16[2,256,128]{2,1,0:T(8,128)(2,1)S(1)} %get-tuple-element.115), channel_id=1, source_target_pairs={{0,6},{1,7},{2,4},{3,5},{4,2},{5,3},{6,0},{7,1},{8,14},{9,15},{10,... | collective-permute-start | bytes 393224 | tf_op jit(solution)/shard_map/ppermute | solution.py:412
  166.2 0.6 collective-permute-start.15
  166.8 1.7 collective-permute-start.16
  168.6 4.0 %collective-permute-done.40.refs_13_ = bf16[2,256,128]{2,1,0:T(8,128)(2,1)S(1)} collective-permute-done((bf16[2,256,128]{2,1,0:T(8,128)(2,1)S(1)}, bf16[2,256,128]{2,1,0:T(8,128)(2,1)S(1)}, u32[]{:S(2)}, u32[]{:S(2)}) %collective-permute-start.40) | collective-permute-done | bytes 131104 | tf_op jit(solution)/shard_map/ppermute | solution.py:412
  172.6 1.9 collective-permute-start.17
  174.5 0.9 collective-permute-start.18
  175.4 1.9 %collective-permute-start.20 = (bf16[2,256,128]{2,1,0:T(8,128)(2,1)S(1)}, bf16[2,256,128]{2,1,0:T(8,128)(2,1)S(1)}, u32[]{:S(2)}, u32[]{:S(2)}) collective-permute-start(bf16[2,256,128]{2,1,0:T(8,128)(2,1)S(1)} %get-tuple-element.92), channel_id=1, source_target_pairs={{0,6},{1,7},{2,4},{3,5},{4,2},{5,3},{6,0},{7,1},{8,14},{9,15},{10,... | collective-permute-start | bytes 393224 | tf_op jit(solution)/shard_map/ppermute | solution.py:412
  177.3 1.6 collective-permute-start.21
  178.9 7.2 %collective-permute-done.18.refs_4_ = bf16[2,256,128]{2,1,0:T(8,128)(2,1)S(1)} collective-permute-done((bf16[2,256,128]{2,1,0:T(8,128)(2,1)S(1)}, bf16[2,256,128]{2,1,0:T(8,128)(2,1)S(1)}, u32[]{:S(2)}, u32[]{:S(2)}) %collective-permute-start.18) | collective-permute-done | bytes 131104 | tf_op jit(solution)/shard_map/ppermute | solution.py:412
  186.1 0.7 collective-permute-done.19.refs_5_
  186.8 1.3 total.1
  (52 shorter events, 1.6 us)
Async XLA Ops:
  7.3 26.2 %all-to-all-start = ((bf16[8,32,3072]{2,1,0:T(8,128)(2,1)}), bf16[8,32,3072]{2,1,0:T(8,128)(2,1)S(1)}, u32[]{:S(2)}, u32[]{:S(2)}) async-start(bf16[8,32,3072]{2,1,0:T(8,128)(2,1)} %shard_map.46), calls=%async_computation | async-start | bytes 3145728 | tf_op jit(solution)/shard_map/all_to_all | solution.py:402
  17.8 20.9 %collective-permute-start.22 = (bf16[4,32,3072]{2,1,0:T(8,128)(2,1)S(1)}, bf16[4,32,3072]{2,1,0:T(8,128)(2,1)}, u32[]{:S(2)}, u32[]{:S(2)}) collective-permute-start(bf16[4,32,3072]{2,1,0:T(8,128)(2,1)S(1)} %get-tuple-element.63.even_ref), channel_id=1, source_target_pairs={{0,8},{8,16},{16,24},{1,9},{9,17},{17,25},{2,10},{10,18},{18,26},{... | collective-permute-start | bytes 2359304 | tf_op jit(solution)/shard_map/ppermute | solution.py:423
  22.1 22.4 %collective-permute-start.23 = (bf16[4,32,3072]{2,1,0:T(8,128)(2,1)S(1)}, bf16[4,32,3072]{2,1,0:T(8,128)(2,1)}, u32[]{:S(2)}, u32[]{:S(2)}) collective-permute-start(bf16[4,32,3072]{2,1,0:T(8,128)(2,1)S(1)} %get-tuple-element.64.odd_ref), channel_id=1, source_target_pairs={{24,16},{16,8},{8,0},{25,17},{17,9},{9,1},{26,18},{18,10},{10,2},{... | collective-permute-start | bytes 2359304 | tf_op jit(solution)/shard_map/ppermute | solution.py:424
  33.5 62.1 %collective-permute-start.7 = (bf16[256,3072]{1,0:T(8,128)(2,1)S(1)}, bf16[256,3072]{1,0:T(8,128)(2,1)S(1)}, u32[]{:S(2)}, u32[]{:S(2)}) collective-permute-start(bf16[256,3072]{1,0:T(8,128)(2,1)S(1)} %bitcast.4), channel_id=1, source_target_pairs={{0,8},{8,16},{16,24},{25,17},{17,9},{9,1},{2,10},{10,18},{18,26},{... | collective-permute-start | bytes 4718600 | tf_op jit(solution)/shard_map/ppermute | solution.py:399
  46.2 4.0 %collective-permute-start.24 = (bf16[32,3072]{1,0:T(8,128)(2,1)S(1)}, bf16[32,3072]{1,0:T(8,128)(2,1)S(1)}, u32[]{:S(2)}, u32[]{:S(2)}) collective-permute-start(bf16[32,3072]{1,0:T(8,128)(2,1)S(1)} %get-tuple-element.95), channel_id=1, source_target_pairs={{0,1},{1,0},{2,3},{3,2},{4,5},{5,4},{6,7},{7,6},{8,9},{9,8},{10,11... | collective-permute-start | bytes 589832 | tf_op jit(solution)/shard_map/ppermute | solution.py:412
  46.2 7.8 %collective-permute-start.25 = (bf16[32,3072]{1,0:T(8,128)(2,1)S(1)}, bf16[32,3072]{1,0:T(8,128)(2,1)S(1)}, u32[]{:S(2)}, u32[]{:S(2)}) collective-permute-start(bf16[32,3072]{1,0:T(8,128)(2,1)S(1)} %get-tuple-element.96), channel_id=1, source_target_pairs={{0,2},{1,3},{2,0},{3,1},{4,6},{5,7},{6,4},{7,5},{8,10},{9,11},{10,... | collective-permute-start | bytes 589832 | tf_op jit(solution)/shard_map/ppermute | solution.py:412
  48.3 9.5 %collective-permute-start.26 = (bf16[32,3072]{1,0:T(8,128)(2,1)S(1)}, bf16[32,3072]{1,0:T(8,128)(2,1)S(1)}, u32[]{:S(2)}, u32[]{:S(2)}) collective-permute-start(bf16[32,3072]{1,0:T(8,128)(2,1)S(1)} %get-tuple-element.97), channel_id=1, source_target_pairs={{0,3},{1,2},{2,1},{3,0},{4,7},{5,6},{6,5},{7,4},{8,11},{9,10},{10,... | collective-permute-start | bytes 589832 | tf_op jit(solution)/shard_map/ppermute | solution.py:412
  48.4 12.6 %collective-permute-start.27 = (bf16[32,3072]{1,0:T(8,128)(2,1)S(1)}, bf16[32,3072]{1,0:T(8,128)(2,1)S(1)}, u32[]{:S(2)}, u32[]{:S(2)}) collective-permute-start(bf16[32,3072]{1,0:T(8,128)(2,1)S(1)} %get-tuple-element.98), channel_id=1, source_target_pairs={{0,4},{1,5},{2,6},{3,7},{4,0},{5,1},{6,2},{7,3},{8,12},{9,13},{10,... | collective-permute-start | bytes 589832 | tf_op jit(solution)/shard_map/ppermute | solution.py:412
  50.1 17.3 %collective-permute-start.28 = (bf16[32,3072]{1,0:T(8,128)(2,1)S(1)}, bf16[32,3072]{1,0:T(8,128)(2,1)S(1)}, u32[]{:S(2)}, u32[]{:S(2)}) collective-permute-start(bf16[32,3072]{1,0:T(8,128)(2,1)S(1)} %get-tuple-element.99), channel_id=1, source_target_pairs={{0,5},{1,4},{2,7},{3,6},{4,1},{5,0},{6,3},{7,2},{8,13},{9,12},{10,... | collective-permute-start | bytes 589832 | tf_op jit(solution)/shard_map/ppermute | solution.py:412
  54.1 13.4 %collective-permute-start.29 = (bf16[32,3072]{1,0:T(8,128)(2,1)S(1)}, bf16[32,3072]{1,0:T(8,128)(2,1)S(1)}, u32[]{:S(2)}, u32[]{:S(2)}) collective-permute-start(bf16[32,3072]{1,0:T(8,128)(2,1)S(1)} %get-tuple-element.100), channel_id=1, source_target_pairs={{0,6},{1,7},{2,4},{3,5},{4,2},{5,3},{6,0},{7,1},{8,14},{9,15},{10,... | collective-permute-start | bytes 589832 | tf_op jit(solution)/shard_map/ppermute | solution.py:412
  57.8 9.6 %collective-permute-start.30 = (bf16[32,3072]{1,0:T(8,128)(2,1)S(1)}, bf16[32,3072]{1,0:T(8,128)(2,1)S(1)}, u32[]{:S(2)}, u32[]{:S(2)}) collective-permute-start(bf16[32,3072]{1,0:T(8,128)(2,1)S(1)} %get-tuple-element.101), channel_id=1, source_target_pairs={{0,7},{1,6},{2,5},{3,4},{4,3},{5,2},{6,1},{7,0},{8,15},{9,14},{10,... | collective-permute-start | bytes 589832 | tf_op jit(solution)/shard_map/ppermute | solution.py:412
  67.6 34.4 %collective-permute-start.31 = (bf16[256,3072]{1,0:T(8,128)(2,1)S(1)}, bf16[256,3072]{1,0:T(8,128)(2,1)S(1)}, u32[]{:S(2)}, u32[]{:S(2)}) collective-permute-start(bf16[256,3072]{1,0:T(8,128)(2,1)S(1)} %assemble.3.m_ref), channel_id=1, source_target_pairs={{8,16},{16,24},{17,9},{9,1},{10,18},{18,26},{19,11},{11,3},{12,20}... | collective-permute-start | bytes 4718600 | tf_op jit(solution)/shard_map/ppermute | solution.py:399
  68.6 2.9 %collective-permute-start = (bf16[32,3072]{1,0:T(8,128)(2,1)S(1)}, bf16[32,3072]{1,0:T(8,128)(2,1)S(1)}, u32[]{:S(2)}, u32[]{:S(2)}) collective-permute-start(bf16[32,3072]{1,0:T(8,128)(2,1)S(1)} %get-tuple-element.66), channel_id=1, source_target_pairs={{0,1},{1,0},{2,3},{3,2},{4,5},{5,4},{6,7},{7,6},{8,9},{9,8},{10,11... | collective-permute-start | bytes 589832 | tf_op jit(solution)/shard_map/ppermute | solution.py:412
  69.8 7.8 %collective-permute-start.1 = (bf16[32,3072]{1,0:T(8,128)(2,1)S(1)}, bf16[32,3072]{1,0:T(8,128)(2,1)S(1)}, u32[]{:S(2)}, u32[]{:S(2)}) collective-permute-start(bf16[32,3072]{1,0:T(8,128)(2,1)S(1)} %get-tuple-element.67), channel_id=1, source_target_pairs={{0,2},{1,3},{2,0},{3,1},{4,6},{5,7},{6,4},{7,5},{8,10},{9,11},{10,... | collective-permute-start | bytes 589832 | tf_op jit(solution)/shard_map/ppermute | solution.py:412
  71.5 8.6 %collective-permute-start.2 = (bf16[32,3072]{1,0:T(8,128)(2,1)S(1)}, bf16[32,3072]{1,0:T(8,128)(2,1)S(1)}, u32[]{:S(2)}, u32[]{:S(2)}) collective-permute-start(bf16[32,3072]{1,0:T(8,128)(2,1)S(1)} %get-tuple-element.68), channel_id=1, source_target_pairs={{0,3},{1,2},{2,1},{3,0},{4,7},{5,6},{6,5},{7,4},{8,11},{9,10},{10,... | collective-permute-start | bytes 589832 | tf_op jit(solution)/shard_map/ppermute | solution.py:412
  71.5 11.1 %collective-permute-start.3 = (bf16[32,3072]{1,0:T(8,128)(2,1)S(1)}, bf16[32,3072]{1,0:T(8,128)(2,1)S(1)}, u32[]{:S(2)}, u32[]{:S(2)}) collective-permute-start(bf16[32,3072]{1,0:T(8,128)(2,1)S(1)} %get-tuple-element.69), channel_id=1, source_target_pairs={{0,4},{1,5},{2,6},{3,7},{4,0},{5,1},{6,2},{7,3},{8,12},{9,13},{10,... | collective-permute-start | bytes 589832 | tf_op jit(solution)/shard_map/ppermute | solution.py:412
  77.5 6.9 %collective-permute-start.4 = (bf16[32,3072]{1,0:T(8,128)(2,1)S(1)}, bf16[32,3072]{1,0:T(8,128)(2,1)S(1)}, u32[]{:S(2)}, u32[]{:S(2)}) collective-permute-start(bf16[32,3072]{1,0:T(8,128)(2,1)S(1)} %get-tuple-element.70), channel_id=1, source_target_pairs={{0,5},{1,4},{2,7},{3,6},{4,1},{5,0},{6,3},{7,2},{8,13},{9,12},{10,... | collective-permute-start | bytes 589832 | tf_op jit(solution)/shard_map/ppermute | solution.py:412
  80.1 8.8 %collective-permute-start.5 = (bf16[32,3072]{1,0:T(8,128)(2,1)S(1)}, bf16[32,3072]{1,0:T(8,128)(2,1)S(1)}, u32[]{:S(2)}, u32[]{:S(2)}) collective-permute-start(bf16[32,3072]{1,0:T(8,128)(2,1)S(1)} %get-tuple-element.71), channel_id=1, source_target_pairs={{0,6},{1,7},{2,4},{3,5},{4,2},{5,3},{6,0},{7,1},{8,14},{9,15},{10,... | collective-permute-start | bytes 589832 | tf_op jit(solution)/shard_map/ppermute | solution.py:412
  82.6 10.3 %collective-permute-start.6 = (bf16[32,3072]{1,0:T(8,128)(2,1)S(1)}, bf16[32,3072]{1,0:T(8,128)(2,1)S(1)}, u32[]{:S(2)}, u32[]{:S(2)}) collective-permute-start(bf16[32,3072]{1,0:T(8,128)(2,1)S(1)} %get-tuple-element.72), channel_id=1, source_target_pairs={{0,7},{1,6},{2,5},{3,4},{4,3},{5,2},{6,1},{7,0},{8,15},{9,14},{10,... | collective-permute-start | bytes 589832 | tf_op jit(solution)/shard_map/ppermute | solution.py:412
  92.9 1.7 copy-start
  92.9 1.7 copy-start.1
  93.0 10.4 %collective-permute-start.12 = (bf16[256,3072]{1,0:T(8,128)(2,1)S(1)}, bf16[256,3072]{1,0:T(8,128)(2,1)S(1)}, u32[]{:S(2)}, u32[]{:S(2)}) collective-permute-start(bf16[256,3072]{1,0:T(8,128)(2,1)S(1)} %assemble.2.m1_ref), channel_id=1, source_target_pairs={{24,16},{1,9},{26,18},{3,11},{28,20},{5,13},{30,22},{7,15}} | collective-permute-start | bytes 4718600 | tf_op jit(solution)/shard_map/ppermute | solution.py:399
  93.8 10.9 %collective-permute-start.11 = (bf16[256,3072]{1,0:T(8,128)(2,1)S(1)}, bf16[256,3072]{1,0:T(8,128)(2,1)S(1)}, u32[]{:S(2)}, u32[]{:S(2)}) collective-permute-start(bf16[256,3072]{1,0:T(8,128)(2,1)S(1)} %bitcast.5), channel_id=1, source_target_pairs={{24,16},{1,9},{26,18},{3,11},{28,20},{5,13},{30,22},{7,15}} | collective-permute-start | bytes 4718600 | tf_op jit(solution)/shard_map/ppermute | solution.py:399
  95.6 10.0 %collective-permute-start.8 = (bf16[256,3072]{1,0:T(8,128)(2,1)S(1)}, bf16[256,3072]{1,0:T(8,128)(2,1)S(1)}, u32[]{:S(2)}, u32[]{:S(2)}) collective-permute-start(bf16[256,3072]{1,0:T(8,128)(2,1)S(1)} %collective-permute-done.7.m_ref), channel_id=1, source_target_pairs={{8,16},{16,24},{17,9},{9,1},{10,18},{18,26},{19,11},{11,3},{12,20}... | collective-permute-start | bytes 4718600 | tf_op jit(solution)/shard_map/ppermute | solution.py:399
  100.7 18.5 %collective-permute-start.32 = (bf16[2,2,256,128]{3,2,1,0:T(8,128)(2,1)S(1)}, bf16[2,2,256,128]{3,2,1,0:T(8,128)(2,1)S(1)}, u32[]{:S(2)}, u32[]{:S(2)}) collective-permute-start(bf16[2,2,256,128]{3,2,1,0:T(8,128)(2,1)S(1)} %get-tuple-element.104), channel_id=1, source_target_pairs={{8,0},{16,8},{24,16},{17,25},{9,17},{1,9},{10,2},{18,10},{26,18},{... | collective-permute-start | bytes 786440 | tf_op jit(solution)/shard_map/ppermute | solution.py:399
  102.0 24.0 %collective-permute-start.33 = (bf16[2,2,256,128]{3,2,1,0:T(8,128)(2,1)S(1)}, bf16[2,2,256,128]{3,2,1,0:T(8,128)(2,1)S(1)}, u32[]{:S(2)}, u32[]{:S(2)}) collective-permute-start(bf16[2,2,256,128]{3,2,1,0:T(8,128)(2,1)S(1)} %get-tuple-element.105), channel_id=1, source_target_pairs={{16,0},{24,8},{9,25},{1,17},{18,2},{26,10},{11,27},{3,19},{20,4},{... | collective-permute-start | bytes 786440 | tf_op jit(solution)/shard_map/ppermute | solution.py:399
  103.4 45.1 %collective-permute-start.9 = (bf16[2,2,256,128]{3,2,1,0:T(8,128)(2,1)S(1)}, bf16[2,2,256,128]{3,2,1,0:T(8,128)(2,1)S(1)}, u32[]{:S(2)}, u32[]{:S(2)}) collective-permute-start(bf16[2,2,256,128]{3,2,1,0:T(8,128)(2,1)S(1)} %get-tuple-element.79), channel_id=1, source_target_pairs={{8,0},{16,8},{24,16},{17,25},{9,17},{1,9},{10,2},{18,10},{26,18},{... | collective-permute-start | bytes 786440 | tf_op jit(solution)/shard_map/ppermute | solution.py:399
  105.0 21.7 %collective-permute-start.34 = (bf16[2,2,256,128]{3,2,1,0:T(8,128)(2,1)S(1)}, bf16[2,2,256,128]{3,2,1,0:T(8,128)(2,1)S(1)}, u32[]{:S(2)}, u32[]{:S(2)}) collective-permute-start(bf16[2,2,256,128]{3,2,1,0:T(8,128)(2,1)S(1)} %get-tuple-element.107), channel_id=1, source_target_pairs={{16,24},{9,1},{18,26},{11,3},{20,28},{13,5},{22,30},{15,7}} | collective-permute-start | bytes 786440 | tf_op jit(solution)/shard_map/ppermute | solution.py:399
  105.7 42.6 %collective-permute-start.35 = (bf16[2,2,256,128]{3,2,1,0:T(8,128)(2,1)S(1)}, bf16[2,2,256,128]{3,2,1,0:T(8,128)(2,1)S(1)}, u32[]{:S(2)}, u32[]{:S(2)}) collective-permute-start(bf16[2,2,256,128]{3,2,1,0:T(8,128)(2,1)S(1)} %get-tuple-element.108), channel_id=1, source_target_pairs={{16,0},{9,25},{18,2},{11,27},{20,4},{13,29},{22,6},{15,31}} | collective-permute-start | bytes 786440 | tf_op jit(solution)/shard_map/ppermute | solution.py:399
  119.2 36.4 %collective-permute-start.10 = (bf16[2,2,256,128]{3,2,1,0:T(8,128)(2,1)S(1)}, bf16[2,2,256,128]{3,2,1,0:T(8,128)(2,1)S(1)}, u32[]{:S(2)}, u32[]{:S(2)}) collective-permute-start(bf16[2,2,256,128]{3,2,1,0:T(8,128)(2,1)S(1)} %get-tuple-element.80), channel_id=1, source_target_pairs={{16,0},{24,8},{9,25},{1,17},{18,2},{26,10},{11,27},{3,19},{20,4},{... | collective-permute-start | bytes 786440 | tf_op jit(solution)/shard_map/ppermute | solution.py:399
  126.0 29.5 %collective-permute-start.13 = (bf16[2,2,256,128]{3,2,1,0:T(8,128)(2,1)S(1)}, bf16[2,2,256,128]{3,2,1,0:T(8,128)(2,1)S(1)}, u32[]{:S(2)}, u32[]{:S(2)}) collective-permute-start(bf16[2,2,256,128]{3,2,1,0:T(8,128)(2,1)S(1)} %get-tuple-element.84), channel_id=1, source_target_pairs={{16,24},{9,1},{18,26},{11,3},{20,28},{13,5},{22,30},{15,7}} | collective-permute-start | bytes 786440 | tf_op jit(solution)/shard_map/ppermute | solution.py:399
  126.7 31.8 %collective-permute-start.14 = (bf16[2,2,256,128]{3,2,1,0:T(8,128)(2,1)S(1)}, bf16[2,2,256,128]{3,2,1,0:T(8,128)(2,1)S(1)}, u32[]{:S(2)}, u32[]{:S(2)}) collective-permute-start(bf16[2,2,256,128]{3,2,1,0:T(8,128)(2,1)S(1)} %get-tuple-element.85), channel_id=1, source_target_pairs={{16,0},{9,25},{18,2},{11,27},{20,4},{13,29},{22,6},{15,31}} | collective-permute-start | bytes 786440 | tf_op jit(solution)/shard_map/ppermute | solution.py:399
  148.4 15.3 %collective-permute-start.36 = (bf16[2,256,128]{2,1,0:T(8,128)(2,1)S(1)}, bf16[2,256,128]{2,1,0:T(8,128)(2,1)S(1)}, u32[]{:S(2)}, u32[]{:S(2)}) collective-permute-start(bf16[2,256,128]{2,1,0:T(8,128)(2,1)S(1)} %get-tuple-element.110), channel_id=1, source_target_pairs={{0,1},{1,0},{2,3},{3,2},{4,5},{5,4},{6,7},{7,6},{8,9},{9,8},{10,11... | collective-permute-start | bytes 393224 | tf_op jit(solution)/shard_map/ppermute | solution.py:412
  148.5 17.6 %collective-permute-start.37 = (bf16[2,256,128]{2,1,0:T(8,128)(2,1)S(1)}, bf16[2,256,128]{2,1,0:T(8,128)(2,1)S(1)}, u32[]{:S(2)}, u32[]{:S(2)}) collective-permute-start(bf16[2,256,128]{2,1,0:T(8,128)(2,1)S(1)} %get-tuple-element.111), channel_id=1, source_target_pairs={{0,2},{1,3},{2,0},{3,1},{4,6},{5,7},{6,4},{7,5},{8,10},{9,11},{10,... | collective-permute-start | bytes 393224 | tf_op jit(solution)/shard_map/ppermute | solution.py:412
  155.5 10.7 %collective-permute-start.38 = (bf16[2,256,128]{2,1,0:T(8,128)(2,1)S(1)}, bf16[2,256,128]{2,1,0:T(8,128)(2,1)S(1)}, u32[]{:S(2)}, u32[]{:S(2)}) collective-permute-start(bf16[2,256,128]{2,1,0:T(8,128)(2,1)S(1)} %get-tuple-element.112), channel_id=1, source_target_pairs={{0,3},{1,2},{2,1},{3,0},{4,7},{5,6},{6,5},{7,4},{8,11},{9,10},{10,... | collective-permute-start | bytes 393224 | tf_op jit(solution)/shard_map/ppermute | solution.py:412
  155.5 11.3 %collective-permute-start.39 = (bf16[2,256,128]{2,1,0:T(8,128)(2,1)S(1)}, bf16[2,256,128]{2,1,0:T(8,128)(2,1)S(1)}, u32[]{:S(2)}, u32[]{:S(2)}) collective-permute-start(bf16[2,256,128]{2,1,0:T(8,128)(2,1)S(1)} %get-tuple-element.113), channel_id=1, source_target_pairs={{0,4},{1,5},{2,6},{3,7},{4,0},{5,1},{6,2},{7,3},{8,12},{9,13},{10,... | collective-permute-start | bytes 393224 | tf_op jit(solution)/shard_map/ppermute | solution.py:412
  158.5 14.1 %collective-permute-start.40 = (bf16[2,256,128]{2,1,0:T(8,128)(2,1)S(1)}, bf16[2,256,128]{2,1,0:T(8,128)(2,1)S(1)}, u32[]{:S(2)}, u32[]{:S(2)}) collective-permute-start(bf16[2,256,128]{2,1,0:T(8,128)(2,1)S(1)} %get-tuple-element.114), channel_id=1, source_target_pairs={{0,5},{1,4},{2,7},{3,6},{4,1},{5,0},{6,3},{7,2},{8,13},{9,12},{10,... | collective-permute-start | bytes 393224 | tf_op jit(solution)/shard_map/ppermute | solution.py:412
  163.7 10.8 %collective-permute-start.41 = (bf16[2,256,128]{2,1,0:T(8,128)(2,1)S(1)}, bf16[2,256,128]{2,1,0:T(8,128)(2,1)S(1)}, u32[]{:S(2)}, u32[]{:S(2)}) collective-permute-start(bf16[2,256,128]{2,1,0:T(8,128)(2,1)S(1)} %get-tuple-element.115), channel_id=1, source_target_pairs={{0,6},{1,7},{2,4},{3,5},{4,2},{5,3},{6,0},{7,1},{8,14},{9,15},{10,... | collective-permute-start | bytes 393224 | tf_op jit(solution)/shard_map/ppermute | solution.py:412
  166.1 9.2 %collective-permute-start.42 = (bf16[2,256,128]{2,1,0:T(8,128)(2,1)S(1)}, bf16[2,256,128]{2,1,0:T(8,128)(2,1)S(1)}, u32[]{:S(2)}, u32[]{:S(2)}) collective-permute-start(bf16[2,256,128]{2,1,0:T(8,128)(2,1)S(1)} %get-tuple-element.116), channel_id=1, source_target_pairs={{0,7},{1,6},{2,5},{3,4},{4,3},{5,2},{6,1},{7,0},{8,15},{9,14},{10,... | collective-permute-start | bytes 393224 | tf_op jit(solution)/shard_map/ppermute | solution.py:412
  166.2 9.2 %collective-permute-start.15 = (bf16[2,256,128]{2,1,0:T(8,128)(2,1)S(1)}, bf16[2,256,128]{2,1,0:T(8,128)(2,1)S(1)}, u32[]{:S(2)}, u32[]{:S(2)}) collective-permute-start(bf16[2,256,128]{2,1,0:T(8,128)(2,1)S(1)} %get-tuple-element.87), channel_id=1, source_target_pairs={{0,1},{1,0},{2,3},{3,2},{4,5},{5,4},{6,7},{7,6},{8,9},{9,8},{10,11... | collective-permute-start | bytes 393224 | tf_op jit(solution)/shard_map/ppermute | solution.py:412
  166.8 10.5 %collective-permute-start.16 = (bf16[2,256,128]{2,1,0:T(8,128)(2,1)S(1)}, bf16[2,256,128]{2,1,0:T(8,128)(2,1)S(1)}, u32[]{:S(2)}, u32[]{:S(2)}) collective-permute-start(bf16[2,256,128]{2,1,0:T(8,128)(2,1)S(1)} %get-tuple-element.88), channel_id=1, source_target_pairs={{0,2},{1,3},{2,0},{3,1},{4,6},{5,7},{6,4},{7,5},{8,10},{9,11},{10,... | collective-permute-start | bytes 393224 | tf_op jit(solution)/shard_map/ppermute | solution.py:412
  172.6 6.3 %collective-permute-start.17 = (bf16[2,256,128]{2,1,0:T(8,128)(2,1)S(1)}, bf16[2,256,128]{2,1,0:T(8,128)(2,1)S(1)}, u32[]{:S(2)}, u32[]{:S(2)}) collective-permute-start(bf16[2,256,128]{2,1,0:T(8,128)(2,1)S(1)} %get-tuple-element.89), channel_id=1, source_target_pairs={{0,3},{1,2},{2,1},{3,0},{4,7},{5,6},{6,5},{7,4},{8,11},{9,10},{10,... | collective-permute-start | bytes 393224 | tf_op jit(solution)/shard_map/ppermute | solution.py:412
  174.5 11.6 %collective-permute-start.18 = (bf16[2,256,128]{2,1,0:T(8,128)(2,1)S(1)}, bf16[2,256,128]{2,1,0:T(8,128)(2,1)S(1)}, u32[]{:S(2)}, u32[]{:S(2)}) collective-permute-start(bf16[2,256,128]{2,1,0:T(8,128)(2,1)S(1)} %get-tuple-element.90), channel_id=1, source_target_pairs={{0,4},{1,5},{2,6},{3,7},{4,0},{5,1},{6,2},{7,3},{8,12},{9,13},{10,... | collective-permute-start | bytes 393224 | tf_op jit(solution)/shard_map/ppermute | solution.py:412
  175.4 11.4 %collective-permute-start.19 = (bf16[2,256,128]{2,1,0:T(8,128)(2,1)S(1)}, bf16[2,256,128]{2,1,0:T(8,128)(2,1)S(1)}, u32[]{:S(2)}, u32[]{:S(2)}) collective-permute-start(bf16[2,256,128]{2,1,0:T(8,128)(2,1)S(1)} %get-tuple-element.91), channel_id=1, source_target_pairs={{0,5},{1,4},{2,7},{3,6},{4,1},{5,0},{6,3},{7,2},{8,13},{9,12},{10,... | collective-permute-start | bytes 393224 | tf_op jit(solution)/shard_map/ppermute | solution.py:412
  175.4 11.4 %collective-permute-start.20 = (bf16[2,256,128]{2,1,0:T(8,128)(2,1)S(1)}, bf16[2,256,128]{2,1,0:T(8,128)(2,1)S(1)}, u32[]{:S(2)}, u32[]{:S(2)}) collective-permute-start(bf16[2,256,128]{2,1,0:T(8,128)(2,1)S(1)} %get-tuple-element.92), channel_id=1, source_target_pairs={{0,6},{1,7},{2,4},{3,5},{4,2},{5,3},{6,0},{7,1},{8,14},{9,15},{10,... | collective-permute-start | bytes 393224 | tf_op jit(solution)/shard_map/ppermute | solution.py:412
  177.3 9.5 %collective-permute-start.21 = (bf16[2,256,128]{2,1,0:T(8,128)(2,1)S(1)}, bf16[2,256,128]{2,1,0:T(8,128)(2,1)S(1)}, u32[]{:S(2)}, u32[]{:S(2)}) collective-permute-start(bf16[2,256,128]{2,1,0:T(8,128)(2,1)S(1)} %get-tuple-element.93), channel_id=1, source_target_pairs={{0,7},{1,6},{2,5},{3,4},{4,3},{5,2},{6,1},{7,0},{8,15},{9,14},{10,... | collective-permute-start | bytes 393224 | tf_op jit(solution)/shard_map/ppermute | solution.py:412

commit v3 on v2

--- a/solution.py
+++ b/solution.py
@@ -181,25 +181,38 @@
                 out_ref[:, col : col + 128] = z[:, j * 128 : (j + 1) * 128]
 
 
-def green_kernel(far, m0_ref, m1_ref, w1_ref, w2_ref, out_ref, kept_ref, y_ref):
-    def run():
-        kept_ref[0] = m0_ref[...]
-        kept_ref[1] = m1_ref[...]
-
-        @pl.loop(0, 2)
-        def _(c):
-            apply_green(kept_ref.at[c], w1_ref, w2_ref, y_ref, out_ref.at[c])
-
-    if far:
-        pl.when(place()[0] == 2)(run)
-    else:
-        run()
-
-
-def green(ms, w1, w2, far):
+def green_kernel(m0_ref, m1_ref, w1_ref, w2_ref, out_ref, kept_ref, y_ref):
+    kept_ref[0] = m0_ref[...]
+    kept_ref[1] = m1_ref[...]
+
+    @pl.loop(0, 2)
+    def _(c):
+        apply_green(kept_ref.at[c], w1_ref, w2_ref, y_ref, out_ref.at[c])
+
+
+def far_kernel(m_ref, w1_ref, w2_ref, out_ref, y_ref):
+    @pl.when(place()[0] == 2)
+    def _():
+        apply_green(m_ref, w1_ref, w2_ref, y_ref, out_ref)
+
+
+def far_green(m, w1, w2):
+    return pl.pallas_call(
+        far_kernel,
+        out_shape=jax.ShapeDtypeStruct(m.shape, BF16),
+        in_specs=[VMEM] * 3,
+        out_specs=VMEM,
+        scratch_shapes=[pltpu.VMEM(m.shape, BF16)],
+        compiler_params=pltpu.CompilerParams(vmem_limit_bytes=12 * MIB),
+        cost_estimate=cost(m.shape[0] * 7e6, m.size * 4),
+        name="far_green",
+    )(m, w1, w2)
+
+
+def green(ms, w1, w2):
     rows = ms[0].shape[0]
     return pl.pallas_call(
-        functools.partial(green_kernel, far),
+        green_kernel,
         out_shape=(jax.ShapeDtypeStruct((2, rows, 3072), BF16),) * 2,
         in_specs=[VMEM] * 4,
         out_specs=(VMEM,) * 2,
@@ -272,26 +285,25 @@
     )(m, w1, w2, kept, b)
 
 
-def cross_kernel(m_ref, b_ref, kept_ref, green_ref, up_ref, down_ref):
+def cross_kernel(m_ref, b_ref, m0_ref, m1_ref, b0_ref, b1_ref, up_ref, down_ref):
     @pl.when(place()[0] == 2)
     def _():
-        @pl.loop(0, 2)
-        def _(i):
-            halves_to(dot_t(b_ref[...], kept_ref[i]), down_ref, i)
-            halves_to(dot_t(green_ref[i], m_ref[...]), up_ref, i)
-
-
-def cross(m, b, kept, far_b):
+        for i, (far_m_ref, far_b_ref) in enumerate(((m0_ref, b0_ref), (m1_ref, b1_ref))):
+            halves_to(dot_t(b_ref[...], far_m_ref[...]), down_ref, i)
+            halves_to(dot_t(far_b_ref[...], m_ref[...]), up_ref, i)
+
+
+def cross(m, b, far_m, far_b):
     rows = m.shape[0]
     return pl.pallas_call(
         cross_kernel,
         out_shape=(jax.ShapeDtypeStruct((2, 2, rows, rows // 2), BF16),) * 2,
-        in_specs=[VMEM] * 4,
+        in_specs=[VMEM] * 6,
         out_specs=(VMEM,) * 2,
         compiler_params=pltpu.CompilerParams(vmem_limit_bytes=12 * MIB),
         cost_estimate=cost(8 * rows * rows * 3072, 5 * rows * 3072 * 2),
         name="cross",
-    )(m, b, kept, far_b)
+    )(m, b, *far_m, *far_b)
 
 
 def select_kernel(own_ref, m1_ref, m2_ref, t1_ref, t2_ref, up_ref, down_ref, *refs):
@@ -419,7 +431,7 @@
     pieces = unpack(*halves)
     pieces = xors(pieces)
     ms.append(assemble(pieces))
-    b, kept = green(ms, w1, w2, False)
+    b, kept = green(ms, w1, w2)
     even = lax.ppermute(halves[0], "ri", [(0, 1), (1, 2), (2, 3)])
     odd = lax.ppermute(halves[1], "ri", [(3, 2), (2, 1), (1, 0)])
     pieces = unpack(even, odd)
@@ -433,11 +445,13 @@
         got["g", c] = send(ms[c], [(3, 2)])
         for kind in USERS:
             mine[kind, c], theirs[kind, c], *b_of[kind, c] = pair(kind, got[kind, c], w1, w2, kept, b)
-    far_b, far_kept = green([got["g", c] for c in range(CHUNKS)], w1, w2, True)
+    far_m, far_b = [got["g", c] for c in range(CHUNKS)], []
+    for c in range(CHUNKS):
+        far_b.append(far_green(far_m[c], w1, w2))
     sums = []
     for c in range(CHUNKS):
         own_block = own(b, kept, c)
-        up, down = cross(got["f2", c], b_of["f2", c][0], far_kept, far_b)
+        up, down = cross(got["f2", c], b_of["f2", c][0], far_m, far_b)
         back = [
             send(theirs["f1", c], [(1, 0), (2, 1), (3, 2)]),
             send(theirs["f2", c], [(2, 0), (3, 1)]),

time: 189 us -> 181 us (0.958)
  starting transfers between devices: 64.2 us -> 53.5 us
  local copies, waits for them, and re-layouts: 3.92 us -> 7.97 us
  waiting for transfers between devices: 99.3 us -> 96.2 us
    ppermute x28, starting transfers between devices: 37.5 us -> 27.6 us  [xors(): out.append(lax.ppermute(pieces[k], ('ri', 'orb'), pairs))]
    all_to_all x1, waiting for transfers between devices: 10.1 us -> 3.23 us  [swap(): return lax.all_to_all(x, 'orb', split_axis=0, concat_axis=0, tiled=True)]
    ppermute x1, waiting for transfers between devices: 5.84 us -> 0.01 us  [local(): odd = lax.ppermute(halves[1], 'ri', [(3, 2), (2, 1), (1, 0)])]
    ppermute x28, waiting for transfers between devices: 40.1 us -> 45.7 us  [xors(): out.append(lax.ppermute(pieces[k], ('ri', 'orb'), pairs))]
    ppermute x13, waiting for transfers between devices: 41.7 us -> 47.3 us  [send(): return lax.ppermute(x, ('ri', 'orb'), flat)]
    unnamed x5 -> x17, local copies, waits for them, and re-layouts: 0.79 us -> 4.85 us
    pallas_call x2 -> x3, Pallas kernels: 4.11 us -> 4.35 us  [the longest x1 4.09 us: green(): pl.pallas_call(green_kernel, out_shape=(jax.ShapeDtypeStruct((2, rows, 30...]
  transfers between devices with their start and end apart: 44 -> 44, of which waited for: 18 -> 16; matrix products, arithmetic and copies ran while one was open for 1% -> 1% of each run, Pallas kernels for 7% -> 9%
where the time goes in v3:
time: 181 us; the launch traced here: 180 us
  waiting for transfers between devices  96.2 us (53%)
  starting transfers between devices  53.5 us (30%)
  Pallas kernels  22.1 us (12%)
  local copies, waits for them, and re-layouts  7.97 us (4%)
    ppermute x13, waiting for transfers between devices, send(): return lax.ppermute(x, ('ri', 'orb'), flat)  47.3 us
    ppermute x28, waiting for transfers between devices, xors(): out.append(lax.ppermute(pieces[k], ('ri', 'orb'), pairs))  45.7 us
    ppermute x28, starting transfers between devices, xors(): out.append(lax.ppermute(pieces[k], ('ri', 'orb'), pairs))  27.6 us
    ppermute x13, starting transfers between devices, send(): return lax.ppermute(x, ('ri', 'orb'), flat)  15.9 us
    pallas_call x2, Pallas kernels, prep(): pl.pallas_call(functools.partial(prep_kernel, groups, blocks, c, per, apa...  9.78 us
    all_to_all x1, starting transfers between devices, swap(): return lax.all_to_all(x, 'orb', split_axis=0, concat_axis=0, tiled=True)  5.2 us
    unnamed x17, local copies, waits for them, and re-layouts  4.85 us
    pallas_call x1, Pallas kernels, green(): pl.pallas_call(green_kernel, out_shape=(jax.ShapeDtypeStruct((2, rows, 30...  4.09 us
  transfers between devices with their start and end apart: 44, of which 16 were waited for; matrix products, arithmetic and copies ran while one was open for 1% of the time, Pallas kernels for 9%

profile of v3, /device:TPU:0, one launch (start us, length us, event | category | flops | bytes accessed | tf_op | source)
XLA Modules:
  0.0 180.2 jit_solution(5451505248374502544)
XLA Ops:
  0.0 0.8 copy.6
  0.9 1.5 slice_bitcast_fusion.x_ref
  2.4 4.9 %shard_map.46 = bf16[8,32,3072]{2,1,0:T(8,128)(2,1)} custom-call(s32[96]{0:T(128)S(1)} %reshape.11.screen_ref, bf16[256,3072]{1,0:T(8,128)(2,1)S(1)} %slice_bitcast_fusion.x_ref), custom_call_target="tpu_custom_call" | custom-call | flops 2415919104 | bytes 3145728 | tf_op jit(solution)/shard_map/pallas_call | solution.py:78
  7.3 5.2 %all-to-all-start = ((bf16[8,32,3072]{2,1,0:T(8,128)(2,1)}), bf16[8,32,3072]{2,1,0:T(8,128)(2,1)S(1)}, u32[]{:S(2)}, u32[]{:S(2)}) async-start(bf16[8,32,3072]{2,1,0:T(8,128)(2,1)} %shard_map.46), calls=%async_computation | async-start | bytes 3145728 | tf_op jit(solution)/shard_map/all_to_all | solution.py:414
  12.5 1.5 slice.11.x_ref
  14.0 4.9 %shard_map.47 = (bf16[4,32,3072]{2,1,0:T(8,128)(2,1)}, bf16[4,32,3072]{2,1,0:T(8,128)(2,1)}) custom-call(s32[96]{0:T(128)S(1)} %reshape.11.screen_ref, bf16[256,3072]{1,0:T(8,128)(2,1)S(1)} %slice.11.x_ref), custom_call_target="tpu_custom_call" | custom-call | flops 2415919104 | bytes 3145728 | tf_op jit(solution)/shard_map/pallas_call | solution.py:78
  18.9 3.5 %collective-permute-start.22 = (bf16[4,32,3072]{2,1,0:T(8,128)(2,1)}, bf16[4,32,3072]{2,1,0:T(8,128)(2,1)S(1)}, u32[]{:S(2)}, u32[]{:S(2)}) collective-permute-start(bf16[4,32,3072]{2,1,0:T(8,128)(2,1)} %get-tuple-element.61.even_ref), channel_id=1, source_target_pairs={{0,8},{8,16},{16,24},{1,9},{9,17},{17,25},{2,10},{10,18},{18,26},{... | collective-permute-start | bytes 2359304 | tf_op jit(solution)/shard_map/ppermute | solution.py:435
  22.4 1.3 collective-permute-start.23
  23.7 2.3 %unpack.2 = (bf16[32,3072]{1,0:T(8,128)(2,1)S(1)}, bf16[32,3072]{1,0:T(8,128)(2,1)}, bf16[32,3072]{1,0:T(8,128)(2,1)S(1)}, bf16[32,3072]{1,0:T(8,128)(2,1)S(1)},...) custom-call(bf16[4,32,3072]{2,1,0:T(8,128)(2,1)} %get-tuple-element., ...), custom_call_target="tpu_custom_call" | custom-call | flops 100000 | bytes 3145728 | tf_op jit(solution)/shard_map/unpack/pallas_call | solution.py:101
  26.0 0.7 copy-done.1
  26.7 0.7 copy-done.2
  27.3 0.7 copy-done.3
  28.0 0.7 copy-done.4
  28.7 0.7 copy-done.5
  29.4 0.7 copy-done.6
  30.3 3.2 %all-to-all-done = bf16[8,32,3072]{2,1,0:T(8,128)(2,1)S(1)} async-done(((bf16[8,32,3072]{2,1,0:T(8,128)(2,1)}), bf16[8,32,3072]{2,1,0:T(8,128)(2,1)S(1)}, u32[]{:S(2)}, u32[]{:S(2)}) %all-to-all-start) | async-done | bytes 1572896 | tf_op jit(solution)/shard_map/all_to_all | solution.py:414
  33.5 3.6 %collective-permute-start.7 = (bf16[256,3072]{1,0:T(8,128)(2,1)S(1)}, bf16[256,3072]{1,0:T(8,128)(2,1)S(1)}, u32[]{:S(2)}, u32[]{:S(2)}) collective-permute-start(bf16[256,3072]{1,0:T(8,128)(2,1)S(1)} %bitcast.4), channel_id=1, source_target_pairs={{0,8},{8,16},{16,24},{25,17},{17,9},{9,1},{2,10},{10,18},{18,26},{... | collective-permute-start | bytes 4718600 | tf_op jit(solution)/shard_map/ppermute | solution.py:411
  37.1 0.6 collective-permute-start.1
  37.7 7.4 %collective-permute-done.1.refs_2_ = bf16[32,3072]{1,0:T(8,128)(2,1)S(1)} collective-permute-done((bf16[32,3072]{1,0:T(8,128)(2,1)}, bf16[32,3072]{1,0:T(8,128)(2,1)S(1)}, u32[]{:S(2)}, u32[]{:S(2)}) %collective-permute-start.1) | collective-permute-done | bytes 196640 | tf_op jit(solution)/shard_map/ppermute | solution.py:424
  45.7 1.6 collective-permute-start.4
  47.2 1.4 collective-permute-start.5
  48.7 0.8 collective-permute-start.6
  49.7 11.8 %collective-permute-done.3.refs_4_ = bf16[32,3072]{1,0:T(8,128)(2,1)S(1)} collective-permute-done((bf16[32,3072]{1,0:T(8,128)(2,1)}, bf16[32,3072]{1,0:T(8,128)(2,1)S(1)}, u32[]{:S(2)}, u32[]{:S(2)}) %collective-permute-start.3) | collective-permute-done | bytes 196640 | tf_op jit(solution)/shard_map/ppermute | solution.py:424
  61.8 0.9 collective-permute-start.25
  62.7 2.1 %collective-permute-start.26 = (bf16[32,3072]{1,0:T(8,128)(2,1)S(1)}, bf16[32,3072]{1,0:T(8,128)(2,1)S(1)}, u32[]{:S(2)}, u32[]{:S(2)}) collective-permute-start(bf16[32,3072]{1,0:T(8,128)(2,1)S(1)} %get-tuple-element.93), channel_id=1, source_target_pairs={{0,3},{1,2},{2,1},{3,0},{4,7},{5,6},{6,5},{7,4},{8,11},{9,10},{10,... | collective-permute-start | bytes 589832 | tf_op jit(solution)/shard_map/ppermute | solution.py:424
  64.8 0.6 collective-permute-start.27
  65.4 3.6 %collective-permute-done.25.refs_2_ = bf16[32,3072]{1,0:T(8,128)(2,1)S(1)} collective-permute-done((bf16[32,3072]{1,0:T(8,128)(2,1)S(1)}, bf16[32,3072]{1,0:T(8,128)(2,1)S(1)}, u32[]{:S(2)}, u32[]{:S(2)}) %collective-permute-start.25) | collective-permute-done | bytes 196640 | tf_op jit(solution)/shard_map/ppermute | solution.py:424
  68.9 1.6 collective-permute-start.29
  70.5 3.3 %collective-permute-done.26.refs_3_ = bf16[32,3072]{1,0:T(8,128)(2,1)S(1)} collective-permute-done((bf16[32,3072]{1,0:T(8,128)(2,1)S(1)}, bf16[32,3072]{1,0:T(8,128)(2,1)S(1)}, u32[]{:S(2)}, u32[]{:S(2)}) %collective-permute-start.26) | collective-permute-done | bytes 196640 | tf_op jit(solution)/shard_map/ppermute | solution.py:424
  73.8 0.6 collective-permute-start.30
  74.6 0.8 collective-permute-start.12
  75.3 7.0 %collective-permute-done.28.refs_5_ = bf16[32,3072]{1,0:T(8,128)(2,1)S(1)} collective-permute-done((bf16[32,3072]{1,0:T(8,128)(2,1)S(1)}, bf16[32,3072]{1,0:T(8,128)(2,1)S(1)}, u32[]{:S(2)}, u32[]{:S(2)}) %collective-permute-start.28) | collective-permute-done | bytes 196640 | tf_op jit(solution)/shard_map/ppermute | solution.py:424
  82.9 0.8 collective-permute-start.31
  83.7 0.8 collective-permute-start.11
  84.4 1.1 weights.1
  85.5 0.9 collective-permute-start.8
  86.5 4.1 %green.1 = (bf16[2,256,3072]{2,1,0:T(8,128)(2,1)S(1)}, bf16[2,256,3072]{2,1,0:T(8,128)(2,1)S(1)}) custom-call(bf16[256,3072]{1,0:T(8,128)(2,1)S(1)} %bitcast.6, bf16[256,3072]{1,0:T(8,128)(2,1)S(1)} %assemble.2.m1_ref, bf16[768,768]{1,0:T(8,128)(2,1)S(1)} %get-tuple-element.71.w1_ref, bf16[512,512]{1,0:T(8,128)(2,1)S(1)} %get-tuple-element.72.w2_ref), custom_call_target="tpu_custom_call" | custom-call | flops 3584000000 | bytes 9437184 | tf_op jit(solution)/shard_map/green/pallas_call | solution.py:214
  90.6 1.3 collective-permute-start.32
  92.0 1.3 collective-permute-start.33
  93.3 1.3 collective-permute-start.9
  94.9 0.7 collective-permute-start.34
  95.6 1.3 collective-permute-start.35
  96.9 13.3 %collective-permute-done.32.t1_ref = bf16[2,2,256,128]{3,2,1,0:T(8,128)(2,1)S(1)} collective-permute-done((bf16[2,2,256,128]{3,2,1,0:T(8,128)(2,1)S(1)}, bf16[2,2,256,128]{3,2,1,0:T(8,128)(2,1)S(1)}, u32[]{:S(2)}, u32[]{:S(2)}) %collective-permute-start.32) | collective-permute-done | bytes 262176 | tf_op jit(solution)/shard_map/ppermute | solution.py:411
  110.2 1.3 collective-permute-start.10
  111.5 13.1 %collective-permute-done.33.t2_ref = bf16[2,2,256,128]{3,2,1,0:T(8,128)(2,1)S(1)} collective-permute-done((bf16[2,2,256,128]{3,2,1,0:T(8,128)(2,1)S(1)}, bf16[2,2,256,128]{3,2,1,0:T(8,128)(2,1)S(1)}, u32[]{:S(2)}, u32[]{:S(2)}) %collective-permute-start.33) | collective-permute-done | bytes 262176 | tf_op jit(solution)/shard_map/ppermute | solution.py:411
  124.6 0.7 collective-permute-start.13
  125.3 1.3 collective-permute-start.14
  126.6 1.2 own.3.own_ref
  127.8 16.4 %collective-permute-done.35.down_ref = bf16[2,2,256,128]{3,2,1,0:T(8,128)(2,1)S(1)} collective-permute-done((bf16[2,2,256,128]{3,2,1,0:T(8,128)(2,1)S(1)}, bf16[2,2,256,128]{3,2,1,0:T(8,128)(2,1)S(1)}, u32[]{:S(2)}, u32[]{:S(2)}) %collective-permute-start.35) | collective-permute-done | bytes 262176 | tf_op jit(solution)/shard_map/ppermute | solution.py:411
  144.6 4.1 %collective-permute-done.10.t2_ref = bf16[2,2,256,128]{3,2,1,0:T(8,128)(2,1)S(1)} collective-permute-done((bf16[2,2,256,128]{3,2,1,0:T(8,128)(2,1)S(1)}, bf16[2,2,256,128]{3,2,1,0:T(8,128)(2,1)S(1)}, u32[]{:S(2)}, u32[]{:S(2)}) %collective-permute-start.10) | collective-permute-done | bytes 262176 | tf_op jit(solution)/shard_map/ppermute | solution.py:411
  148.7 1.2 collective-permute-start.39
  149.8 1.2 own.2.own_ref
  151.5 4.4 %collective-permute-start.40 = (bf16[2,256,128]{2,1,0:T(8,128)(2,1)S(1)}, bf16[2,256,128]{2,1,0:T(8,128)(2,1)S(1)}, u32[]{:S(2)}, u32[]{:S(2)}) collective-permute-start(bf16[2,256,128]{2,1,0:T(8,128)(2,1)S(1)} %get-tuple-element.110), channel_id=1, source_target_pairs={{0,5},{1,4},{2,7},{3,6},{4,1},{5,0},{6,3},{7,2},{8,13},{9,12},{10,... | collective-permute-start | bytes 393224 | tf_op jit(solution)/shard_map/ppermute | solution.py:424
  156.1 1.4 collective-permute-start.41
  157.5 0.8 collective-permute-start.42
  158.3 0.9 collective-permute-start.15
  159.2 1.3 collective-permute-start.16
  160.5 4.1 %collective-permute-done.40.refs_13_ = bf16[2,256,128]{2,1,0:T(8,128)(2,1)S(1)} collective-permute-done((bf16[2,256,128]{2,1,0:T(8,128)(2,1)S(1)}, bf16[2,256,128]{2,1,0:T(8,128)(2,1)S(1)}, u32[]{:S(2)}, u32[]{:S(2)}) %collective-permute-start.40) | collective-permute-done | bytes 131104 | tf_op jit(solution)/shard_map/ppermute | solution.py:424
  164.6 2.1 %collective-permute-start.17 = (bf16[2,256,128]{2,1,0:T(8,128)(2,1)S(1)}, bf16[2,256,128]{2,1,0:T(8,128)(2,1)S(1)}, u32[]{:S(2)}, u32[]{:S(2)}) collective-permute-start(bf16[2,256,128]{2,1,0:T(8,128)(2,1)S(1)} %get-tuple-element.85), channel_id=1, source_target_pairs={{0,3},{1,2},{2,1},{3,0},{4,7},{5,6},{6,5},{7,4},{8,11},{9,10},{10,... | collective-permute-start | bytes 393224 | tf_op jit(solution)/shard_map/ppermute | solution.py:424
  166.7 0.8 collective-permute-start.18
  167.5 1.4 collective-permute-start.20
  168.9 2.2 %collective-permute-start.21 = (bf16[2,256,128]{2,1,0:T(8,128)(2,1)S(1)}, bf16[2,256,128]{2,1,0:T(8,128)(2,1)S(1)}, u32[]{:S(2)}, u32[]{:S(2)}) collective-permute-start(bf16[2,256,128]{2,1,0:T(8,128)(2,1)S(1)} %get-tuple-element.89), channel_id=1, source_target_pairs={{0,7},{1,6},{2,5},{3,4},{4,3},{5,2},{6,1},{7,0},{8,15},{9,14},{10,... | collective-permute-start | bytes 393224 | tf_op jit(solution)/shard_map/ppermute | solution.py:424
  171.1 7.3 %collective-permute-done.18.refs_4_ = bf16[2,256,128]{2,1,0:T(8,128)(2,1)S(1)} collective-permute-done((bf16[2,256,128]{2,1,0:T(8,128)(2,1)S(1)}, bf16[2,256,128]{2,1,0:T(8,128)(2,1)S(1)}, u32[]{:S(2)}, u32[]{:S(2)}) %collective-permute-start.18) | collective-permute-done | bytes 131104 | tf_op jit(solution)/shard_map/ppermute | solution.py:424
  178.9 1.3 total.1
  (65 shorter events, 3.9 us)
Async XLA Ops:
  7.3 26.2 %all-to-all-start = ((bf16[8,32,3072]{2,1,0:T(8,128)(2,1)}), bf16[8,32,3072]{2,1,0:T(8,128)(2,1)S(1)}, u32[]{:S(2)}, u32[]{:S(2)}) async-start(bf16[8,32,3072]{2,1,0:T(8,128)(2,1)} %shard_map.46), calls=%async_computation | async-start | bytes 3145728 | tf_op jit(solution)/shard_map/all_to_all | solution.py:414
  18.9 28.3 %collective-permute-start.22 = (bf16[4,32,3072]{2,1,0:T(8,128)(2,1)}, bf16[4,32,3072]{2,1,0:T(8,128)(2,1)S(1)}, u32[]{:S(2)}, u32[]{:S(2)}) collective-permute-start(bf16[4,32,3072]{2,1,0:T(8,128)(2,1)} %get-tuple-element.61.even_ref), channel_id=1, source_target_pairs={{0,8},{8,16},{16,24},{1,9},{9,17},{17,25},{2,10},{10,18},{18,26},{... | collective-permute-start | bytes 2359304 | tf_op jit(solution)/shard_map/ppermute | solution.py:435
  22.4 26.2 %collective-permute-start.23 = (bf16[4,32,3072]{2,1,0:T(8,128)(2,1)}, bf16[4,32,3072]{2,1,0:T(8,128)(2,1)S(1)}, u32[]{:S(2)}, u32[]{:S(2)}) collective-permute-start(bf16[4,32,3072]{2,1,0:T(8,128)(2,1)} %get-tuple-element.62.odd_ref), channel_id=1, source_target_pairs={{24,16},{16,8},{8,0},{25,17},{17,9},{9,1},{26,18},{18,10},{10,2},{... | collective-permute-start | bytes 2359304 | tf_op jit(solution)/shard_map/ppermute | solution.py:436
  26.0 0.7 copy-start.1
  26.7 0.7 copy-start.2
  27.3 0.7 copy-start.3
  28.0 0.7 copy-start.4
  28.7 0.7 copy-start.5
  29.4 0.7 copy-start.6
  30.1 7.6 %collective-permute-start = (bf16[32,3072]{1,0:T(8,128)(2,1)}, bf16[32,3072]{1,0:T(8,128)(2,1)S(1)}, u32[]{:S(2)}, u32[]{:S(2)}) collective-permute-start(bf16[32,3072]{1,0:T(8,128)(2,1)} %get-tuple-element.64), channel_id=1, source_target_pairs={{0,1},{1,0},{2,3},{3,2},{4,5},{5,4},{6,7},{7,6},{8,9},{9,8},{10,11... | collective-permute-start | bytes 589832 | tf_op jit(solution)/shard_map/ppermute | solution.py:424
  33.5 52.0 %collective-permute-start.7 = (bf16[256,3072]{1,0:T(8,128)(2,1)S(1)}, bf16[256,3072]{1,0:T(8,128)(2,1)S(1)}, u32[]{:S(2)}, u32[]{:S(2)}) collective-permute-start(bf16[256,3072]{1,0:T(8,128)(2,1)S(1)} %bitcast.4), channel_id=1, source_target_pairs={{0,8},{8,16},{16,24},{25,17},{17,9},{9,1},{2,10},{10,18},{18,26},{... | collective-permute-start | bytes 4718600 | tf_op jit(solution)/shard_map/ppermute | solution.py:411
  37.1 8.0 %collective-permute-start.1 = (bf16[32,3072]{1,0:T(8,128)(2,1)}, bf16[32,3072]{1,0:T(8,128)(2,1)S(1)}, u32[]{:S(2)}, u32[]{:S(2)}) collective-permute-start(bf16[32,3072]{1,0:T(8,128)(2,1)} %copy-done.6), channel_id=1, source_target_pairs={{0,2},{1,3},{2,0},{3,1},{4,6},{5,7},{6,4},{7,5},{8,10},{9,11},{10,... | collective-permute-start | bytes 589832 | tf_op jit(solution)/shard_map/ppermute | solution.py:424
  37.7 8.0 %collective-permute-start.2 = (bf16[32,3072]{1,0:T(8,128)(2,1)}, bf16[32,3072]{1,0:T(8,128)(2,1)S(1)}, u32[]{:S(2)}, u32[]{:S(2)}) collective-permute-start(bf16[32,3072]{1,0:T(8,128)(2,1)} %copy-done.5), channel_id=1, source_target_pairs={{0,3},{1,2},{2,1},{3,0},{4,7},{5,6},{6,5},{7,4},{8,11},{9,10},{10,... | collective-permute-start | bytes 589832 | tf_op jit(solution)/shard_map/ppermute | solution.py:424
  45.1 16.4 %collective-permute-start.3 = (bf16[32,3072]{1,0:T(8,128)(2,1)}, bf16[32,3072]{1,0:T(8,128)(2,1)S(1)}, u32[]{:S(2)}, u32[]{:S(2)}) collective-permute-start(bf16[32,3072]{1,0:T(8,128)(2,1)} %copy-done.4), channel_id=1, source_target_pairs={{0,4},{1,5},{2,6},{3,7},{4,0},{5,1},{6,2},{7,3},{8,12},{9,13},{10,... | collective-permute-start | bytes 589832 | tf_op jit(solution)/shard_map/ppermute | solution.py:424
  45.7 16.1 %collective-permute-start.4 = (bf16[32,3072]{1,0:T(8,128)(2,1)}, bf16[32,3072]{1,0:T(8,128)(2,1)S(1)}, u32[]{:S(2)}, u32[]{:S(2)}) collective-permute-start(bf16[32,3072]{1,0:T(8,128)(2,1)} %copy-done.3), channel_id=1, source_target_pairs={{0,5},{1,4},{2,7},{3,6},{4,1},{5,0},{6,3},{7,2},{8,13},{9,12},{10,... | collective-permute-start | bytes 589832 | tf_op jit(solution)/shard_map/ppermute | solution.py:424
  47.2 15.4 %collective-permute-start.5 = (bf16[32,3072]{1,0:T(8,128)(2,1)}, bf16[32,3072]{1,0:T(8,128)(2,1)S(1)}, u32[]{:S(2)}, u32[]{:S(2)}) collective-permute-start(bf16[32,3072]{1,0:T(8,128)(2,1)} %copy-done.2), channel_id=1, source_target_pairs={{0,6},{1,7},{2,4},{3,5},{4,2},{5,3},{6,0},{7,1},{8,14},{9,15},{10,... | collective-permute-start | bytes 589832 | tf_op jit(solution)/shard_map/ppermute | solution.py:424
  48.7 16.1 %collective-permute-start.6 = (bf16[32,3072]{1,0:T(8,128)(2,1)}, bf16[32,3072]{1,0:T(8,128)(2,1)S(1)}, u32[]{:S(2)}, u32[]{:S(2)}) collective-permute-start(bf16[32,3072]{1,0:T(8,128)(2,1)} %copy-done.1), channel_id=1, source_target_pairs={{0,7},{1,6},{2,5},{3,4},{4,3},{5,2},{6,1},{7,0},{8,15},{9,14},{10,... | collective-permute-start | bytes 589832 | tf_op jit(solution)/shard_map/ppermute | solution.py:424
  61.5 3.9 %collective-permute-start.24 = (bf16[32,3072]{1,0:T(8,128)(2,1)S(1)}, bf16[32,3072]{1,0:T(8,128)(2,1)S(1)}, u32[]{:S(2)}, u32[]{:S(2)}) collective-permute-start(bf16[32,3072]{1,0:T(8,128)(2,1)S(1)} %get-tuple-element.91), channel_id=1, source_target_pairs={{0,1},{1,0},{2,3},{3,2},{4,5},{5,4},{6,7},{7,6},{8,9},{9,8},{10,11... | collective-permute-start | bytes 589832 | tf_op jit(solution)/shard_map/ppermute | solution.py:424
  61.8 7.1 %collective-permute-start.25 = (bf16[32,3072]{1,0:T(8,128)(2,1)S(1)}, bf16[32,3072]{1,0:T(8,128)(2,1)S(1)}, u32[]{:S(2)}, u32[]{:S(2)}) collective-permute-start(bf16[32,3072]{1,0:T(8,128)(2,1)S(1)} %get-tuple-element.92), channel_id=1, source_target_pairs={{0,2},{1,3},{2,0},{3,1},{4,6},{5,7},{6,4},{7,5},{8,10},{9,11},{10,... | collective-permute-start | bytes 589832 | tf_op jit(solution)/shard_map/ppermute | solution.py:424
  62.7 11.1 %collective-permute-start.26 = (bf16[32,3072]{1,0:T(8,128)(2,1)S(1)}, bf16[32,3072]{1,0:T(8,128)(2,1)S(1)}, u32[]{:S(2)}, u32[]{:S(2)}) collective-permute-start(bf16[32,3072]{1,0:T(8,128)(2,1)S(1)} %get-tuple-element.93), channel_id=1, source_target_pairs={{0,3},{1,2},{2,1},{3,0},{4,7},{5,6},{6,5},{7,4},{8,11},{9,10},{10,... | collective-permute-start | bytes 589832 | tf_op jit(solution)/shard_map/ppermute | solution.py:424
  64.8 9.8 %collective-permute-start.27 = (bf16[32,3072]{1,0:T(8,128)(2,1)S(1)}, bf16[32,3072]{1,0:T(8,128)(2,1)S(1)}, u32[]{:S(2)}, u32[]{:S(2)}) collective-permute-start(bf16[32,3072]{1,0:T(8,128)(2,1)S(1)} %get-tuple-element.94), channel_id=1, source_target_pairs={{0,4},{1,5},{2,6},{3,7},{4,0},{5,1},{6,2},{7,3},{8,12},{9,13},{10,... | collective-permute-start | bytes 589832 | tf_op jit(solution)/shard_map/ppermute | solution.py:424
  65.4 17.0 %collective-permute-start.28 = (bf16[32,3072]{1,0:T(8,128)(2,1)S(1)}, bf16[32,3072]{1,0:T(8,128)(2,1)S(1)}, u32[]{:S(2)}, u32[]{:S(2)}) collective-permute-start(bf16[32,3072]{1,0:T(8,128)(2,1)S(1)} %get-tuple-element.95), channel_id=1, source_target_pairs={{0,5},{1,4},{2,7},{3,6},{4,1},{5,0},{6,3},{7,2},{8,13},{9,12},{10,... | collective-permute-start | bytes 589832 | tf_op jit(solution)/shard_map/ppermute | solution.py:424
  68.9 13.4 %collective-permute-start.29 = (bf16[32,3072]{1,0:T(8,128)(2,1)S(1)}, bf16[32,3072]{1,0:T(8,128)(2,1)S(1)}, u32[]{:S(2)}, u32[]{:S(2)}) collective-permute-start(bf16[32,3072]{1,0:T(8,128)(2,1)S(1)} %get-tuple-element.96), channel_id=1, source_target_pairs={{0,6},{1,7},{2,4},{3,5},{4,2},{5,3},{6,0},{7,1},{8,14},{9,15},{10,... | collective-permute-start | bytes 589832 | tf_op jit(solution)/shard_map/ppermute | solution.py:424
  73.8 9.0 %collective-permute-start.30 = (bf16[32,3072]{1,0:T(8,128)(2,1)S(1)}, bf16[32,3072]{1,0:T(8,128)(2,1)S(1)}, u32[]{:S(2)}, u32[]{:S(2)}) collective-permute-start(bf16[32,3072]{1,0:T(8,128)(2,1)S(1)} %get-tuple-element.97), channel_id=1, source_target_pairs={{0,7},{1,6},{2,5},{3,4},{4,3},{5,2},{6,1},{7,0},{8,15},{9,14},{10,... | collective-permute-start | bytes 589832 | tf_op jit(solution)/shard_map/ppermute | solution.py:424
  74.6 17.3 %collective-permute-start.12 = (bf16[256,3072]{1,0:T(8,128)(2,1)S(1)}, bf16[256,3072]{1,0:T(8,128)(2,1)S(1)}, u32[]{:S(2)}, u32[]{:S(2)}) collective-permute-start(bf16[256,3072]{1,0:T(8,128)(2,1)S(1)} %assemble.2.m1_ref), channel_id=1, source_target_pairs={{24,16},{1,9},{26,18},{3,11},{28,20},{5,13},{30,22},{7,15}} | collective-permute-start | bytes 4718600 | tf_op jit(solution)/shard_map/ppermute | solution.py:411
  82.8 1.7 copy-start
  82.8 1.7 copy-start.7
  82.9 9.0 %collective-permute-start.31 = (bf16[256,3072]{1,0:T(8,128)(2,1)S(1)}, bf16[256,3072]{1,0:T(8,128)(2,1)S(1)}, u32[]{:S(2)}, u32[]{:S(2)}) collective-permute-start(bf16[256,3072]{1,0:T(8,128)(2,1)S(1)} %assemble.3.m_ref), channel_id=1, source_target_pairs={{8,16},{16,24},{17,9},{9,1},{10,18},{18,26},{19,11},{11,3},{12,20}... | collective-permute-start | bytes 4718600 | tf_op jit(solution)/shard_map/ppermute | solution.py:411
  83.7 10.9 %collective-permute-start.11 = (bf16[256,3072]{1,0:T(8,128)(2,1)S(1)}, bf16[256,3072]{1,0:T(8,128)(2,1)S(1)}, u32[]{:S(2)}, u32[]{:S(2)}) collective-permute-start(bf16[256,3072]{1,0:T(8,128)(2,1)S(1)} %bitcast.5), channel_id=1, source_target_pairs={{24,16},{1,9},{26,18},{3,11},{28,20},{5,13},{30,22},{7,15}} | collective-permute-start | bytes 4718600 | tf_op jit(solution)/shard_map/ppermute | solution.py:411
  85.5 10.1 %collective-permute-start.8 = (bf16[256,3072]{1,0:T(8,128)(2,1)S(1)}, bf16[256,3072]{1,0:T(8,128)(2,1)S(1)}, u32[]{:S(2)}, u32[]{:S(2)}) collective-permute-start(bf16[256,3072]{1,0:T(8,128)(2,1)S(1)} %collective-permute-done.7.m_ref), channel_id=1, source_target_pairs={{8,16},{16,24},{17,9},{9,1},{10,18},{18,26},{19,11},{11,3},{12,20}... | collective-permute-start | bytes 4718600 | tf_op jit(solution)/shard_map/ppermute | solution.py:411
  90.6 19.6 %collective-permute-start.32 = (bf16[2,2,256,128]{3,2,1,0:T(8,128)(2,1)S(1)}, bf16[2,2,256,128]{3,2,1,0:T(8,128)(2,1)S(1)}, u32[]{:S(2)}, u32[]{:S(2)}) collective-permute-start(bf16[2,2,256,128]{3,2,1,0:T(8,128)(2,1)S(1)} %get-tuple-element.100), channel_id=1, source_target_pairs={{8,0},{16,8},{24,16},{17,25},{9,17},{1,9},{10,2},{18,10},{26,18},{... | collective-permute-start | bytes 786440 | tf_op jit(solution)/shard_map/ppermute | solution.py:411
  92.0 32.6 %collective-permute-start.33 = (bf16[2,2,256,128]{3,2,1,0:T(8,128)(2,1)S(1)}, bf16[2,2,256,128]{3,2,1,0:T(8,128)(2,1)S(1)}, u32[]{:S(2)}, u32[]{:S(2)}) collective-permute-start(bf16[2,2,256,128]{3,2,1,0:T(8,128)(2,1)S(1)} %get-tuple-element.101), channel_id=1, source_target_pairs={{16,0},{24,8},{9,25},{1,17},{18,2},{26,10},{11,27},{3,19},{20,4},{... | collective-permute-start | bytes 786440 | tf_op jit(solution)/shard_map/ppermute | solution.py:411
  93.3 51.2 %collective-permute-start.9 = (bf16[2,2,256,128]{3,2,1,0:T(8,128)(2,1)S(1)}, bf16[2,2,256,128]{3,2,1,0:T(8,128)(2,1)S(1)}, u32[]{:S(2)}, u32[]{:S(2)}) collective-permute-start(bf16[2,2,256,128]{3,2,1,0:T(8,128)(2,1)S(1)} %get-tuple-element.77), channel_id=1, source_target_pairs={{8,0},{16,8},{24,16},{17,25},{9,17},{1,9},{10,2},{18,10},{26,18},{... | collective-permute-start | bytes 786440 | tf_op jit(solution)/shard_map/ppermute | solution.py:411
  94.9 30.4 %collective-permute-start.34 = (bf16[2,2,256,128]{3,2,1,0:T(8,128)(2,1)S(1)}, bf16[2,2,256,128]{3,2,1,0:T(8,128)(2,1)S(1)}, u32[]{:S(2)}, u32[]{:S(2)}) collective-permute-start(bf16[2,2,256,128]{3,2,1,0:T(8,128)(2,1)S(1)} %get-tuple-element.103), channel_id=1, source_target_pairs={{16,24},{9,1},{18,26},{11,3},{20,28},{13,5},{22,30},{15,7}} | collective-permute-start | bytes 786440 | tf_op jit(solution)/shard_map/ppermute | solution.py:411
  95.6 48.6 %collective-permute-start.35 = (bf16[2,2,256,128]{3,2,1,0:T(8,128)(2,1)S(1)}, bf16[2,2,256,128]{3,2,1,0:T(8,128)(2,1)S(1)}, u32[]{:S(2)}, u32[]{:S(2)}) collective-permute-start(bf16[2,2,256,128]{3,2,1,0:T(8,128)(2,1)S(1)} %get-tuple-element.104), channel_id=1, source_target_pairs={{16,0},{9,25},{18,2},{11,27},{20,4},{13,29},{22,6},{15,31}} | collective-permute-start | bytes 786440 | tf_op jit(solution)/shard_map/ppermute | solution.py:411
  110.2 38.4 %collective-permute-start.10 = (bf16[2,2,256,128]{3,2,1,0:T(8,128)(2,1)S(1)}, bf16[2,2,256,128]{3,2,1,0:T(8,128)(2,1)S(1)}, u32[]{:S(2)}, u32[]{:S(2)}) collective-permute-start(bf16[2,2,256,128]{3,2,1,0:T(8,128)(2,1)S(1)} %get-tuple-element.78), channel_id=1, source_target_pairs={{16,0},{24,8},{9,25},{1,17},{18,2},{26,10},{11,27},{3,19},{20,4},{... | collective-permute-start | bytes 786440 | tf_op jit(solution)/shard_map/ppermute | solution.py:411
  124.6 24.1 %collective-permute-start.13 = (bf16[2,2,256,128]{3,2,1,0:T(8,128)(2,1)S(1)}, bf16[2,2,256,128]{3,2,1,0:T(8,128)(2,1)S(1)}, u32[]{:S(2)}, u32[]{:S(2)}) collective-permute-start(bf16[2,2,256,128]{3,2,1,0:T(8,128)(2,1)S(1)} %get-tuple-element.80), channel_id=1, source_target_pairs={{16,24},{9,1},{18,26},{11,3},{20,28},{13,5},{22,30},{15,7}} | collective-permute-start | bytes 786440 | tf_op jit(solution)/shard_map/ppermute | solution.py:411
  125.3 26.2 %collective-permute-start.14 = (bf16[2,2,256,128]{3,2,1,0:T(8,128)(2,1)S(1)}, bf16[2,2,256,128]{3,2,1,0:T(8,128)(2,1)S(1)}, u32[]{:S(2)}, u32[]{:S(2)}) collective-permute-start(bf16[2,2,256,128]{3,2,1,0:T(8,128)(2,1)S(1)} %get-tuple-element.81), channel_id=1, source_target_pairs={{16,0},{9,25},{18,2},{11,27},{20,4},{13,29},{22,6},{15,31}} | collective-permute-start | bytes 786440 | tf_op jit(solution)/shard_map/ppermute | solution.py:411
  144.4 11.7 %collective-permute-start.36 = (bf16[2,256,128]{2,1,0:T(8,128)(2,1)S(1)}, bf16[2,256,128]{2,1,0:T(8,128)(2,1)S(1)}, u32[]{:S(2)}, u32[]{:S(2)}) collective-permute-start(bf16[2,256,128]{2,1,0:T(8,128)(2,1)S(1)} %get-tuple-element.106), channel_id=1, source_target_pairs={{0,1},{1,0},{2,3},{3,2},{4,5},{5,4},{6,7},{7,6},{8,9},{9,8},{10,11... | collective-permute-start | bytes 393224 | tf_op jit(solution)/shard_map/ppermute | solution.py:424
  144.5 13.0 %collective-permute-start.37 = (bf16[2,256,128]{2,1,0:T(8,128)(2,1)S(1)}, bf16[2,256,128]{2,1,0:T(8,128)(2,1)S(1)}, u32[]{:S(2)}, u32[]{:S(2)}) collective-permute-start(bf16[2,256,128]{2,1,0:T(8,128)(2,1)S(1)} %get-tuple-element.107), channel_id=1, source_target_pairs={{0,2},{1,3},{2,0},{3,1},{4,6},{5,7},{6,4},{7,5},{8,10},{9,11},{10,... | collective-permute-start | bytes 393224 | tf_op jit(solution)/shard_map/ppermute | solution.py:424
  148.7 9.6 %collective-permute-start.38 = (bf16[2,256,128]{2,1,0:T(8,128)(2,1)S(1)}, bf16[2,256,128]{2,1,0:T(8,128)(2,1)S(1)}, u32[]{:S(2)}, u32[]{:S(2)}) collective-permute-start(bf16[2,256,128]{2,1,0:T(8,128)(2,1)S(1)} %get-tuple-element.108), channel_id=1, source_target_pairs={{0,3},{1,2},{2,1},{3,0},{4,7},{5,6},{6,5},{7,4},{8,11},{9,10},{10,... | collective-permute-start | bytes 393224 | tf_op jit(solution)/shard_map/ppermute | solution.py:424
  148.7 10.5 %collective-permute-start.39 = (bf16[2,256,128]{2,1,0:T(8,128)(2,1)S(1)}, bf16[2,256,128]{2,1,0:T(8,128)(2,1)S(1)}, u32[]{:S(2)}, u32[]{:S(2)}) collective-permute-start(bf16[2,256,128]{2,1,0:T(8,128)(2,1)S(1)} %get-tuple-element.109), channel_id=1, source_target_pairs={{0,4},{1,5},{2,6},{3,7},{4,0},{5,1},{6,2},{7,3},{8,12},{9,13},{10,... | collective-permute-start | bytes 393224 | tf_op jit(solution)/shard_map/ppermute | solution.py:424
  151.5 13.2 %collective-permute-start.40 = (bf16[2,256,128]{2,1,0:T(8,128)(2,1)S(1)}, bf16[2,256,128]{2,1,0:T(8,128)(2,1)S(1)}, u32[]{:S(2)}, u32[]{:S(2)}) collective-permute-start(bf16[2,256,128]{2,1,0:T(8,128)(2,1)S(1)} %get-tuple-element.110), channel_id=1, source_target_pairs={{0,5},{1,4},{2,7},{3,6},{4,1},{5,0},{6,3},{7,2},{8,13},{9,12},{10,... | collective-permute-start | bytes 393224 | tf_op jit(solution)/shard_map/ppermute | solution.py:424
  156.1 10.6 %collective-permute-start.41 = (bf16[2,256,128]{2,1,0:T(8,128)(2,1)S(1)}, bf16[2,256,128]{2,1,0:T(8,128)(2,1)S(1)}, u32[]{:S(2)}, u32[]{:S(2)}) collective-permute-start(bf16[2,256,128]{2,1,0:T(8,128)(2,1)S(1)} %get-tuple-element.111), channel_id=1, source_target_pairs={{0,6},{1,7},{2,4},{3,5},{4,2},{5,3},{6,0},{7,1},{8,14},{9,15},{10,... | collective-permute-start | bytes 393224 | tf_op jit(solution)/shard_map/ppermute | solution.py:424
  157.5 10.0 %collective-permute-start.42 = (bf16[2,256,128]{2,1,0:T(8,128)(2,1)S(1)}, bf16[2,256,128]{2,1,0:T(8,128)(2,1)S(1)}, u32[]{:S(2)}, u32[]{:S(2)}) collective-permute-start(bf16[2,256,128]{2,1,0:T(8,128)(2,1)S(1)} %get-tuple-element.112), channel_id=1, source_target_pairs={{0,7},{1,6},{2,5},{3,4},{4,3},{5,2},{6,1},{7,0},{8,15},{9,14},{10,... | collective-permute-start | bytes 393224 | tf_op jit(solution)/shard_map/ppermute | solution.py:424
  158.3 9.2 %collective-permute-start.15 = (bf16[2,256,128]{2,1,0:T(8,128)(2,1)S(1)}, bf16[2,256,128]{2,1,0:T(8,128)(2,1)S(1)}, u32[]{:S(2)}, u32[]{:S(2)}) collective-permute-start(bf16[2,256,128]{2,1,0:T(8,128)(2,1)S(1)} %get-tuple-element.83), channel_id=1, source_target_pairs={{0,1},{1,0},{2,3},{3,2},{4,5},{5,4},{6,7},{7,6},{8,9},{9,8},{10,11... | collective-permute-start | bytes 393224 | tf_op jit(solution)/shard_map/ppermute | solution.py:424
  159.2 9.7 %collective-permute-start.16 = (bf16[2,256,128]{2,1,0:T(8,128)(2,1)S(1)}, bf16[2,256,128]{2,1,0:T(8,128)(2,1)S(1)}, u32[]{:S(2)}, u32[]{:S(2)}) collective-permute-start(bf16[2,256,128]{2,1,0:T(8,128)(2,1)S(1)} %get-tuple-element.84), channel_id=1, source_target_pairs={{0,2},{1,3},{2,0},{3,1},{4,6},{5,7},{6,4},{7,5},{8,10},{9,11},{10,... | collective-permute-start | bytes 393224 | tf_op jit(solution)/shard_map/ppermute | solution.py:424
  164.6 6.5 %collective-permute-start.17 = (bf16[2,256,128]{2,1,0:T(8,128)(2,1)S(1)}, bf16[2,256,128]{2,1,0:T(8,128)(2,1)S(1)}, u32[]{:S(2)}, u32[]{:S(2)}) collective-permute-start(bf16[2,256,128]{2,1,0:T(8,128)(2,1)S(1)} %get-tuple-element.85), channel_id=1, source_target_pairs={{0,3},{1,2},{2,1},{3,0},{4,7},{5,6},{6,5},{7,4},{8,11},{9,10},{10,... | collective-permute-start | bytes 393224 | tf_op jit(solution)/shard_map/ppermute | solution.py:424
  166.7 11.7 %collective-permute-start.18 = (bf16[2,256,128]{2,1,0:T(8,128)(2,1)S(1)}, bf16[2,256,128]{2,1,0:T(8,128)(2,1)S(1)}, u32[]{:S(2)}, u32[]{:S(2)}) collective-permute-start(bf16[2,256,128]{2,1,0:T(8,128)(2,1)S(1)} %get-tuple-element.86), channel_id=1, source_target_pairs={{0,4},{1,5},{2,6},{3,7},{4,0},{5,1},{6,2},{7,3},{8,12},{9,13},{10,... | collective-permute-start | bytes 393224 | tf_op jit(solution)/shard_map/ppermute | solution.py:424
  167.5 11.4 %collective-permute-start.19 = (bf16[2,256,128]{2,1,0:T(8,128)(2,1)S(1)}, bf16[2,256,128]{2,1,0:T(8,128)(2,1)S(1)}, u32[]{:S(2)}, u32[]{:S(2)}) collective-permute-start(bf16[2,256,128]{2,1,0:T(8,128)(2,1)S(1)} %get-tuple-element.87), channel_id=1, source_target_pairs={{0,5},{1,4},{2,7},{3,6},{4,1},{5,0},{6,3},{7,2},{8,13},{9,12},{10,... | collective-permute-start | bytes 393224 | tf_op jit(solution)/shard_map/ppermute | solution.py:424
  167.5 11.4 %collective-permute-start.20 = (bf16[2,256,128]{2,1,0:T(8,128)(2,1)S(1)}, bf16[2,256,128]{2,1,0:T(8,128)(2,1)S(1)}, u32[]{:S(2)}, u32[]{:S(2)}) collective-permute-start(bf16[2,256,128]{2,1,0:T(8,128)(2,1)S(1)} %get-tuple-element.88), channel_id=1, source_target_pairs={{0,6},{1,7},{2,4},{3,5},{4,2},{5,3},{6,0},{7,1},{8,14},{9,15},{10,... | collective-permute-start | bytes 393224 | tf_op jit(solution)/shard_map/ppermute | solution.py:424
  168.9 10.0 %collective-permute-start.21 = (bf16[2,256,128]{2,1,0:T(8,128)(2,1)S(1)}, bf16[2,256,128]{2,1,0:T(8,128)(2,1)S(1)}, u32[]{:S(2)}, u32[]{:S(2)}) collective-permute-start(bf16[2,256,128]{2,1,0:T(8,128)(2,1)S(1)} %get-tuple-element.89), channel_id=1, source_target_pairs={{0,7},{1,6},{2,5},{3,4},{4,3},{5,2},{6,1},{7,0},{8,15},{9,14},{10,... | collective-permute-start | bytes 393224 | tf_op jit(solution)/shard_map/ppermute | solution.py:424
